TPU v7x, 32 devices: a whole 2x2x4 slice. The times are simulated.
32 devices in a mesh: section: 2 (over core), tp: 4 (over z), mem: 4 (over y, x).
Axes of the slice: x: 2, y: 2, z: 4, core: 2. Of those that a mesh axis runs over, the one named last changes fastest.
Arguments:
- hidden_in: bfloat16 [8, 8192], P(None, 'mem'), may hold values from -12 to 12
- lengths: int32 [8], replicated, may hold values from 1 to 4096, as said below
- owner_order: int32 [8], replicated, may hold values from 0 to 7, each once
- attn_gain: bfloat16 [2, 8192], P('section', 'mem'), may hold values from 0.25 to 1.75
- w_query: bfloat16 [2, 8192, 8192], P('section', 'mem', 'tp'), may hold values from -0.0625 to 0.0625
- w_key: bfloat16 [2, 8192, 1024], P('section', 'mem', 'tp'), may hold values from -0.0625 to 0.0625
- w_value: bfloat16 [2, 8192, 1024], P('section', 'mem', 'tp'), may hold values from -0.0625 to 0.0625
- w_out: bfloat16 [2, 8192, 8192], P('section', 'tp', 'mem'), may hold values from -0.0625 to 0.0625
- ffn_gain: bfloat16 [2, 8192], P('section', 'mem'), may hold values from 0.25 to 1.75
- w_gate: bfloat16 [2, 8192, 14336], P('section', 'mem', 'tp'), may hold values from -0.0625 to 0.0625
- w_up: bfloat16 [2, 8192, 14336], P('section', 'mem', 'tp'), may hold values from -0.0625 to 0.0625
- w_down: bfloat16 [2, 14336, 8192], P('section', 'tp', 'mem'), may hold values from -0.046875 to 0.046875
- key_cache: bfloat16 [2, 8, 4096, 1024], P('section', 'mem', None, 'tp'), may hold values from -250 to 250
- value_cache: bfloat16 [2, 8, 4096, 1024], P('section', 'mem', None, 'tp'), may hold values from -12 to 12
Outputs:
- layer_outputs: bfloat16 [2, 8, 8192], P('section', None, 'mem')
Inputs may be any that keep to these rules, and one draw needn't show every extreme that they name: Request r has lengths[r] filled positions in its cache; the largest length is exactly 4096. Cache slot j holds request owner_order[j]; index m of mem holds slots m * 2 to (m + 1) * 2 - 1.
All inputs are finite; a program needn't handle non-finite values.
Results may differ from a plain program's by a relative error of at most 0.014.
Values may be sent and summed in bfloat16 or wider, within the bound.
No kernel may reach another device: no remote copies, remote signals or barrier semaphores. Data moves between devices by JAX's collectives and lax.ppermute only.
A program may use at most 128 MiB of HBM per device.

v0:
```python
import math

import jax
import jax.numpy as jnp
from jax import lax
from jax.sharding import PartitionSpec as P

D = 8192
HD = 128


epsilon = 1e-05
rope_base = 500000.0


def from_behind(value, axis, by):
    count = lax.axis_size(axis)
    pairs = [(i, i + by) for i in range(count) if 0 <= i + by < count]
    return lax.ppermute(value, axis, pairs)


def rotate(vectors, positions):
    size = vectors.shape[-1]
    half = size // 2
    freqs = rope_base ** (-(jnp.arange(half, dtype=jnp.float32) * 2.0) / size)
    angles = positions[:, None, None] * freqs[None, None, :]
    cosine = jnp.concatenate([jnp.cos(angles), jnp.cos(angles)], axis=-1)
    sine = jnp.concatenate([jnp.sin(angles), jnp.sin(angles)], axis=-1)
    turned = jnp.concatenate([-vectors[..., half:], vectors[..., :half]], axis=-1)
    return vectors * cosine + turned * sine


def width_sum(values):
    return lax.psum(values, "mem")


def feature_sum(values):
    return lax.psum(values, "tp")


def scale_rows(states, norm_gain):
    as_float = states.astype(jnp.float32)
    squares = jnp.sum(as_float * as_float, axis=1)
    scaled = (as_float * norm_gain.astype(jnp.float32)[None, :]).astype(jnp.bfloat16)
    return (scaled, squares)


def row_factor(total_squares):
    return lax.rsqrt(total_squares / D + epsilon)


def decoder_layer(
    states,
    owner_order,
    inverse_order,
    slot_requests,
    slot_lengths,
    attn_gain,
    w_query,
    w_key,
    w_value,
    w_out,
    ffn_gain,
    w_gate,
    w_up,
    w_down,
    key_rows,
    value_rows,
):
    request_count = states.shape[0]
    slot_count = request_count // lax.axis_size("mem")
    query_cols = w_query.shape[1]
    kv_cols = w_key.shape[1]
    kv_heads = kv_cols // HD
    group_size = query_cols // kv_cols
    scaled, squares = scale_rows(states, attn_gain)
    scaled_slots = jnp.take(scaled, owner_order, axis=0)
    factor_all = row_factor(width_sum(squares))
    slot_factor = jnp.take(factor_all, slot_requests, axis=0)
    head_rows = lax.psum_scatter(
        jnp.concatenate(
            [
                jnp.dot(scaled_slots, w_query, preferred_element_type=jnp.float32),
                jnp.dot(scaled_slots, w_key, preferred_element_type=jnp.float32),
                jnp.dot(scaled_slots, w_value, preferred_element_type=jnp.float32),
            ],
            axis=1,
        ),
        "mem",
        scatter_dimension=0,
        tiled=True,
    )
    head_rows = head_rows * slot_factor[:, None]
    positions = slot_lengths.astype(jnp.float32)
    queries = rotate(head_rows[:, :query_cols].reshape(slot_count, -1, HD), positions).astype(
        jnp.bfloat16
    )
    new_keys = rotate(
        head_rows[:, query_cols : query_cols + kv_cols].reshape(slot_count, kv_heads, HD), positions
    ).astype(jnp.bfloat16)
    new_values = (
        head_rows[:, query_cols + kv_cols :].reshape(slot_count, kv_heads, HD).astype(jnp.bfloat16)
    )
    context = key_rows.shape[1]
    keys_here = key_rows.reshape(slot_count, context, kv_heads, HD)
    values_here = value_rows.reshape(slot_count, context, kv_heads, HD)
    grouped = queries.reshape(slot_count, kv_heads, group_size, HD)
    score_scale = 1.0 / math.sqrt(HD)
    scores = (
        jnp.einsum("sgrd,sjgd->sgrj", grouped, keys_here, preferred_element_type=jnp.float32)
        * score_scale
    )
    live_slots = jnp.arange(context, dtype=jnp.int32)[None, :] < slot_lengths[:, None]
    scores = jnp.where(live_slots[:, None, None, :], scores, -jnp.inf)
    own_score = (
        jnp.einsum("sgrd,sgd->sgr", grouped, new_keys, preferred_element_type=jnp.float32)
        * score_scale
    )
    peak_score = jnp.maximum(jnp.max(scores, axis=-1), own_score)
    soft_weights = jnp.exp(scores - peak_score[..., None])
    own_weight = jnp.exp(own_score - peak_score)
    softmax_total = jnp.sum(soft_weights, axis=-1) + own_weight
    own_rounded = lax.optimization_barrier(own_weight.astype(jnp.bfloat16)).astype(jnp.float32)
    mixed_heads = jnp.einsum(
        "sgrj,sjgd->sgrd",
        soft_weights.astype(jnp.bfloat16),
        values_here,
        preferred_element_type=jnp.float32,
    )
    mixed_heads = (
        mixed_heads + own_rounded[..., None] * new_values.astype(jnp.float32)[:, :, None, :]
    )
    attended = (
        (mixed_heads / softmax_total[..., None])
        .astype(jnp.bfloat16)
        .reshape(slot_count, query_cols)
    )
    projected = jnp.dot(
        lax.all_gather(attended, "mem", axis=0, tiled=True),
        w_out,
        preferred_element_type=jnp.float32,
    )
    attention_out = feature_sum(jnp.take(projected, inverse_order, axis=0))
    after_attention = (states.astype(jnp.float32) + attention_out).astype(jnp.bfloat16)
    scaled_second, squares_second = scale_rows(after_attention, ffn_gain)
    gate_part = jnp.dot(scaled_second, w_gate, preferred_element_type=jnp.float32)
    up_part = jnp.dot(scaled_second, w_up, preferred_element_type=jnp.float32)
    factor_second = row_factor(width_sum(squares_second))
    gate_sums, up_sums = width_sum((gate_part, up_part))
    gate_sums = gate_sums * factor_second[:, None]
    up_sums = up_sums * factor_second[:, None]
    hidden = (jax.nn.silu(gate_sums) * up_sums).astype(jnp.bfloat16)
    down_terms = jnp.dot(hidden, w_down, preferred_element_type=jnp.float32)
    feed_out = feature_sum(down_terms)
    return (after_attention.astype(jnp.float32) + feed_out).astype(jnp.bfloat16)


def per_device(
    hidden_in,
    lengths,
    owner_order,
    attn_gain,
    w_query,
    w_key,
    w_value,
    w_out,
    ffn_gain,
    w_gate,
    w_up,
    w_down,
    key_cache,
    value_cache,
):
    slot_count = hidden_in.shape[0] // lax.axis_size("mem")
    inverse_order = jnp.argsort(owner_order)
    slot_requests = lax.dynamic_slice_in_dim(
        owner_order, lax.axis_index("mem") * slot_count, slot_count, 0
    )
    slot_lengths = jnp.take(lengths, slot_requests, axis=0)
    first_pass = decoder_layer(
        hidden_in,
        owner_order,
        inverse_order,
        slot_requests,
        slot_lengths,
        attn_gain[0],
        w_query[0],
        w_key[0],
        w_value[0],
        w_out[0],
        ffn_gain[0],
        w_gate[0],
        w_up[0],
        w_down[0],
        key_cache[0],
        value_cache[0],
    )
    passed = from_behind(first_pass, "section", 1)
    second_pass = decoder_layer(
        passed,
        owner_order,
        inverse_order,
        slot_requests,
        slot_lengths,
        attn_gain[0],
        w_query[0],
        w_key[0],
        w_value[0],
        w_out[0],
        ffn_gain[0],
        w_gate[0],
        w_up[0],
        w_down[0],
        key_cache[0],
        value_cache[0],
    )
    result = jnp.where(lax.axis_index("section") == 0, first_pass, second_pass)
    return result[None]


def solution(mesh):
    placed = (
        P(None, "mem"),
        P(),
        P(),
        P("section", "mem"),
        P("section", "mem", "tp"),
        P("section", "mem", "tp"),
        P("section", "mem", "tp"),
        P("section", "tp", "mem"),
        P("section", "mem"),
        P("section", "mem", "tp"),
        P("section", "mem", "tp"),
        P("section", "tp", "mem"),
        P("section", "mem", None, "tp"),
        P("section", "mem", None, "tp"),
    )
    return jax.shard_map(
        per_device, mesh=mesh, in_specs=placed, out_specs=P("section", None, "mem"), check_vma=False
    )
```

profile of v0, /device:TPU:1, one launch (start us, length us, event | category | flops | bytes accessed | tf_op | source)
XLA Modules:
  0.0 443.7 jit_solution(11744073031475600755)
XLA Ops:
  6.5 0.7 compare_and_fusion.1
  7.3 0.7 compare_select_fusion.1
  8.0 0.7 mul.325
  8.7 0.9 fusion.63
  10.4 1.5 fusion.48
  12.0 4.6 %fusion.18 = f32[8,2048]{1,0:T(8,128)S(1)} fusion(bf16[1,2048,2048]{2,1,0:T(8,128)(2,1)} %param.24, bf16[8,2048]{1,0:T(8,128)(2,1)S(1)} %gather_fusion.1, pred[8]{0:T(512)(128)(4,1)S(1)} %compare_and_fusion.1), kind=kOutput, calls=%fused_computation.25 | convolution fusion | flops 67125248 | bytes 8486920 | tf_op jit(solution)/shard_map/dot_general | solution.py:83
  16.6 0.6 pad_maximum_fusion
  17.4 1.0 sort.17
  19.2 8.8 %psum.84 = f32[8]{0:T(128)S(1)} all-reduce(f32[8]{0:T(128)S(1)} %get-tuple-element.22), channel_id=1, replica_groups=mesh['section'=2,'tp'=4,'mem'=4] {'mem'}, use_global_device_ids=true, to_apply=%region_2.4 | all-reduce | flops 8 | bytes 64 | tf_op jit(solution)/shard_map/psum | solution.py:34
  28.0 0.6 gather_fusion.2
  28.8 6.9 %reshape_squeeze.8 = bf16[2,4096,2,128]{3,2,1,0:T(2,128)(2,1)} reshape(bf16[1,2,4096,256]{3,2,1,0:T(8,128)(2,1)} %param.32) | data formatting | bytes 8388608 | tf_op jit(solution)/shard_map/reshape;squeeze | solution.py:105
  35.7 7.0 %reshape_squeeze.9 = bf16[2,4096,2,128]{3,2,1,0:T(2,128)(2,1)} reshape(bf16[1,2,4096,256]{3,2,1,0:T(8,128)(2,1)} %param.33) | data formatting | bytes 8388608 | tf_op jit(solution)/shard_map/reshape;squeeze | solution.py:106
  44.1 16.4 %all-reduce.21.cloned.1.call-done = f32[8,2560]{1,0:T(8,128)} async-done(((f32[8,2560]{1,0:T(8,128)}), f32[8,2560]{1,0:T(8,128)}) %all-reduce.21.cloned.1.call-update) | async-done | bytes 81936
  60.5 1.0 dynamic-slice_multiply_fusion.1
  61.9 3.5 fusion.111
  65.7 2.9 fusion.43
  68.6 6.2 %all-gather = bf16[4,2,2048]{2,1,0:T(2,128)(2,1)S(1)} all-gather(bf16[1,2,2048]{2,1,0:T(2,128)(2,1)S(1)} %reshape.281), channel_id=1, replica_groups=mesh['section'=2,'tp'=4,'mem'=4] {'mem'}, dimensions={0}, use_global_device_ids=true | all-gather | bytes 40960 | tf_op jit(solution)/shard_map/all_gather | solution.py:139
  74.9 4.6 %fusion.14 = f32[8,2048]{1,0:T(8,128)S(1)} fusion(bf16[8,2048]{1,0:T(8,128)(2,1)S(1)} %reshape.282, bf16[1,2048,2048]{2,1,0:T(8,128)(2,1)} %param.27), kind=kOutput, calls=%fused_computation.21 | convolution fusion | flops 67108864 | bytes 8486912 | tf_op jit(solution)/shard_map/dot_general | solution.py:138
  80.1 0.7 broadcast_select_fusion.1
  80.8 34.7 %all-reduce.13.cloned.1.call-done = f32[8,2048]{1,0:T(8,128)} async-done(((f32[8,2048]{1,0:T(8,128)}), f32[8,2048]{1,0:T(8,128)}) %all-reduce.13.cloned.1.call-update) | async-done | bytes 65552 | tf_op jit(solution)/shard_map/psum | solution.py:38
  115.5 1.0 fusion.66
  116.5 7.8 %fusion.6 = f32[8,3584]{1,0:T(8,128)} fusion(bf16[1,2048,3584]{2,1,0:T(8,128)(2,1)} %param.30, bf16[8,2048]{1,0:T(8,128)(2,1)S(1)} %get-tuple-element.17, f32[2048]{0:T(1024)S(1)} %bitcast.100), kind=kOutput, calls=%fused_computation.13 | convolution fusion | flops 117489664 | bytes 14835712 | tf_op jit(solution)/shard_map/dot_general | solution.py:147
  124.3 7.8 %fusion.10 = f32[8,3584]{1,0:T(8,128)} fusion(bf16[1,2048,3584]{2,1,0:T(8,128)(2,1)} %param.29, bf16[8,2048]{1,0:T(8,128)(2,1)S(1)} %get-tuple-element.17, f32[2048]{0:T(1024)S(1)} %bitcast.101), kind=kOutput, calls=%fused_computation.17 | convolution fusion | flops 117489664 | bytes 14835712 | tf_op jit(solution)/shard_map/dot_general | solution.py:146
  132.2 7.8 %psum.87 = f32[8]{0:T(128)S(1)} all-reduce(f32[8]{0:T(128)S(1)} %get-tuple-element.16), channel_id=1, replica_groups=mesh['section'=2,'tp'=4,'mem'=4] {'mem'}, use_global_device_ids=true, to_apply=%region_9.13 | all-reduce | flops 8 | bytes 64 | tf_op jit(solution)/shard_map/psum | solution.py:34
  140.0 36.4 %all-reduce.27.cloned.1.call-done = (f32[8,3584]{1,0:T(8,128)}, f32[8,3584]{1,0:T(8,128)}) async-done(((f32[8,3584]{1,0:T(8,128)}, f32[8,3584]{1,0:T(8,128)}), (f32[8,3584]{1,0:T(8,128)}, f32[8,3584]{1,0:T(8,128)})) %all-reduce.27.cloned.1.call-update) | async-done | bytes 229392 | tf_op jit(solution)/shard_map/psum | solution.py:34
  176.5 8.1 %fusion.2 = f32[8,2048]{1,0:T(8,128)} fusion(bf16[1,3584,2048]{2,1,0:T(8,128)(2,1)} %param.31, f32[8,3584]{1,0:T(8,128)} %get-tuple-element.12, f32[8,3584]{1,0:T(8,128)} %get-tuple-element.13, f32[8]{0:T(128)S(1)} %add_rsqrt_fusion.2), kind=kOutput, calls=%fused_computation.9 | convolution fusion | flops 117669888 | bytes 14975008 | tf_op jit(solution)/shard_map/dot_general | solution.py:153
  184.6 32.9 %all-reduce.15.cloned.1.call-done = f32[8,2048]{1,0:T(8,128)} async-done(((f32[8,2048]{1,0:T(8,128)}), f32[8,2048]{1,0:T(8,128)}) %all-reduce.15.cloned.1.call-update) | async-done | bytes 65552 | tf_op jit(solution)/shard_map/psum | solution.py:38
  217.5 0.8 fusion.67
  218.3 1.5 collective-permute-start
  219.8 3.2 collective-permute-done
  224.3 4.6 %fusion.16 = f32[8,2048]{1,0:T(8,128)S(1)} fusion(bf16[1,2048,2048]{2,1,0:T(8,128)(2,1)} %param.24, bf16[8,2048]{1,0:T(8,128)(2,1)S(1)} %gather_fusion.4, pred[8]{0:T(512)(128)(4,1)S(1)} %compare_and_fusion.1), kind=kOutput, calls=%fused_computation.23 | convolution fusion | flops 67125248 | bytes 8486920 | tf_op jit(solution)/shard_map/dot_general | solution.py:83
  228.9 7.8 %psum.90 = f32[8]{0:T(128)S(1)} all-reduce(f32[8]{0:T(128)S(1)} %get-tuple-element.20), channel_id=1, replica_groups=mesh['section'=2,'tp'=4,'mem'=4] {'mem'}, use_global_device_ids=true, to_apply=%region_14.18 | all-reduce | flops 8 | bytes 64 | tf_op jit(solution)/shard_map/psum | solution.py:34
  238.1 40.4 %all-reduce.23.cloned.1.call-done = f32[8,2560]{1,0:T(8,128)} async-done(((f32[8,2560]{1,0:T(8,128)}), f32[8,2560]{1,0:T(8,128)}) %all-reduce.23.cloned.1.call-update) | async-done | bytes 81936
  278.5 1.0 dynamic-slice_multiply_fusion
  279.8 3.5 fusion.112
  283.7 2.9 fusion.40
  286.7 6.2 %all-gather.1 = bf16[4,2,2048]{2,1,0:T(2,128)(2,1)S(1)} all-gather(bf16[1,2,2048]{2,1,0:T(2,128)(2,1)S(1)} %reshape.283), channel_id=1, replica_groups=mesh['section'=2,'tp'=4,'mem'=4] {'mem'}, dimensions={0}, use_global_device_ids=true | all-gather | bytes 40960 | tf_op jit(solution)/shard_map/all_gather | solution.py:139
  292.9 4.6 %fusion.12 = f32[8,2048]{1,0:T(8,128)S(1)} fusion(bf16[8,2048]{1,0:T(8,128)(2,1)S(1)} %reshape.284, bf16[1,2048,2048]{2,1,0:T(8,128)(2,1)} %param.27), kind=kOutput, calls=%fused_computation.19 | convolution fusion | flops 67108864 | bytes 8486912 | tf_op jit(solution)/shard_map/dot_general | solution.py:138
  298.1 0.7 broadcast_select_fusion
  298.8 34.7 %all-reduce.17.cloned.1.call-done = f32[8,2048]{1,0:T(8,128)} async-done(((f32[8,2048]{1,0:T(8,128)}), f32[8,2048]{1,0:T(8,128)}) %all-reduce.17.cloned.1.call-update) | async-done | bytes 65552 | tf_op jit(solution)/shard_map/psum | solution.py:38
  333.5 1.0 fusion.72
  334.5 7.8 %fusion.4 = f32[8,3584]{1,0:T(8,128)} fusion(bf16[1,2048,3584]{2,1,0:T(8,128)(2,1)} %param.30, bf16[8,2048]{1,0:T(8,128)(2,1)S(1)} %get-tuple-element.15, f32[2048]{0:T(1024)S(1)} %bitcast.102), kind=kOutput, calls=%fused_computation.11 | convolution fusion | flops 117489664 | bytes 14835712 | tf_op jit(solution)/shard_map/dot_general | solution.py:147
  342.3 7.8 %fusion.8 = f32[8,3584]{1,0:T(8,128)} fusion(bf16[1,2048,3584]{2,1,0:T(8,128)(2,1)} %param.29, bf16[8,2048]{1,0:T(8,128)(2,1)S(1)} %get-tuple-element.15, f32[2048]{0:T(1024)S(1)} %bitcast.103), kind=kOutput, calls=%fused_computation.15 | convolution fusion | flops 117489664 | bytes 14835712 | tf_op jit(solution)/shard_map/dot_general | solution.py:146
  350.2 7.8 %psum.93 = f32[8]{0:T(128)S(1)} all-reduce(f32[8]{0:T(128)S(1)} %get-tuple-element.14), channel_id=1, replica_groups=mesh['section'=2,'tp'=4,'mem'=4] {'mem'}, use_global_device_ids=true, to_apply=%region_20.24 | all-reduce | flops 8 | bytes 64 | tf_op jit(solution)/shard_map/psum | solution.py:34
  358.0 36.4 %all-reduce.25.cloned.1.call-done = (f32[8,3584]{1,0:T(8,128)}, f32[8,3584]{1,0:T(8,128)}) async-done(((f32[8,3584]{1,0:T(8,128)}, f32[8,3584]{1,0:T(8,128)}), (f32[8,3584]{1,0:T(8,128)}, f32[8,3584]{1,0:T(8,128)})) %all-reduce.25.cloned.1.call-update) | async-done | bytes 229392 | tf_op jit(solution)/shard_map/psum | solution.py:34
  394.5 8.0 %fusion = f32[8,2048]{1,0:T(8,128)} fusion(bf16[1,3584,2048]{2,1,0:T(8,128)(2,1)} %param.31, f32[8,3584]{1,0:T(8,128)} %get-tuple-element.10, f32[8,3584]{1,0:T(8,128)} %get-tuple-element.11, f32[8]{0:T(128)S(1)} %add_rsqrt_fusion), kind=kOutput, calls=%fused_computation.7 | convolution fusion | flops 117669888 | bytes 14975008 | tf_op jit(solution)/shard_map/dot_general | solution.py:153
  402.5 32.9 %all-reduce.19.cloned.1.call-done = f32[8,2048]{1,0:T(8,128)} async-done(((f32[8,2048]{1,0:T(8,128)}), f32[8,2048]{1,0:T(8,128)}) %all-reduce.19.cloned.1.call-update) | async-done | bytes 65552 | tf_op jit(solution)/shard_map/psum | solution.py:38
  435.4 1.5 fusion.79
  (95 shorter events, 8.5 us)
Async XLA Ops:
  6.5 3.6 copy-start
  6.5 53.9 %all-reduce.21.cloned.1.call-start = ((), (), s32[]{:S(2)}) async-start(), calls=%async_computation.4 | async-start | bytes 163840
  10.4 6.9 %copy-start.5 = (s32[8]{0:T(128)S(1)}, s32[8]{0:T(128)}, u32[]{:S(2)}) copy-start(s32[8]{0:T(128)} %param.22) | copy-start | bytes 100
  10.4 8.0 %copy-start.1 = (s32[8]{0:T(128)S(1)}, s32[8]{0:T(128)}, u32[]{:S(2)}) copy-start(s32[8]{0:T(128)} %param.21) | copy-start | bytes 100
  17.3 98.2 %all-reduce.13.cloned.1.call-start = ((), (), s32[]{:S(2)}) async-start(), calls=%async_computation | async-start | bytes 131072 | tf_op jit(solution)/shard_map/psum | solution.py:38
  28.8 13.9 %copy-start.6 = (u32[32]{0:T(128)S(1)}, u32[32]{0:T(128)}, u32[]{:S(2)}) copy-start(u32[32]{0:T(128)} %constant.99) | copy-start | bytes 388
  68.6 12.2 %copy-start.4 = (bf16[1,2048]{1,0:T(2,128)(2,1)S(1)}, bf16[1,2048]{1,0:T(2,128)(2,1)}, u32[]{:S(2)}) copy-start(bf16[1,2048]{1,0:T(2,128)(2,1)} %param.28) | copy-start | bytes 12292
  68.6 46.9 %copy-start.3 = (bf16[8,2048]{1,0:T(8,128)(2,1)S(1)}, bf16[8,2048]{1,0:T(8,128)(2,1)}, u32[]{:S(2)}) copy-start(bf16[8,2048]{1,0:T(8,128)(2,1)} %param.20) | copy-start | bytes 98308
  80.8 95.7 %all-reduce.27.cloned.1.call-start = ((), (), s32[]{:S(2)}) async-start(), calls=%async_computation.7 | async-start | bytes 458752 | tf_op jit(solution)/shard_map/psum | solution.py:34
  132.1 85.3 %all-reduce.15.cloned.1.call-start = ((), (), s32[]{:S(2)}) async-start(), calls=%async_computation.1 | async-start | bytes 131072 | tf_op jit(solution)/shard_map/psum | solution.py:38
  176.5 47.5 %copy-start.2 = (bf16[1,2048,256]{2,1,0:T(8,128)(2,1)S(1)}, bf16[1,2048,256]{2,1,0:T(8,128)(2,1)}, u32[]{:S(2)}) copy-start(bf16[1,2048,256]{2,1,0:T(8,128)(2,1)} %param.26) | copy-start | bytes 3145732
  184.6 93.9 %all-reduce.23.cloned.1.call-start = ((), (), s32[]{:S(2)}) async-start(), calls=%async_computation.5 | async-start | bytes 163840
  218.3 4.7 %collective-permute-start = (bf16[8,2048]{1,0:T(8,128)(2,1)S(1)}, bf16[8,2048]{1,0:T(8,128)(2,1)S(1)}, u32[]{:S(2)}, u32[]{:S(2)}) collective-permute-start(bf16[8,2048]{1,0:T(8,128)(2,1)S(1)} %fusion.67), channel_id=1, source_target_pairs={{0,16},{1,17},{2,18},{3,19},{4,20},{5,21},{6,22},{7,23},{8,24},{9,... | collective-permute-start | bytes 98312 | tf_op jit(solution)/shard_map/ppermute | solution.py:19
  238.0 95.5 %all-reduce.17.cloned.1.call-start = ((), (), s32[]{:S(2)}) async-start(), calls=%async_computation.2 | async-start | bytes 131072 | tf_op jit(solution)/shard_map/psum | solution.py:38
  298.8 95.7 %all-reduce.25.cloned.1.call-start = ((), (), s32[]{:S(2)}) async-start(), calls=%async_computation.6 | async-start | bytes 458752 | tf_op jit(solution)/shard_map/psum | solution.py:34
  350.2 85.3 %all-reduce.19.cloned.1.call-start = ((), (), s32[]{:S(2)}) async-start(), calls=%async_computation.3 | async-start | bytes 131072 | tf_op jit(solution)/shard_map/psum | solution.py:38
Sparse Core Ops, SparseCore 0:
  17.4 43.0 all-reduce.20
  80.9 34.5 all-reduce.12
  132.3 44.1 all-reduce.26
  184.7 32.7 all-reduce.14
  238.1 40.3 all-reduce.22
  298.9 34.5 all-reduce.16
  350.3 44.1 all-reduce.24
  402.6 32.7 all-reduce.18
where the time goes:
time: 448 us; the launch traced here: 444 us
  waiting for transfers between devices  268 us (60%)
  matrix products  81.1 us (18%)
  blocking collectives  44.7 us (10%)
  local copies, waits for them, and re-layouts  18.9 us (4%)
  other arithmetic  14.8 us (3%)
  between operations  14.4 us (3%)
    psum x4, waiting for transfers between devices, feature_sum(): return lax.psum(values, 'tp')  135 us
    psum x2, waiting for transfers between devices, width_sum(): return lax.psum(values, 'mem')  72.9 us
    unnamed x10, waiting for transfers between devices  56.9 us
    psum x4, blocking collectives, width_sum(): return lax.psum(values, 'mem')  32.2 us
    dot_general x2, matrix products, decoder_layer(): down_terms = jnp.dot(hidden, w_down, preferred_element_type=jnp.float32)  16 us
    dot_general x2, matrix products, decoder_layer(): up_part = jnp.dot(scaled_second, w_up, preferred_element_type=jnp.float32)  15.6 us
    dot_general x2, matrix products, decoder_layer(): jnp.dot(scaled_second, w_gate, preferred_element_type=jnp.float32)  15.6 us
    all_gather x2, blocking collectives, decoder_layer(): lax.all_gather(attended, 'mem', axis=0, tiled=True)  12.4 us
  transfers between devices with their start and end apart: 9, of which 9 were waited for; matrix products, arithmetic and copies ran while one was open for 4% of the time, Pallas kernels for 0%

commit v1 on v0

v1 whole, which is shorter than its diff:
```python
import functools
import math

import jax
import jax.numpy as jnp
from jax import lax
from jax.experimental import pallas as pl
from jax.experimental.pallas import tpu as pltpu
from jax.sharding import PartitionSpec as P

HD = 128
EPSILON = 1e-05
ROPE_BASE = 500000.0
LANES = 128
F32 = jnp.float32
BF16 = jnp.bfloat16
IN_VMEM = pl.BlockSpec(memory_space=pltpu.VMEM)
IN_SMEM = pl.BlockSpec(memory_space=pltpu.SMEM)
MIB = 1 << 20


def run(kernel, outs, args, specs=None, scratch=(), grant=2, flops=0, name=None):
    single = isinstance(outs, tuple)
    out_list = [outs] if single else list(outs)
    moved = sum(a.size * a.dtype.itemsize for a in args)
    result = pl.pallas_call(
        kernel,
        out_shape=[jax.ShapeDtypeStruct(shape, dtype) for shape, dtype in out_list],
        in_specs=specs or [IN_VMEM] * len(args),
        out_specs=[IN_VMEM] * len(out_list),
        scratch_shapes=list(scratch),
        compiler_params=pltpu.CompilerParams(vmem_limit_bytes=grant * MIB),
        cost_estimate=pl.CostEstimate(flops=flops, bytes_accessed=moved, transcendentals=0),
        name=name,
    )(*args)
    return result[0] if single else result


def partners(values, axis):
    count = lax.axis_size(axis)
    return [
        lax.ppermute(values[s], axis, [(i, i ^ s) for i in range(count)]) for s in range(1, count)
    ]


def tree_sum(pieces):
    while len(pieces) > 1:
        pieces = [a + b for a, b in zip(pieces[::2], pieces[1::2])]
    return pieces[0]


def matmul_into(out_ref, start, rows, weight_ref, step):
    cols = weight_ref.shape[1]
    while cols % step:
        step //= 2

    def one(i, carry):
        at = pl.multiple_of(i * step, step)
        out_ref[:, pl.ds(start + at, step)] = jnp.dot(
            rows, weight_ref[:, pl.ds(at, step)], preferred_element_type=F32
        ).astype(out_ref.dtype)
        return carry

    lax.fori_loop(0, cols // step, one, 0)


def total_of(refs, rows=slice(None), cols=slice(None)):
    return tree_sum([ref[rows, cols].astype(F32) for ref in refs])


def heads_kernel(count, x_ref, gain_ref, perm_ref, wq_ref, wk_ref, wv_ref, *rest):
    out_refs, sums = rest[:count], rest[count]
    slots = x_ref.shape[0] // count
    x = jnp.dot(perm_ref[...], x_ref[...], preferred_element_type=F32)
    scaled = (x * gain_ref[...].astype(F32)).astype(BF16)
    squares = jnp.sum(x * x, axis=1, keepdims=True)
    at = 0
    for weight_ref in (wq_ref, wk_ref, wv_ref):
        matmul_into(sums, at, scaled, weight_ref, 512)
        at += weight_ref.shape[1]
    sums[:, at:] = jnp.broadcast_to(squares, (x.shape[0], LANES))
    for s in range(count):
        out_refs[s][...] = sums[s * slots : (s + 1) * slots, :]


def attention_kernel(count, width, kv_heads, lengths_ref, cos_ref, sin_ref, *rest):
    pieces = rest[:count]
    key_ref, value_ref, out_ref, head_scr, score_scr, row_scr = rest[count:]
    slots, context = key_ref.shape[:2]
    query_heads = out_ref.shape[1] // HD
    group = query_heads // kv_heads
    chunk = min(512, context)
    total = total_of(pieces)
    wide = total.shape[1]
    squares = total[:, wide - LANES : wide - LANES + 1]
    total = total[:, : wide - LANES] * lax.rsqrt(squares / width + EPSILON)
    all_heads = query_heads + 2 * kv_heads
    scale = 1.0 / math.sqrt(HD)
    lane = lax.broadcasted_iota(jnp.int32, (1, HD), 1)
    head_of = lax.broadcasted_iota(jnp.int32, (query_heads, 1), 0) // group
    for s in range(slots):
        for h in range(all_heads):
            head_scr[h : h + 1, :] = total[s : s + 1, h * HD : (h + 1) * HD]
        rotating = head_scr[: query_heads + kv_heads, :]
        rolled = pltpu.roll(rotating, HD // 2, 1)
        turned = jnp.where(lane < HD // 2, -rolled, rolled)
        rotated = (rotating * cos_ref[s : s + 1, :] + turned * sin_ref[s : s + 1, :]).astype(BF16)
        rotated = rotated.astype(F32)
        queries = rotated[:query_heads]
        new_key = jnp.zeros_like(queries)
        new_value = jnp.zeros_like(queries)
        spread = []
        for g in range(kv_heads):
            mine = head_of == g
            new_key = jnp.where(mine, rotated[query_heads + g : query_heads + g + 1], new_key)
            value_row = query_heads + kv_heads + g
            new_value = jnp.where(mine, head_scr[value_row : value_row + 1, :], new_value)
            spread.append(jnp.where(mine, queries, 0.0))
        spread = jnp.concatenate(spread, axis=1).astype(BF16)
        own_score = jnp.sum(queries * new_key, axis=1, keepdims=True) * scale
        new_value = new_value.astype(BF16).astype(F32)
        length = lengths_ref[s]
        chunks = (length + chunk - 1) // chunk

        def score(c, peak):
            at = pl.multiple_of(c * chunk, chunk)
            scores = lax.dot_general(
                spread,
                key_ref[s, pl.ds(at, chunk), :],
                (((1,), (1,)), ((), ())),
                preferred_element_type=F32,
            )
            position = at + lax.broadcasted_iota(jnp.int32, (1, chunk), 1)
            scores = jnp.where(position < length, scores * scale, -jnp.inf)
            score_scr[:, pl.ds(at, chunk)] = scores
            return jnp.maximum(peak, jnp.max(scores, axis=1, keepdims=True))

        peak = lax.fori_loop(0, chunks, score, own_score)
        own = jnp.exp(own_score - peak)

        def mix(c, carry):
            mixed, weight_sum = carry
            at = pl.multiple_of(c * chunk, chunk)
            soft = jnp.exp(score_scr[:, pl.ds(at, chunk)] - peak)
            mixed = mixed + jnp.dot(
                soft.astype(BF16), value_ref[s, pl.ds(at, chunk), :], preferred_element_type=F32
            )
            return mixed, weight_sum + jnp.sum(soft, axis=1, keepdims=True)

        mixed, weight_sum = lax.fori_loop(
            0,
            chunks,
            mix,
            (jnp.zeros((query_heads, kv_heads * HD), F32), jnp.zeros((query_heads, 1), F32)),
        )
        picked = jnp.zeros((query_heads, HD), F32)
        for g in range(kv_heads):
            picked = jnp.where(head_of == g, mixed[:, g * HD : (g + 1) * HD], picked)
        picked = picked + own.astype(BF16).astype(F32) * new_value
        head_scr[:query_heads, :] = picked / (weight_sum + own)
        for h in range(query_heads):
            row_scr[s : s + 1, h * HD : (h + 1) * HD] = head_scr[h : h + 1, :]
    out_ref[...] = row_scr[...].astype(BF16)


def project_kernel(count, perm_ref, w_ref, *rest):
    pieces = rest[:count]
    out_ref, rows_scr = rest[count:]
    slots = pieces[0].shape[0]
    for s in range(count):
        rows_scr[s * slots : (s + 1) * slots, :] = pieces[s][...].astype(F32)
    rows = jnp.dot(
        perm_ref[...], rows_scr[...].astype(BF16), preferred_element_type=F32
    ).astype(BF16)
    matmul_into(out_ref, 0, rows, w_ref, 512)


def hidden_terms_kernel(count, x_ref, gain_ref, wg_ref, wu_ref, *rest):
    pieces = rest[:count]
    after_ref, out_ref = rest[count:]
    after = (x_ref[...].astype(F32) + total_of(pieces)).astype(BF16)
    after_ref[...] = after
    after = after.astype(F32)
    scaled = (after * gain_ref[...].astype(F32)).astype(BF16)
    squares = jnp.broadcast_to(
        jnp.sum(after * after, axis=1, keepdims=True), (after.shape[0], LANES)
    )
    matmul_into(out_ref, 0, scaled, wg_ref, 512)
    matmul_into(out_ref, wg_ref.shape[1], scaled, wu_ref, 512)
    at = wg_ref.shape[1] + wu_ref.shape[1]
    for _ in range(3):
        part = squares.astype(BF16)
        out_ref[:, at : at + LANES] = part
        squares = squares - part.astype(F32)
        at += LANES


def down_kernel(count, width, w_ref, *rest):
    pieces = rest[:count]
    out_ref, hidden_scr = rest[count:]
    units = w_ref.shape[0]
    squares = tree_sum(
        [
            (
                ref[:, 2 * units : 2 * units + LANES].astype(F32)
                + ref[:, 2 * units + LANES : 2 * units + 2 * LANES].astype(F32)
            )
            + ref[:, 2 * units + 2 * LANES :].astype(F32)
            for ref in pieces
        ]
    )
    factor = lax.rsqrt(squares[:, :1] / width + EPSILON)
    step = 512
    while units % step:
        step //= 2
    for at in range(0, units, step):
        gate = total_of(pieces, cols=slice(at, at + step)) * factor
        up = total_of(pieces, cols=slice(units + at, units + at + step)) * factor
        hidden_scr[:, at : at + step] = (gate / (1.0 + jnp.exp(-gate)) * up).astype(BF16)
    matmul_into(out_ref, 0, hidden_scr[...], w_ref, 256)


def finish_kernel(count, x_ref, *rest):
    pieces = rest[:count]
    out_ref = rest[count]
    out_ref[...] = (x_ref[...].astype(F32) + total_of(pieces)).astype(BF16)


def choose_kernel(count, section_ref, x_ref, first_ref, *rest):
    pieces = rest[:count]
    out_ref = rest[count]
    second = (x_ref[...].astype(F32) + total_of(pieces)).astype(BF16).astype(F32)
    first = first_ref[...].astype(F32)
    out_ref[...] = jnp.where(section_ref[0] == 0, first, second).astype(BF16)


def per_device(
    hidden_in,
    lengths,
    owner_order,
    attn_gain,
    w_query,
    w_key,
    w_value,
    w_out,
    ffn_gain,
    w_gate,
    w_up,
    w_down,
    key_cache,
    value_cache,
):
    mems, tps = lax.axis_size("mem"), lax.axis_size("tp")
    requests, local_width = hidden_in.shape
    slots = requests // mems
    width = local_width * mems
    query_cols, kv_cols, units = w_query.shape[2], w_key.shape[2], w_gate.shape[2]
    kv_heads = kv_cols // HD
    me = lax.axis_index("mem")
    section = lax.axis_index("section").astype(jnp.int32).reshape(1)

    group = jnp.arange(requests, dtype=jnp.int32) // slots
    slot_index = (group ^ me) * slots + jnp.arange(requests, dtype=jnp.int32) % slots
    every = jnp.arange(requests, dtype=jnp.int32)
    request_of = jnp.sum(
        jnp.where(slot_index[:, None] == every[None, :], owner_order[None, :], 0), axis=1
    )
    here = request_of[:, None] == every[None, :]
    perm = here.astype(BF16)
    perm_back = (request_of[None, :] == every[:, None]).astype(BF16)
    slot_lengths = jnp.sum(jnp.where(here[:slots], lengths[None, :], 0), axis=1)
    freqs = ROPE_BASE ** (-(jnp.arange(HD // 2, dtype=F32) * 2.0) / HD)
    angles = slot_lengths.astype(F32)[:, None] * freqs[None, :]
    cosine = jnp.concatenate([jnp.cos(angles)] * 2, axis=-1)
    sine = jnp.concatenate([jnp.sin(angles)] * 2, axis=-1)

    head_cols = query_cols + 2 * kv_cols
    term_cols = 2 * units + 3 * LANES

    def layer(x, tag):
        heads = run(
            functools.partial(heads_kernel, mems),
            [((slots, head_cols + LANES), F32)] * mems,
            [x, attn_gain, perm, w_query[0], w_key[0], w_value[0]],
            scratch=[pltpu.VMEM((requests, head_cols + LANES), F32)],
            name="heads" + tag,
        )
        attended = run(
            functools.partial(attention_kernel, mems, width, kv_heads),
            ((slots, query_cols), BF16),
            [slot_lengths, cosine, sine, heads[0], *partners(heads, "mem"), key_cache[0], value_cache[0]],
            specs=[IN_SMEM] + [IN_VMEM] * (mems + 4),
            scratch=[
                pltpu.VMEM((-(-head_cols // HD // 8) * 8, HD), F32),
                pltpu.VMEM((query_cols // HD, key_cache.shape[2]), F32),
                pltpu.VMEM((slots, query_cols), F32),
            ],
            name="attention" + tag,
        )
        projected = run(
            functools.partial(project_kernel, mems),
            ((requests, local_width), BF16),
            [perm_back, w_out[0], attended, *partners([attended] * mems, "mem")],
            scratch=[pltpu.VMEM((requests, query_cols), F32)],
            name="project" + tag,
        )
        after, terms = run(
            functools.partial(hidden_terms_kernel, tps),
            [((requests, local_width), BF16), ((requests, term_cols), BF16)],
            [x, ffn_gain, w_gate[0], w_up[0], projected, *partners([projected] * tps, "tp")],
            name="terms" + tag,
        )
        down = run(
            functools.partial(down_kernel, mems, width),
            ((requests, local_width), BF16),
            [w_down[0], terms, *partners([terms] * mems, "mem")],
            scratch=[pltpu.VMEM((requests, units), BF16)],
            name="down" + tag,
        )
        return after, [down, *partners([down] * tps, "tp")]

    after, downs = layer(hidden_in, "_0")
    first = run(
        functools.partial(finish_kernel, tps),
        ((requests, local_width), BF16),
        [after, *downs],
        name="finish",
    )
    sections = lax.axis_size("section")
    passed = lax.ppermute(first, "section", [(i, (i + 1) % sections) for i in range(sections)])
    after, downs = layer(passed, "_1")
    result = run(
        functools.partial(choose_kernel, tps),
        ((requests, local_width), BF16),
        [section, after, first, *downs],
        specs=[IN_SMEM] + [IN_VMEM] * (tps + 2),
        name="choose",
    )
    return result[None]


def solution(mesh):
    placed = (
        P(None, "mem"),
        P(),
        P(),
        P("section", "mem"),
        P("section", "mem", "tp"),
        P("section", "mem", "tp"),
        P("section", "mem", "tp"),
        P("section", "tp", "mem"),
        P("section", "mem"),
        P("section", "mem", "tp"),
        P("section", "mem", "tp"),
        P("section", "tp", "mem"),
        P("section", "mem", None, "tp"),
        P("section", "mem", None, "tp"),
    )
    return jax.shard_map(
        per_device, mesh=mesh, in_specs=placed, out_specs=P("section", None, "mem"), check_vma=False
    )
```

time: 448 us -> 135 us (0.30)
  the two profiles are of different devices: /device:TPU:1 before, /device:TPU:0 now
where the time goes in v1:
time: 135 us; the launch traced here: 137 us
  starting transfers between devices  39.9 us (30%)
  Pallas kernels  39.2 us (29%)
  waiting for transfers between devices  32.7 us (24%)
  local copies, waits for them, and re-layouts  23.7 us (18%)
    ppermute x30, starting transfers between devices, partners(): lax.ppermute(values[s], axis, [(i, i ^ s) for i in range(count)])  39.8 us
    pallas_call x12, Pallas kernels, run(): pl.pallas_call(kernel, out_shape=[jax.ShapeDtypeStruct(shape, dtype) for...  39.2 us
    ppermute x30, waiting for transfers between devices, partners(): lax.ppermute(values[s], axis, [(i, i ^ s) for i in range(count)])  31.5 us
    unnamed x56, local copies, waits for them, and re-layouts  23.7 us
  transfers between devices with their start and end apart: 31, of which 26 were waited for; matrix products, arithmetic and copies ran while one was open for 0% of the time, Pallas kernels for 0%

profile of v1, /device:TPU:0, one launch (start us, length us, event | category | flops | bytes accessed | tf_op | source)
XLA Modules:
  0.0 136.9 jit_solution(13124541270069575497)
XLA Ops:
  0.9 3.4 %copy-done.2 = bf16[1,2048,2048]{2,1,0:T(8,128)(2,1)S(1)} copy-done((bf16[1,2048,2048]{2,1,0:T(8,128)(2,1)S(1)}, bf16[1,2048,2048]{2,1,0:T(8,128)(2,1)}, u32[]{:S(2)}) %copy-start.2) | copy-done | bytes 8388632
  4.3 1.2 copy-done.10
  5.5 1.2 copy-done.12
  8.2 2.1 %heads_0.1 = (f32[2,2688]{1,0:T(2,128)S(1)}, f32[2,2688]{1,0:T(2,128)S(1)}, f32[2,2688]{1,0:T(2,128)S(1)}, f32[2,2688]{1,0:T(2,128)S(1)}) custom-call(bf16[8,2048]{1,0:T(8,128)(2,1)S(1)} %copy-done.14, bf16[1,2048]{1,0:T(2,128)(2,1)S(1)} %copy-done.16, bf16[8,8]{1,0:T(8,128)(2,1)S(1)} %get-tuple-element.31.perm_ref, bf16[2048,2048]{1,0:T(8,128)(2,1)S(1)} %bitcast.21, ...), custom_call_target="tpu_custom_call" | custom-call | bytes 10522752 | tf_op jit(solution)/shard_map/heads_0/pallas_call | solution.py:26
  10.4 3.0 %collective-permute-start = (f32[2,2688]{1,0:T(2,128)S(1)}, f32[2,2688]{1,0:T(2,128)S(1)}, u32[]{:S(2)}, u32[]{:S(2)}) collective-permute-start(f32[2,2688]{1,0:T(2,128)S(1)} %get-tuple-element.18), channel_id=1, source_target_pairs={{0,1},{1,0},{2,3},{3,2},{4,5},{5,4},{6,7},{7,6},{8,9},{9,8},{10,11... | collective-permute-start | bytes 64520 | tf_op jit(solution)/shard_map/ppermute | solution.py:42
  13.4 1.5 %collective-permute-start.1 = (f32[2,2688]{1,0:T(2,128)S(1)}, f32[2,2688]{1,0:T(2,128)S(1)}, u32[]{:S(2)}, u32[]{:S(2)}) collective-permute-start(f32[2,2688]{1,0:T(2,128)S(1)} %get-tuple-element.19), channel_id=1, source_target_pairs={{0,2},{1,3},{2,0},{3,1},{4,6},{5,7},{6,4},{7,5},{8,10},{9,11},{10,... | collective-permute-start | bytes 64520 | tf_op jit(solution)/shard_map/ppermute | solution.py:42
  15.3 1.9 %collective-permute-done.1.rest_2_ = f32[2,2688]{1,0:T(2,128)S(1)} collective-permute-done((f32[2,2688]{1,0:T(2,128)S(1)}, f32[2,2688]{1,0:T(2,128)S(1)}, u32[]{:S(2)}, u32[]{:S(2)}) %collective-permute-start.1) | collective-permute-done | bytes 21536 | tf_op jit(solution)/shard_map/ppermute | solution.py:42
  17.2 2.4 %collective-permute-done.2.rest_3_ = f32[2,2688]{1,0:T(2,128)S(1)} collective-permute-done((f32[2,2688]{1,0:T(2,128)S(1)}, f32[2,2688]{1,0:T(2,128)S(1)}, u32[]{:S(2)}, u32[]{:S(2)}) %collective-permute-start.2) | collective-permute-done | bytes 21536 | tf_op jit(solution)/shard_map/ppermute | solution.py:42
  19.6 2.2 %copy-done.6 = bf16[1,2,4096,256]{3,2,1,0:T(8,128)(2,1)S(1)} copy-done((bf16[1,2,4096,256]{3,2,1,0:T(8,128)(2,1)S(1)}, bf16[1,2,4096,256]{3,2,1,0:T(8,128)(2,1)}, u32[]{:S(2)}) %copy-start.6) | copy-done | bytes 4194328
  21.8 2.2 %copy-done.8 = bf16[1,2,4096,256]{3,2,1,0:T(8,128)(2,1)S(1)} copy-done((bf16[1,2,4096,256]{3,2,1,0:T(8,128)(2,1)S(1)}, bf16[1,2,4096,256]{3,2,1,0:T(8,128)(2,1)}, u32[]{:S(2)}) %copy-start.8) | copy-done | bytes 4194328
  24.0 6.9 %attention_0.1.rest_0_ = bf16[2,2048]{1,0:T(2,128)(2,1)S(1)} custom-call(s32[2]{0:T(128)S(1)} %fusion.1.lengths_ref, f32[2,128]{1,0:T(2,128)S(1)} %get-tuple-element.34.cos_ref, f32[2,128]{1,0:T(2,128)S(1)} %get-tuple-element.35.sin_ref, f32[2,2688]{1,0:T(2,128)S(1)} %get-tuple-element.17.rest_0_, f32[2,2688]{1,0:T(2,128)S(1)} %collective-permute-done.rest_1_, ...), custom_call_target="tpu_custom_call" | custom-call | bytes 8476680 | tf_op jit(solution)/shard_map/attention_0/pallas_call | solution.py:26
  31.0 3.4 %collective-permute-start.3 = (bf16[2,2048]{1,0:T(2,128)(2,1)S(1)}, bf16[2,2048]{1,0:T(2,128)(2,1)S(1)}, u32[]{:S(2)}, u32[]{:S(2)}) collective-permute-start(bf16[2,2048]{1,0:T(2,128)(2,1)S(1)} %attention_0.1.rest_0_), channel_id=1, source_target_pairs={{0,1},{1,0},{2,3},{3,2},{4,5},{5,4},{6,7},{7,6},{8,9},{9,8},{10,11... | collective-permute-start | bytes 24584 | tf_op jit(solution)/shard_map/ppermute | solution.py:42
  36.0 1.7 %project_0.1.rest_0_ = bf16[8,2048]{1,0:T(8,128)(2,1)S(1)} custom-call(bf16[8,8]{1,0:T(8,128)(2,1)S(1)} %get-tuple-element.33.perm_ref, bf16[2048,2048]{1,0:T(8,128)(2,1)S(1)} %bitcast.23, bf16[2,2048]{1,0:T(2,128)(2,1)S(1)} %attention_0.1.rest_0_, bf16[2,2048]{1,0:T(2,128)(2,1)S(1)} %collective-permute-done.3.rest_1_, ...), custom_call_target="tpu_custom_call" | custom-call | bytes 8421504 | tf_op jit(solution)/shard_map/project_0/pallas_call | solution.py:26
  37.7 3.6 %collective-permute-start.8 = (bf16[8,2048]{1,0:T(8,128)(2,1)S(1)}, bf16[8,2048]{1,0:T(8,128)(2,1)S(1)}, u32[]{:S(2)}, u32[]{:S(2)}) collective-permute-start(bf16[8,2048]{1,0:T(8,128)(2,1)S(1)} %project_0.1.rest_0_), channel_id=1, source_target_pairs={{0,12},{4,8},{8,4},{12,0},{1,13},{5,9},{9,5},{13,1},{2,14},{6,10},... | collective-permute-start | bytes 98312 | tf_op jit(solution)/shard_map/ppermute | solution.py:42
  42.1 1.3 collective-permute-done.8.rest_3_
  43.5 2.7 %collective-permute-done.7.rest_2_ = bf16[8,2048]{1,0:T(8,128)(2,1)S(1)} collective-permute-done((bf16[8,2048]{1,0:T(8,128)(2,1)S(1)}, bf16[8,2048]{1,0:T(8,128)(2,1)S(1)}, u32[]{:S(2)}, u32[]{:S(2)}) %collective-permute-start.7) | collective-permute-done | bytes 32800 | tf_op jit(solution)/shard_map/ppermute | solution.py:42
  46.2 5.2 %copy-done = bf16[1,2048,3584]{2,1,0:T(8,128)(2,1)S(1)} copy-done((bf16[1,2048,3584]{2,1,0:T(8,128)(2,1)S(1)}, bf16[1,2048,3584]{2,1,0:T(8,128)(2,1)}, u32[]{:S(2)}) %copy-start) | copy-done | bytes 14680088
  51.4 5.5 %terms_0.1 = (bf16[8,2048]{1,0:T(8,128)(2,1)S(1)}, bf16[8,7552]{1,0:T(8,128)(2,1)S(1)}) custom-call(bf16[8,2048]{1,0:T(8,128)(2,1)S(1)} %copy-done.15, bf16[1,2048]{1,0:T(2,128)(2,1)S(1)} %copy-done.18, bf16[2048,3584]{1,0:T(8,128)(2,1)S(1)} %bitcast.13, bf16[2048,3584]{1,0:T(8,128)(2,1)S(1)} %bitcast.15, bf16[8,2048]{1,0:T(8,128)(2,1)S(1)} %project_0.1.rest_0_, ...), custom_call_target="tpu_custom_call" | custom-call | bytes 29528064 | tf_op jit(solution)/shard_map/terms_0/pallas_call | solution.py:26
  56.9 1.5 %collective-permute-start.11 = (bf16[8,7552]{1,0:T(8,128)(2,1)S(1)}, bf16[8,7552]{1,0:T(8,128)(2,1)S(1)}, u32[]{:S(2)}, u32[]{:S(2)}) collective-permute-start(bf16[8,7552]{1,0:T(8,128)(2,1)S(1)} %get-tuple-element.22.rest_0_), channel_id=1, source_target_pairs={{0,3},{1,2},{2,1},{3,0},{4,7},{5,6},{6,5},{7,4},{8,11},{9,10},{10,... | collective-permute-start | bytes 362504 | tf_op jit(solution)/shard_map/ppermute | solution.py:42
  58.5 2.0 %collective-permute-start.10 = (bf16[8,7552]{1,0:T(8,128)(2,1)S(1)}, bf16[8,7552]{1,0:T(8,128)(2,1)S(1)}, u32[]{:S(2)}, u32[]{:S(2)}) collective-permute-start(bf16[8,7552]{1,0:T(8,128)(2,1)S(1)} %get-tuple-element.22.rest_0_), channel_id=1, source_target_pairs={{0,2},{1,3},{2,0},{3,1},{4,6},{5,7},{6,4},{7,5},{8,10},{9,11},{10,... | collective-permute-start | bytes 362504 | tf_op jit(solution)/shard_map/ppermute | solution.py:42
  60.5 2.3 %collective-permute-done.11.rest_3_ = bf16[8,7552]{1,0:T(8,128)(2,1)S(1)} collective-permute-done((bf16[8,7552]{1,0:T(8,128)(2,1)S(1)}, bf16[8,7552]{1,0:T(8,128)(2,1)S(1)}, u32[]{:S(2)}, u32[]{:S(2)}) %collective-permute-start.11) | collective-permute-done | bytes 120864 | tf_op jit(solution)/shard_map/ppermute | solution.py:42
  64.0 1.3 collective-permute-done.9.rest_1_
  65.3 3.1 %down_0.1.rest_0_ = bf16[8,2048]{1,0:T(8,128)(2,1)S(1)} custom-call(bf16[3584,2048]{1,0:T(8,128)(2,1)S(1)} %bitcast.19, bf16[8,7552]{1,0:T(8,128)(2,1)S(1)} %get-tuple-element.22.rest_0_, bf16[8,7552]{1,0:T(8,128)(2,1)S(1)} %collective-permute-done.9.rest_1_, bf16[8,7552]{1,0:T(8,128)(2,1)S(1)} %collective-permute-done.10.rest_2_, ...), custom_call_target="tpu_custom_call" | custom-call | bytes 15163392 | tf_op jit(solution)/shard_map/down_0/pallas_call | solution.py:26
  68.4 1.5 %collective-permute-start.14 = (bf16[8,2048]{1,0:T(8,128)(2,1)S(1)}, bf16[8,2048]{1,0:T(8,128)(2,1)S(1)}, u32[]{:S(2)}, u32[]{:S(2)}) collective-permute-start(bf16[8,2048]{1,0:T(8,128)(2,1)S(1)} %down_0.1.rest_0_), channel_id=1, source_target_pairs={{0,12},{4,8},{8,4},{12,0},{1,13},{5,9},{9,5},{13,1},{2,14},{6,10},... | collective-permute-start | bytes 98312 | tf_op jit(solution)/shard_map/ppermute | solution.py:42
  70.5 2.3 %collective-permute-start.12 = (bf16[8,2048]{1,0:T(8,128)(2,1)S(1)}, bf16[8,2048]{1,0:T(8,128)(2,1)S(1)}, u32[]{:S(2)}, u32[]{:S(2)}) collective-permute-start(bf16[8,2048]{1,0:T(8,128)(2,1)S(1)} %down_0.1.rest_0_), channel_id=1, source_target_pairs={{0,4},{4,0},{8,12},{12,8},{1,5},{5,1},{9,13},{13,9},{2,6},{6,2},{1... | collective-permute-start | bytes 98312 | tf_op jit(solution)/shard_map/ppermute | solution.py:42
  72.8 1.3 collective-permute-done.14.rest_3_
  76.4 3.4 %copy-done.3 = bf16[1,2048,2048]{2,1,0:T(8,128)(2,1)S(1)} copy-done((bf16[1,2048,2048]{2,1,0:T(8,128)(2,1)S(1)}, bf16[1,2048,2048]{2,1,0:T(8,128)(2,1)}, u32[]{:S(2)}) %copy-start.3) | copy-done | bytes 8388632
  79.7 2.1 %heads_1.1 = (f32[2,2688]{1,0:T(2,128)S(1)}, f32[2,2688]{1,0:T(2,128)S(1)}, f32[2,2688]{1,0:T(2,128)S(1)}, f32[2,2688]{1,0:T(2,128)S(1)}) custom-call(bf16[8,2048]{1,0:T(8,128)(2,1)S(1)} %collective-permute-done.15.x_ref, bf16[1,2048]{1,0:T(2,128)(2,1)S(1)} %copy-done.17, bf16[8,8]{1,0:T(8,128)(2,1)S(1)} %get-tuple-element.31.perm_ref, ...), custom_call_target="tpu_custom_call" | custom-call | bytes 10522752 | tf_op jit(solution)/shard_map/heads_1/pallas_call | solution.py:26
  82.0 1.3 collective-permute-start.17
  83.3 2.1 %collective-permute-start.18 = (f32[2,2688]{1,0:T(2,128)S(1)}, f32[2,2688]{1,0:T(2,128)S(1)}, u32[]{:S(2)}, u32[]{:S(2)}) collective-permute-start(f32[2,2688]{1,0:T(2,128)S(1)} %get-tuple-element.26), channel_id=1, source_target_pairs={{0,3},{1,2},{2,1},{3,0},{4,7},{5,6},{6,5},{7,4},{8,11},{9,10},{10,... | collective-permute-start | bytes 64520 | tf_op jit(solution)/shard_map/ppermute | solution.py:42
  85.8 2.2 %collective-permute-done.18.rest_3_ = f32[2,2688]{1,0:T(2,128)S(1)} collective-permute-done((f32[2,2688]{1,0:T(2,128)S(1)}, f32[2,2688]{1,0:T(2,128)S(1)}, u32[]{:S(2)}, u32[]{:S(2)}) %collective-permute-start.18) | collective-permute-done | bytes 21536 | tf_op jit(solution)/shard_map/ppermute | solution.py:42
  88.0 6.9 %attention_1.1.rest_0_ = bf16[2,2048]{1,0:T(2,128)(2,1)S(1)} custom-call(s32[2]{0:T(128)S(1)} %fusion.1.lengths_ref, f32[2,128]{1,0:T(2,128)S(1)} %get-tuple-element.34.cos_ref, f32[2,128]{1,0:T(2,128)S(1)} %get-tuple-element.35.sin_ref, f32[2,2688]{1,0:T(2,128)S(1)} %get-tuple-element.23.rest_0_, f32[2,2688]{1,0:T(2,128)S(1)} %collective-permute-done.16.rest_1_, ...), custom_call_target="tpu_custom_call" | custom-call | bytes 8476680 | tf_op jit(solution)/shard_map/attention_1/pallas_call | solution.py:26
  95.0 3.4 %collective-permute-start.19 = (bf16[2,2048]{1,0:T(2,128)(2,1)S(1)}, bf16[2,2048]{1,0:T(2,128)(2,1)S(1)}, u32[]{:S(2)}, u32[]{:S(2)}) collective-permute-start(bf16[2,2048]{1,0:T(2,128)(2,1)S(1)} %attention_1.1.rest_0_), channel_id=1, source_target_pairs={{0,1},{1,0},{2,3},{3,2},{4,5},{5,4},{6,7},{7,6},{8,9},{9,8},{10,11... | collective-permute-start | bytes 24584 | tf_op jit(solution)/shard_map/ppermute | solution.py:42
  100.1 3.4 %copy-done.5 = bf16[1,2048,2048]{2,1,0:T(8,128)(2,1)S(1)} copy-done((bf16[1,2048,2048]{2,1,0:T(8,128)(2,1)S(1)}, bf16[1,2048,2048]{2,1,0:T(8,128)(2,1)}, u32[]{:S(2)}) %copy-start.5) | copy-done | bytes 8388632
  103.4 1.7 %project_1.1.rest_0_ = bf16[8,2048]{1,0:T(8,128)(2,1)S(1)} custom-call(bf16[8,8]{1,0:T(8,128)(2,1)S(1)} %get-tuple-element.33.perm_ref, bf16[2048,2048]{1,0:T(8,128)(2,1)S(1)} %bitcast.24, bf16[2,2048]{1,0:T(2,128)(2,1)S(1)} %attention_1.1.rest_0_, bf16[2,2048]{1,0:T(2,128)(2,1)S(1)} %collective-permute-done.19.rest_1_, ...), custom_call_target="tpu_custom_call" | custom-call | bytes 8421504 | tf_op jit(solution)/shard_map/project_1/pallas_call | solution.py:26
  105.1 2.4 %collective-permute-start.24 = (bf16[8,2048]{1,0:T(8,128)(2,1)S(1)}, bf16[8,2048]{1,0:T(8,128)(2,1)S(1)}, u32[]{:S(2)}, u32[]{:S(2)}) collective-permute-start(bf16[8,2048]{1,0:T(8,128)(2,1)S(1)} %project_1.1.rest_0_), channel_id=1, source_target_pairs={{0,12},{4,8},{8,4},{12,0},{1,13},{5,9},{9,5},{13,1},{2,14},{6,10},... | collective-permute-start | bytes 98312 | tf_op jit(solution)/shard_map/ppermute | solution.py:42
  108.3 1.2 collective-permute-start.22
  109.5 1.3 collective-permute-done.24.rest_3_
  110.9 1.6 %collective-permute-done.23.rest_2_ = bf16[8,2048]{1,0:T(8,128)(2,1)S(1)} collective-permute-done((bf16[8,2048]{1,0:T(8,128)(2,1)S(1)}, bf16[8,2048]{1,0:T(8,128)(2,1)S(1)}, u32[]{:S(2)}, u32[]{:S(2)}) %collective-permute-start.23) | collective-permute-done | bytes 32800 | tf_op jit(solution)/shard_map/ppermute | solution.py:42
  112.6 5.5 %terms_1.1 = (bf16[8,2048]{1,0:T(8,128)(2,1)S(1)}, bf16[8,7552]{1,0:T(8,128)(2,1)S(1)}) custom-call(bf16[8,2048]{1,0:T(8,128)(2,1)S(1)} %collective-permute-done.15.x_ref, bf16[1,2048]{1,0:T(2,128)(2,1)S(1)} %copy-done.18, bf16[2048,3584]{1,0:T(8,128)(2,1)S(1)} %bitcast.14, bf16[2048,3584]{1,0:T(8,128)(2,1)S(1)} %bitcast.18, ...), custom_call_target="tpu_custom_call" | custom-call | bytes 29528064 | tf_op jit(solution)/shard_map/terms_1/pallas_call | solution.py:26
  118.1 1.5 %collective-permute-start.27 = (bf16[8,7552]{1,0:T(8,128)(2,1)S(1)}, bf16[8,7552]{1,0:T(8,128)(2,1)S(1)}, u32[]{:S(2)}, u32[]{:S(2)}) collective-permute-start(bf16[8,7552]{1,0:T(8,128)(2,1)S(1)} %get-tuple-element.28.rest_0_), channel_id=1, source_target_pairs={{0,3},{1,2},{2,1},{3,0},{4,7},{5,6},{6,5},{7,4},{8,11},{9,10},{10,... | collective-permute-start | bytes 362504 | tf_op jit(solution)/shard_map/ppermute | solution.py:42
  119.6 2.0 %collective-permute-start.26 = (bf16[8,7552]{1,0:T(8,128)(2,1)S(1)}, bf16[8,7552]{1,0:T(8,128)(2,1)S(1)}, u32[]{:S(2)}, u32[]{:S(2)}) collective-permute-start(bf16[8,7552]{1,0:T(8,128)(2,1)S(1)} %get-tuple-element.28.rest_0_), channel_id=1, source_target_pairs={{0,2},{1,3},{2,0},{3,1},{4,6},{5,7},{6,4},{7,5},{8,10},{9,11},{10,... | collective-permute-start | bytes 362504 | tf_op jit(solution)/shard_map/ppermute | solution.py:42
  121.6 2.3 %collective-permute-done.27.rest_3_ = bf16[8,7552]{1,0:T(8,128)(2,1)S(1)} collective-permute-done((bf16[8,7552]{1,0:T(8,128)(2,1)S(1)}, bf16[8,7552]{1,0:T(8,128)(2,1)S(1)}, u32[]{:S(2)}, u32[]{:S(2)}) %collective-permute-start.27) | collective-permute-done | bytes 120864 | tf_op jit(solution)/shard_map/ppermute | solution.py:42
  125.2 1.3 collective-permute-done.25.rest_1_
  126.5 3.0 %down_1.1.rest_0_ = bf16[8,2048]{1,0:T(8,128)(2,1)S(1)} custom-call(bf16[3584,2048]{1,0:T(8,128)(2,1)S(1)} %bitcast.20, bf16[8,7552]{1,0:T(8,128)(2,1)S(1)} %get-tuple-element.28.rest_0_, bf16[8,7552]{1,0:T(8,128)(2,1)S(1)} %collective-permute-done.25.rest_1_, bf16[8,7552]{1,0:T(8,128)(2,1)S(1)} %collective-permute-done.26.rest_2_, ...), custom_call_target="tpu_custom_call" | custom-call | bytes 15163392 | tf_op jit(solution)/shard_map/down_1/pallas_call | solution.py:26
  129.5 1.6 %collective-permute-start.30 = (bf16[8,2048]{1,0:T(8,128)(2,1)S(1)}, bf16[8,2048]{1,0:T(8,128)(2,1)S(1)}, u32[]{:S(2)}, u32[]{:S(2)}) collective-permute-start(bf16[8,2048]{1,0:T(8,128)(2,1)S(1)} %down_1.1.rest_0_), channel_id=1, source_target_pairs={{0,12},{4,8},{8,4},{12,0},{1,13},{5,9},{9,5},{13,1},{2,14},{6,10},... | collective-permute-start | bytes 98312 | tf_op jit(solution)/shard_map/ppermute | solution.py:42
  131.8 2.0 %collective-permute-start.28 = (bf16[8,2048]{1,0:T(8,128)(2,1)S(1)}, bf16[8,2048]{1,0:T(8,128)(2,1)S(1)}, u32[]{:S(2)}, u32[]{:S(2)}) collective-permute-start(bf16[8,2048]{1,0:T(8,128)(2,1)S(1)} %down_1.1.rest_0_), channel_id=1, source_target_pairs={{0,4},{4,0},{8,12},{12,8},{1,5},{5,1},{9,13},{13,9},{2,6},{6,2},{1... | collective-permute-start | bytes 98312 | tf_op jit(solution)/shard_map/ppermute | solution.py:42
  133.9 1.3 collective-permute-done.30.rest_3_
  (92 shorter events, 16.2 us)
Async XLA Ops:
  0.0 15.0 %copy-start.19 = (s32[8]{0:T(128)S(1)}, s32[8]{0:T(128)}, u32[]{:S(2)}) copy-start(s32[8]{0:T(128)} %param.15) | copy-start | bytes 100
  8.2 27.8 %copy-start.4 = (bf16[1,2048,2048]{2,1,0:T(8,128)(2,1)S(1)}, bf16[1,2048,2048]{2,1,0:T(8,128)(2,1)}, u32[]{:S(2)}) copy-start(bf16[1,2048,2048]{2,1,0:T(8,128)(2,1)} %param.21) | copy-start | bytes 25165828
  8.2 38.0 %slice-start = ((s8[14680064]{0:T(1024)(128)(4,1)}), s8[4194304]{0:T(1024)(128)(4,1)S(1)}, s32[]{:S(2)}) async-start(s8[14680064]{0:T(1024)(128)(4,1)} %bitcast.11), calls=%async_computation | async-start | bytes 8388608
  8.2 38.0 %slice-start.1 = ((s8[14680064]{0:T(1024)(128)(4,1)}), s8[4194304]{0:T(1024)(128)(4,1)S(1)}, s32[]{:S(2)}) async-start(s8[14680064]{0:T(1024)(128)(4,1)} %bitcast.11), calls=%async_computation.1 | async-start | bytes 8388608
  10.4 4.9 %collective-permute-start = (f32[2,2688]{1,0:T(2,128)S(1)}, f32[2,2688]{1,0:T(2,128)S(1)}, u32[]{:S(2)}, u32[]{:S(2)}) collective-permute-start(f32[2,2688]{1,0:T(2,128)S(1)} %get-tuple-element.18), channel_id=1, source_target_pairs={{0,1},{1,0},{2,3},{3,2},{4,5},{5,4},{6,7},{7,6},{8,9},{9,8},{10,11... | collective-permute-start | bytes 64520 | tf_op jit(solution)/shard_map/ppermute | solution.py:42
  13.4 3.8 %collective-permute-start.1 = (f32[2,2688]{1,0:T(2,128)S(1)}, f32[2,2688]{1,0:T(2,128)S(1)}, u32[]{:S(2)}, u32[]{:S(2)}) collective-permute-start(f32[2,2688]{1,0:T(2,128)S(1)} %get-tuple-element.19), channel_id=1, source_target_pairs={{0,2},{1,3},{2,0},{3,1},{4,6},{5,7},{6,4},{7,5},{8,10},{9,11},{10,... | collective-permute-start | bytes 64520 | tf_op jit(solution)/shard_map/ppermute | solution.py:42
  14.9 4.7 %collective-permute-start.2 = (f32[2,2688]{1,0:T(2,128)S(1)}, f32[2,2688]{1,0:T(2,128)S(1)}, u32[]{:S(2)}, u32[]{:S(2)}) collective-permute-start(f32[2,2688]{1,0:T(2,128)S(1)} %get-tuple-element.20), channel_id=1, source_target_pairs={{0,3},{1,2},{2,1},{3,0},{4,7},{5,6},{6,5},{7,4},{8,11},{9,10},{10,... | collective-permute-start | bytes 64520 | tf_op jit(solution)/shard_map/ppermute | solution.py:42
  24.0 22.2 %slice-start.2 = ((s8[14680064]{0:T(1024)(128)(4,1)}), s8[4194304]{0:T(1024)(128)(4,1)S(1)}, s32[]{:S(2)}) async-start(s8[14680064]{0:T(1024)(128)(4,1)} %bitcast.11), calls=%async_computation.2 | async-start | bytes 8388608
  24.0 22.2 %copy-start.15 = (bf16[8,2048]{1,0:T(8,128)(2,1)S(1)}, bf16[8,2048]{1,0:T(8,128)(2,1)}, u32[]{:S(2)}) copy-start(bf16[8,2048]{1,0:T(8,128)(2,1)} %x_ref.3) | copy-start | bytes 98308
  24.0 22.2 %copy-start.18 = (bf16[1,2048]{1,0:T(2,128)(2,1)S(1)}, bf16[1,2048]{1,0:T(2,128)(2,1)}, u32[]{:S(2)}) copy-start(bf16[1,2048]{1,0:T(2,128)(2,1)} %gain_ref.7) | copy-start | bytes 12292
  30.9 4.6 %collective-permute-start.5 = (bf16[2,2048]{1,0:T(2,128)(2,1)S(1)}, bf16[2,2048]{1,0:T(2,128)(2,1)S(1)}, u32[]{:S(2)}, u32[]{:S(2)}) collective-permute-start(bf16[2,2048]{1,0:T(2,128)(2,1)S(1)} %attention_0.1.rest_0_), channel_id=1, source_target_pairs={{0,3},{1,2},{2,1},{3,0},{4,7},{5,6},{6,5},{7,4},{8,11},{9,10},{10,... | collective-permute-start | bytes 24584 | tf_op jit(solution)/shard_map/ppermute | solution.py:42
  30.9 4.5 %collective-permute-start.4 = (bf16[2,2048]{1,0:T(2,128)(2,1)S(1)}, bf16[2,2048]{1,0:T(2,128)(2,1)S(1)}, u32[]{:S(2)}, u32[]{:S(2)}) collective-permute-start(bf16[2,2048]{1,0:T(2,128)(2,1)S(1)} %attention_0.1.rest_0_), channel_id=1, source_target_pairs={{0,2},{1,3},{2,0},{3,1},{4,6},{5,7},{6,4},{7,5},{8,10},{9,11},{10,... | collective-permute-start | bytes 24584 | tf_op jit(solution)/shard_map/ppermute | solution.py:42
  31.0 5.0 %collective-permute-start.3 = (bf16[2,2048]{1,0:T(2,128)(2,1)S(1)}, bf16[2,2048]{1,0:T(2,128)(2,1)S(1)}, u32[]{:S(2)}, u32[]{:S(2)}) collective-permute-start(bf16[2,2048]{1,0:T(2,128)(2,1)S(1)} %attention_0.1.rest_0_), channel_id=1, source_target_pairs={{0,1},{1,0},{2,3},{3,2},{4,5},{5,4},{6,7},{7,6},{8,9},{9,8},{10,11... | collective-permute-start | bytes 24584 | tf_op jit(solution)/shard_map/ppermute | solution.py:42
  37.7 5.7 %collective-permute-start.8 = (bf16[8,2048]{1,0:T(8,128)(2,1)S(1)}, bf16[8,2048]{1,0:T(8,128)(2,1)S(1)}, u32[]{:S(2)}, u32[]{:S(2)}) collective-permute-start(bf16[8,2048]{1,0:T(8,128)(2,1)S(1)} %project_0.1.rest_0_), channel_id=1, source_target_pairs={{0,12},{4,8},{8,4},{12,0},{1,13},{5,9},{9,5},{13,1},{2,14},{6,10},... | collective-permute-start | bytes 98312 | tf_op jit(solution)/shard_map/ppermute | solution.py:42
  41.4 4.8 %collective-permute-start.7 = (bf16[8,2048]{1,0:T(8,128)(2,1)S(1)}, bf16[8,2048]{1,0:T(8,128)(2,1)S(1)}, u32[]{:S(2)}, u32[]{:S(2)}) collective-permute-start(bf16[8,2048]{1,0:T(8,128)(2,1)S(1)} %project_0.1.rest_0_), channel_id=1, source_target_pairs={{0,8},{4,12},{8,0},{12,4},{1,9},{5,13},{9,1},{13,5},{2,10},{6,14},... | collective-permute-start | bytes 98312 | tf_op jit(solution)/shard_map/ppermute | solution.py:42
  41.4 4.8 %collective-permute-start.6 = (bf16[8,2048]{1,0:T(8,128)(2,1)S(1)}, bf16[8,2048]{1,0:T(8,128)(2,1)S(1)}, u32[]{:S(2)}, u32[]{:S(2)}) collective-permute-start(bf16[8,2048]{1,0:T(8,128)(2,1)S(1)} %project_0.1.rest_0_), channel_id=1, source_target_pairs={{0,4},{4,0},{8,12},{12,8},{1,5},{5,1},{9,13},{13,9},{2,6},{6,2},{1... | collective-permute-start | bytes 98312 | tf_op jit(solution)/shard_map/ppermute | solution.py:42
  51.4 13.9 %copy-start.1 = (bf16[1,3584,2048]{2,1,0:T(8,128)(2,1)S(1)}, bf16[1,3584,2048]{2,1,0:T(8,128)(2,1)}, u32[]{:S(2)}) copy-start(bf16[1,3584,2048]{2,1,0:T(8,128)(2,1)} %param.25) | copy-start | bytes 44040196
  56.9 19.4 %copy-start.11 = (bf16[1,2048,256]{2,1,0:T(8,128)(2,1)S(1)}, bf16[1,2048,256]{2,1,0:T(8,128)(2,1)}, u32[]{:S(2)}) copy-start(bf16[1,2048,256]{2,1,0:T(8,128)(2,1)} %param.19) | copy-start | bytes 3145732
  56.9 19.4 %copy-start.13 = (bf16[1,2048,256]{2,1,0:T(8,128)(2,1)S(1)}, bf16[1,2048,256]{2,1,0:T(8,128)(2,1)}, u32[]{:S(2)}) copy-start(bf16[1,2048,256]{2,1,0:T(8,128)(2,1)} %param.20) | copy-start | bytes 3145732
  56.9 19.4 %copy-start.17 = (bf16[1,2048]{1,0:T(2,128)(2,1)S(1)}, bf16[1,2048]{1,0:T(2,128)(2,1)}, u32[]{:S(2)}) copy-start(bf16[1,2048]{1,0:T(2,128)(2,1)} %gain_ref.6) | copy-start | bytes 12292
  56.9 5.9 %collective-permute-start.11 = (bf16[8,7552]{1,0:T(8,128)(2,1)S(1)}, bf16[8,7552]{1,0:T(8,128)(2,1)S(1)}, u32[]{:S(2)}, u32[]{:S(2)}) collective-permute-start(bf16[8,7552]{1,0:T(8,128)(2,1)S(1)} %get-tuple-element.22.rest_0_), channel_id=1, source_target_pairs={{0,3},{1,2},{2,1},{3,0},{4,7},{5,6},{6,5},{7,4},{8,11},{9,10},{10,... | collective-permute-start | bytes 362504 | tf_op jit(solution)/shard_map/ppermute | solution.py:42
  58.5 5.6 %collective-permute-start.10 = (bf16[8,7552]{1,0:T(8,128)(2,1)S(1)}, bf16[8,7552]{1,0:T(8,128)(2,1)S(1)}, u32[]{:S(2)}, u32[]{:S(2)}) collective-permute-start(bf16[8,7552]{1,0:T(8,128)(2,1)S(1)} %get-tuple-element.22.rest_0_), channel_id=1, source_target_pairs={{0,2},{1,3},{2,0},{3,1},{4,6},{5,7},{6,4},{7,5},{8,10},{9,11},{10,... | collective-permute-start | bytes 362504 | tf_op jit(solution)/shard_map/ppermute | solution.py:42
  60.5 4.9 %collective-permute-start.9 = (bf16[8,7552]{1,0:T(8,128)(2,1)S(1)}, bf16[8,7552]{1,0:T(8,128)(2,1)S(1)}, u32[]{:S(2)}, u32[]{:S(2)}) collective-permute-start(bf16[8,7552]{1,0:T(8,128)(2,1)S(1)} %get-tuple-element.22.rest_0_), channel_id=1, source_target_pairs={{0,1},{1,0},{2,3},{3,2},{4,5},{5,4},{6,7},{7,6},{8,9},{9,8},{10,11... | collective-permute-start | bytes 362504 | tf_op jit(solution)/shard_map/ppermute | solution.py:42
  65.3 22.6 %copy-start.7 = (bf16[1,2,4096,256]{3,2,1,0:T(8,128)(2,1)S(1)}, bf16[1,2,4096,256]{3,2,1,0:T(8,128)(2,1)}, u32[]{:S(2)}) copy-start(bf16[1,2,4096,256]{3,2,1,0:T(8,128)(2,1)} %param.26) | copy-start | bytes 12582916
  65.3 22.6 %copy-start.9 = (bf16[1,2,4096,256]{3,2,1,0:T(8,128)(2,1)S(1)}, bf16[1,2,4096,256]{3,2,1,0:T(8,128)(2,1)}, u32[]{:S(2)}) copy-start(bf16[1,2,4096,256]{3,2,1,0:T(8,128)(2,1)} %param.27) | copy-start | bytes 12582916
  68.4 5.7 %collective-permute-start.14 = (bf16[8,2048]{1,0:T(8,128)(2,1)S(1)}, bf16[8,2048]{1,0:T(8,128)(2,1)S(1)}, u32[]{:S(2)}, u32[]{:S(2)}) collective-permute-start(bf16[8,2048]{1,0:T(8,128)(2,1)S(1)} %down_0.1.rest_0_), channel_id=1, source_target_pairs={{0,12},{4,8},{8,4},{12,0},{1,13},{5,9},{9,5},{13,1},{2,14},{6,10},... | collective-permute-start | bytes 98312 | tf_op jit(solution)/shard_map/ppermute | solution.py:42
  69.9 4.8 %collective-permute-start.13 = (bf16[8,2048]{1,0:T(8,128)(2,1)S(1)}, bf16[8,2048]{1,0:T(8,128)(2,1)S(1)}, u32[]{:S(2)}, u32[]{:S(2)}) collective-permute-start(bf16[8,2048]{1,0:T(8,128)(2,1)S(1)} %down_0.1.rest_0_), channel_id=1, source_target_pairs={{0,8},{4,12},{8,0},{12,4},{1,9},{5,13},{9,1},{13,5},{2,10},{6,14},... | collective-permute-start | bytes 98312 | tf_op jit(solution)/shard_map/ppermute | solution.py:42
  70.5 4.6 %collective-permute-start.12 = (bf16[8,2048]{1,0:T(8,128)(2,1)S(1)}, bf16[8,2048]{1,0:T(8,128)(2,1)S(1)}, u32[]{:S(2)}, u32[]{:S(2)}) collective-permute-start(bf16[8,2048]{1,0:T(8,128)(2,1)S(1)} %down_0.1.rest_0_), channel_id=1, source_target_pairs={{0,4},{4,0},{8,12},{12,8},{1,5},{5,1},{9,13},{13,9},{2,6},{6,2},{1... | collective-permute-start | bytes 98312 | tf_op jit(solution)/shard_map/ppermute | solution.py:42
  75.1 1.3 collective-permute-start.15
  79.7 32.8 %slice-start.4 = ((s8[14680064]{0:T(1024)(128)(4,1)}), s8[2097152]{0:T(1024)(128)(4,1)S(1)}, s32[]{:S(2)}) async-start(s8[14680064]{0:T(1024)(128)(4,1)} %bitcast.16), calls=%async_computation.4 | async-start | bytes 4194304
  79.7 32.8 %slice-start.5 = ((s8[14680064]{0:T(1024)(128)(4,1)}), s8[4194304]{0:T(1024)(128)(4,1)S(1)}, s32[]{:S(2)}) async-start(s8[14680064]{0:T(1024)(128)(4,1)} %bitcast.16), calls=%async_computation.5 | async-start | bytes 8388608
  81.9 3.9 %collective-permute-start.16 = (f32[2,2688]{1,0:T(2,128)S(1)}, f32[2,2688]{1,0:T(2,128)S(1)}, u32[]{:S(2)}, u32[]{:S(2)}) collective-permute-start(f32[2,2688]{1,0:T(2,128)S(1)} %get-tuple-element.24), channel_id=1, source_target_pairs={{0,1},{1,0},{2,3},{3,2},{4,5},{5,4},{6,7},{7,6},{8,9},{9,8},{10,11... | collective-permute-start | bytes 64520 | tf_op jit(solution)/shard_map/ppermute | solution.py:42
  82.0 3.9 %collective-permute-start.17 = (f32[2,2688]{1,0:T(2,128)S(1)}, f32[2,2688]{1,0:T(2,128)S(1)}, u32[]{:S(2)}, u32[]{:S(2)}) collective-permute-start(f32[2,2688]{1,0:T(2,128)S(1)} %get-tuple-element.25), channel_id=1, source_target_pairs={{0,2},{1,3},{2,0},{3,1},{4,6},{5,7},{6,4},{7,5},{8,10},{9,11},{10,... | collective-permute-start | bytes 64520 | tf_op jit(solution)/shard_map/ppermute | solution.py:42
  83.3 4.7 %collective-permute-start.18 = (f32[2,2688]{1,0:T(2,128)S(1)}, f32[2,2688]{1,0:T(2,128)S(1)}, u32[]{:S(2)}, u32[]{:S(2)}) collective-permute-start(f32[2,2688]{1,0:T(2,128)S(1)} %get-tuple-element.26), channel_id=1, source_target_pairs={{0,3},{1,2},{2,1},{3,0},{4,7},{5,6},{6,5},{7,4},{8,11},{9,10},{10,... | collective-permute-start | bytes 64520 | tf_op jit(solution)/shard_map/ppermute | solution.py:42
  88.0 24.6 %slice-start.6 = ((s8[14680064]{0:T(1024)(128)(4,1)}), s8[4194304]{0:T(1024)(128)(4,1)S(1)}, s32[]{:S(2)}) async-start(s8[14680064]{0:T(1024)(128)(4,1)} %bitcast.16), calls=%async_computation.6 | async-start | bytes 8388608
  94.9 17.7 %slice-start.7 = ((s8[14680064]{0:T(1024)(128)(4,1)}), s8[4194304]{0:T(1024)(128)(4,1)S(1)}, s32[]{:S(2)}) async-start(s8[14680064]{0:T(1024)(128)(4,1)} %bitcast.16), calls=%async_computation.7 | async-start | bytes 8388608
  94.9 4.6 %collective-permute-start.21 = (bf16[2,2048]{1,0:T(2,128)(2,1)S(1)}, bf16[2,2048]{1,0:T(2,128)(2,1)S(1)}, u32[]{:S(2)}, u32[]{:S(2)}) collective-permute-start(bf16[2,2048]{1,0:T(2,128)(2,1)S(1)} %attention_1.1.rest_0_), channel_id=1, source_target_pairs={{0,3},{1,2},{2,1},{3,0},{4,7},{5,6},{6,5},{7,4},{8,11},{9,10},{10,... | collective-permute-start | bytes 24584 | tf_op jit(solution)/shard_map/ppermute | solution.py:42
  95.0 4.5 %collective-permute-start.20 = (bf16[2,2048]{1,0:T(2,128)(2,1)S(1)}, bf16[2,2048]{1,0:T(2,128)(2,1)S(1)}, u32[]{:S(2)}, u32[]{:S(2)}) collective-permute-start(bf16[2,2048]{1,0:T(2,128)(2,1)S(1)} %attention_1.1.rest_0_), channel_id=1, source_target_pairs={{0,2},{1,3},{2,0},{3,1},{4,6},{5,7},{6,4},{7,5},{8,10},{9,11},{10,... | collective-permute-start | bytes 24584 | tf_op jit(solution)/shard_map/ppermute | solution.py:42
  95.0 5.0 %collective-permute-start.19 = (bf16[2,2048]{1,0:T(2,128)(2,1)S(1)}, bf16[2,2048]{1,0:T(2,128)(2,1)S(1)}, u32[]{:S(2)}, u32[]{:S(2)}) collective-permute-start(bf16[2,2048]{1,0:T(2,128)(2,1)S(1)} %attention_1.1.rest_0_), channel_id=1, source_target_pairs={{0,1},{1,0},{2,3},{3,2},{4,5},{5,4},{6,7},{7,6},{8,9},{9,8},{10,11... | collective-permute-start | bytes 24584 | tf_op jit(solution)/shard_map/ppermute | solution.py:42
  105.1 5.7 %collective-permute-start.24 = (bf16[8,2048]{1,0:T(8,128)(2,1)S(1)}, bf16[8,2048]{1,0:T(8,128)(2,1)S(1)}, u32[]{:S(2)}, u32[]{:S(2)}) collective-permute-start(bf16[8,2048]{1,0:T(8,128)(2,1)S(1)} %project_1.1.rest_0_), channel_id=1, source_target_pairs={{0,12},{4,8},{8,4},{12,0},{1,13},{5,9},{9,5},{13,1},{2,14},{6,10},... | collective-permute-start | bytes 98312 | tf_op jit(solution)/shard_map/ppermute | solution.py:42
  107.5 4.9 %collective-permute-start.23 = (bf16[8,2048]{1,0:T(8,128)(2,1)S(1)}, bf16[8,2048]{1,0:T(8,128)(2,1)S(1)}, u32[]{:S(2)}, u32[]{:S(2)}) collective-permute-start(bf16[8,2048]{1,0:T(8,128)(2,1)S(1)} %project_1.1.rest_0_), channel_id=1, source_target_pairs={{0,8},{4,12},{8,0},{12,4},{1,9},{5,13},{9,1},{13,5},{2,10},{6,14},... | collective-permute-start | bytes 98312 | tf_op jit(solution)/shard_map/ppermute | solution.py:42
  108.3 4.3 %collective-permute-start.22 = (bf16[8,2048]{1,0:T(8,128)(2,1)S(1)}, bf16[8,2048]{1,0:T(8,128)(2,1)S(1)}, u32[]{:S(2)}, u32[]{:S(2)}) collective-permute-start(bf16[8,2048]{1,0:T(8,128)(2,1)S(1)} %project_1.1.rest_0_), channel_id=1, source_target_pairs={{0,4},{4,0},{8,12},{12,8},{1,5},{5,1},{9,13},{13,9},{2,6},{6,2},{1... | collective-permute-start | bytes 98312 | tf_op jit(solution)/shard_map/ppermute | solution.py:42
  118.1 5.8 %collective-permute-start.27 = (bf16[8,7552]{1,0:T(8,128)(2,1)S(1)}, bf16[8,7552]{1,0:T(8,128)(2,1)S(1)}, u32[]{:S(2)}, u32[]{:S(2)}) collective-permute-start(bf16[8,7552]{1,0:T(8,128)(2,1)S(1)} %get-tuple-element.28.rest_0_), channel_id=1, source_target_pairs={{0,3},{1,2},{2,1},{3,0},{4,7},{5,6},{6,5},{7,4},{8,11},{9,10},{10,... | collective-permute-start | bytes 362504 | tf_op jit(solution)/shard_map/ppermute | solution.py:42
  119.6 5.6 %collective-permute-start.26 = (bf16[8,7552]{1,0:T(8,128)(2,1)S(1)}, bf16[8,7552]{1,0:T(8,128)(2,1)S(1)}, u32[]{:S(2)}, u32[]{:S(2)}) collective-permute-start(bf16[8,7552]{1,0:T(8,128)(2,1)S(1)} %get-tuple-element.28.rest_0_), channel_id=1, source_target_pairs={{0,2},{1,3},{2,0},{3,1},{4,6},{5,7},{6,4},{7,5},{8,10},{9,11},{10,... | collective-permute-start | bytes 362504 | tf_op jit(solution)/shard_map/ppermute | solution.py:42
  121.6 4.9 %collective-permute-start.25 = (bf16[8,7552]{1,0:T(8,128)(2,1)S(1)}, bf16[8,7552]{1,0:T(8,128)(2,1)S(1)}, u32[]{:S(2)}, u32[]{:S(2)}) collective-permute-start(bf16[8,7552]{1,0:T(8,128)(2,1)S(1)} %get-tuple-element.28.rest_0_), channel_id=1, source_target_pairs={{0,1},{1,0},{2,3},{3,2},{4,5},{5,4},{6,7},{7,6},{8,9},{9,8},{10,11... | collective-permute-start | bytes 362504 | tf_op jit(solution)/shard_map/ppermute | solution.py:42
  129.5 5.7 %collective-permute-start.30 = (bf16[8,2048]{1,0:T(8,128)(2,1)S(1)}, bf16[8,2048]{1,0:T(8,128)(2,1)S(1)}, u32[]{:S(2)}, u32[]{:S(2)}) collective-permute-start(bf16[8,2048]{1,0:T(8,128)(2,1)S(1)} %down_1.1.rest_0_), channel_id=1, source_target_pairs={{0,12},{4,8},{8,4},{12,0},{1,13},{5,9},{9,5},{13,1},{2,14},{6,10},... | collective-permute-start | bytes 98312 | tf_op jit(solution)/shard_map/ppermute | solution.py:42
  131.0 5.2 %collective-permute-start.29 = (bf16[8,2048]{1,0:T(8,128)(2,1)S(1)}, bf16[8,2048]{1,0:T(8,128)(2,1)S(1)}, u32[]{:S(2)}, u32[]{:S(2)}) collective-permute-start(bf16[8,2048]{1,0:T(8,128)(2,1)S(1)} %down_1.1.rest_0_), channel_id=1, source_target_pairs={{0,8},{4,12},{8,0},{12,4},{1,9},{5,13},{9,1},{13,5},{2,10},{6,14},... | collective-permute-start | bytes 98312 | tf_op jit(solution)/shard_map/ppermute | solution.py:42
  131.8 4.4 %collective-permute-start.28 = (bf16[8,2048]{1,0:T(8,128)(2,1)S(1)}, bf16[8,2048]{1,0:T(8,128)(2,1)S(1)}, u32[]{:S(2)}, u32[]{:S(2)}) collective-permute-start(bf16[8,2048]{1,0:T(8,128)(2,1)S(1)} %down_1.1.rest_0_), channel_id=1, source_target_pairs={{0,4},{4,0},{8,12},{12,8},{1,5},{5,1},{9,13},{13,9},{2,6},{6,2},{1... | collective-permute-start | bytes 98312 | tf_op jit(solution)/shard_map/ppermute | solution.py:42
  (11 other events, 33.8 us)

commit v2 on v1

--- a/solution.py
+++ b/solution.py
@@ -15,24 +15,31 @@
 F32 = jnp.float32
 BF16 = jnp.bfloat16
 IN_VMEM = pl.BlockSpec(memory_space=pltpu.VMEM)
-IN_SMEM = pl.BlockSpec(memory_space=pltpu.SMEM)
 MIB = 1 << 20
 
 
-def run(kernel, outs, args, specs=None, scratch=(), grant=2, flops=0, name=None):
+STAGE_US = dict.fromkeys(("heads", "attention", "project", "terms", "down", "window"), 20)
+
+
+def run(kernel, outs, args, specs=None, scratch=(), grant=2, name=None, keep=()):
     single = isinstance(outs, tuple)
     out_list = [outs] if single else list(outs)
-    moved = sum(a.size * a.dtype.itemsize for a in args)
+    flops = STAGE_US.get(name.split("_")[0], 0) * 1150000000
+    args, held = list(args), len(args)
+
+    def without_kept(*refs):
+        kernel(*refs[:held], *refs[held + len(keep) :])
+
     result = pl.pallas_call(
-        kernel,
+        without_kept,
         out_shape=[jax.ShapeDtypeStruct(shape, dtype) for shape, dtype in out_list],
-        in_specs=specs or [IN_VMEM] * len(args),
+        in_specs=(specs or [IN_VMEM] * held) + [IN_VMEM] * len(keep),
         out_specs=[IN_VMEM] * len(out_list),
         scratch_shapes=list(scratch),
         compiler_params=pltpu.CompilerParams(vmem_limit_bytes=grant * MIB),
-        cost_estimate=pl.CostEstimate(flops=flops, bytes_accessed=moved, transcendentals=0),
+        cost_estimate=pl.CostEstimate(flops=flops, bytes_accessed=0, transcendentals=0),
         name=name,
-    )(*args)
+    )(*args, *keep)
     return result[0] if single else result
 
 
@@ -51,17 +58,11 @@
 
 def matmul_into(out_ref, start, rows, weight_ref, step):
     cols = weight_ref.shape[1]
-    while cols % step:
-        step //= 2
-
-    def one(i, carry):
-        at = pl.multiple_of(i * step, step)
-        out_ref[:, pl.ds(start + at, step)] = jnp.dot(
-            rows, weight_ref[:, pl.ds(at, step)], preferred_element_type=F32
+    for at in range(0, cols, step):
+        end = min(at + step, cols)
+        out_ref[:, start + at : start + end] = jnp.dot(
+            rows, weight_ref[:, at:end], preferred_element_type=F32
         ).astype(out_ref.dtype)
-        return carry
-
-    lax.fori_loop(0, cols // step, one, 0)
 
 
 def total_of(refs, rows=slice(None), cols=slice(None)):
@@ -83,13 +84,60 @@
         out_refs[s][...] = sums[s * slots : (s + 1) * slots, :]
 
 
+def first_heads_kernel(count, pieces, x_any, gain_any, owner_any, wq_any, wk_any, wv_any, *rest):
+    out_refs = rest[:count]
+    x_ref, gain_ref, owner, wq_ref, wk_ref, wv_ref, sums, sems = rest[count:]
+    depth, query_cols = wq_ref.shape
+    kv_cols = wk_ref.shape[1]
+    rows = depth // pieces
+    small = [
+        pltpu.make_async_copy(source, target, sems.at[i])
+        for i, (source, target) in enumerate(
+            ((x_any, x_ref), (gain_any, gain_ref), (owner_any, owner), (wk_any, wk_ref), (wv_any, wv_ref))
+        )
+    ]
+    large = [
+        pltpu.make_async_copy(
+            wq_any.at[p * rows : (p + 1) * rows], wq_ref.at[p * rows : (p + 1) * rows], sems.at[5 + p]
+        )
+        for p in range(pieces)
+    ]
+    for copy in small[:3] + large + small[3:]:
+        copy.start()
+    for copy in small[:3]:
+        copy.wait()
+    x = x_ref[...].astype(F32)
+    scaled = (x * gain_ref[...].astype(F32)).astype(BF16)
+    squares = jnp.sum(x * x, axis=1, keepdims=True)
+    end = query_cols + 2 * kv_cols
+    sums[:, end:] = jnp.broadcast_to(squares, (x.shape[0], LANES))
+    for p in range(pieces):
+        large[p].wait()
+        part = jnp.dot(
+            scaled[:, p * rows : (p + 1) * rows],
+            wq_ref[p * rows : (p + 1) * rows, :],
+            preferred_element_type=F32,
+        )
+        sums[:, :query_cols] = part if p == 0 else sums[:, :query_cols] + part
+    for copy, weight_ref, at in ((small[3], wk_ref, query_cols), (small[4], wv_ref, query_cols + kv_cols)):
+        copy.wait()
+        matmul_into(sums, at, scaled, weight_ref, 512)
+    slots = x.shape[0] // count
+    me = lax.axis_index("mem")
+    for s in range(count):
+        for k in range(slots):
+            request = owner[(me ^ s) * slots + k]
+            out_refs[s][k : k + 1, :] = sums[pl.ds(request, 1), :]
+
+
 def attention_kernel(count, width, kv_heads, lengths_ref, cos_ref, sin_ref, *rest):
     pieces = rest[:count]
-    key_ref, value_ref, out_ref, head_scr, score_scr, row_scr = rest[count:]
+    key_ref, value_ref = rest[count : count + 2]
+    out_ref, head_scr, score_scr, row_scr = rest[count + 2 :]
     slots, context = key_ref.shape[:2]
     query_heads = out_ref.shape[1] // HD
     group = query_heads // kv_heads
-    chunk = min(512, context)
+    chunk = min(1024, context)
     total = total_of(pieces)
     wide = total.shape[1]
     squares = total[:, wide - LANES : wide - LANES + 1]
@@ -100,8 +148,10 @@
     head_of = lax.broadcasted_iota(jnp.int32, (query_heads, 1), 0) // group
     for s in range(slots):
         for h in range(all_heads):
-            head_scr[h : h + 1, :] = total[s : s + 1, h * HD : (h + 1) * HD]
-        rotating = head_scr[: query_heads + kv_heads, :]
+            head_scr[s, h : h + 1, :] = total[s : s + 1, h * HD : (h + 1) * HD]
+    spreads, own_scores, new_values, peaks = [], [], [], []
+    for s in range(slots):
+        rotating = head_scr[s, : query_heads + kv_heads, :]
         rolled = pltpu.roll(rotating, HD // 2, 1)
         turned = jnp.where(lane < HD // 2, -rolled, rolled)
         rotated = (rotating * cos_ref[s : s + 1, :] + turned * sin_ref[s : s + 1, :]).astype(BF16)
@@ -114,52 +164,49 @@
             mine = head_of == g
             new_key = jnp.where(mine, rotated[query_heads + g : query_heads + g + 1], new_key)
             value_row = query_heads + kv_heads + g
-            new_value = jnp.where(mine, head_scr[value_row : value_row + 1, :], new_value)
+            new_value = jnp.where(mine, head_scr[s, value_row : value_row + 1, :], new_value)
             spread.append(jnp.where(mine, queries, 0.0))
-        spread = jnp.concatenate(spread, axis=1).astype(BF16)
-        own_score = jnp.sum(queries * new_key, axis=1, keepdims=True) * scale
-        new_value = new_value.astype(BF16).astype(F32)
-        length = lengths_ref[s]
-        chunks = (length + chunk - 1) // chunk
-
-        def score(c, peak):
-            at = pl.multiple_of(c * chunk, chunk)
+        spreads.append(jnp.concatenate(spread, axis=1).astype(BF16))
+        own_scores.append(jnp.sum(queries * new_key, axis=1, keepdims=True) * scale)
+        new_values.append(new_value.astype(BF16).astype(F32))
+        peaks.append(jnp.full((query_heads, LANES), -jnp.inf, F32))
+    position = lax.broadcasted_iota(jnp.int32, (1, chunk), 1)
+    for at in range(0, context, chunk):
+        for s in range(slots):
             scores = lax.dot_general(
-                spread,
-                key_ref[s, pl.ds(at, chunk), :],
+                spreads[s],
+                key_ref[s, at : at + chunk, :],
                 (((1,), (1,)), ((), ())),
                 preferred_element_type=F32,
             )
-            position = at + lax.broadcasted_iota(jnp.int32, (1, chunk), 1)
-            scores = jnp.where(position < length, scores * scale, -jnp.inf)
-            score_scr[:, pl.ds(at, chunk)] = scores
-            return jnp.maximum(peak, jnp.max(scores, axis=1, keepdims=True))
-
-        peak = lax.fori_loop(0, chunks, score, own_score)
-        own = jnp.exp(own_score - peak)
-
-        def mix(c, carry):
-            mixed, weight_sum = carry
-            at = pl.multiple_of(c * chunk, chunk)
-            soft = jnp.exp(score_scr[:, pl.ds(at, chunk)] - peak)
-            mixed = mixed + jnp.dot(
-                soft.astype(BF16), value_ref[s, pl.ds(at, chunk), :], preferred_element_type=F32
+            scores = jnp.where(position + at < lengths_ref[s : s + 1, :1], scores * scale, -jnp.inf)
+            score_scr[s, :, at : at + chunk] = scores
+            for i in range(0, chunk, LANES):
+                peaks[s] = jnp.maximum(peaks[s], scores[:, i : i + LANES])
+    owns, sums, mixes = [], [], []
+    for s in range(slots):
+        peaks[s] = jnp.maximum(jnp.max(peaks[s], axis=1, keepdims=True), own_scores[s])
+        owns.append(jnp.exp(own_scores[s] - peaks[s]))
+        sums.append(jnp.zeros((query_heads, LANES), F32))
+        mixes.append(jnp.zeros((query_heads, kv_heads * HD), F32))
+    for at in range(0, context, chunk):
+        for s in range(slots):
+            soft = jnp.exp(score_scr[s, :, at : at + chunk] - peaks[s])
+            for i in range(0, chunk, LANES):
+                sums[s] = sums[s] + soft[:, i : i + LANES]
+            mixes[s] = mixes[s] + jnp.dot(
+                soft.astype(BF16), value_ref[s, at : at + chunk, :], preferred_element_type=F32
             )
-            return mixed, weight_sum + jnp.sum(soft, axis=1, keepdims=True)
-
-        mixed, weight_sum = lax.fori_loop(
-            0,
-            chunks,
-            mix,
-            (jnp.zeros((query_heads, kv_heads * HD), F32), jnp.zeros((query_heads, 1), F32)),
-        )
+    for s in range(slots):
         picked = jnp.zeros((query_heads, HD), F32)
         for g in range(kv_heads):
-            picked = jnp.where(head_of == g, mixed[:, g * HD : (g + 1) * HD], picked)
-        picked = picked + own.astype(BF16).astype(F32) * new_value
-        head_scr[:query_heads, :] = picked / (weight_sum + own)
+            picked = jnp.where(head_of == g, mixes[s][:, g * HD : (g + 1) * HD], picked)
+        picked = picked + owns[s].astype(BF16).astype(F32) * new_values[s]
+        total_weight = jnp.sum(sums[s], axis=1, keepdims=True) + owns[s]
+        head_scr[s, :query_heads, :] = picked / total_weight
+    for s in range(slots):
         for h in range(query_heads):
-            row_scr[s : s + 1, h * HD : (h + 1) * HD] = head_scr[h : h + 1, :]
+            row_scr[s : s + 1, h * HD : (h + 1) * HD] = head_scr[s, h : h + 1, :]
     out_ref[...] = row_scr[...].astype(BF16)
 
 
@@ -217,7 +264,7 @@
         gate = total_of(pieces, cols=slice(at, at + step)) * factor
         up = total_of(pieces, cols=slice(units + at, units + at + step)) * factor
         hidden_scr[:, at : at + step] = (gate / (1.0 + jnp.exp(-gate)) * up).astype(BF16)
-    matmul_into(out_ref, 0, hidden_scr[...], w_ref, 256)
+    matmul_into(out_ref, 0, hidden_scr[...], w_ref, 512)
 
 
 def finish_kernel(count, x_ref, *rest):
@@ -226,12 +273,12 @@
     out_ref[...] = (x_ref[...].astype(F32) + total_of(pieces)).astype(BF16)
 
 
-def choose_kernel(count, section_ref, x_ref, first_ref, *rest):
+def choose_kernel(count, x_ref, first_ref, *rest):
     pieces = rest[:count]
     out_ref = rest[count]
     second = (x_ref[...].astype(F32) + total_of(pieces)).astype(BF16).astype(F32)
     first = first_ref[...].astype(F32)
-    out_ref[...] = jnp.where(section_ref[0] == 0, first, second).astype(BF16)
+    out_ref[...] = jnp.where(lax.axis_index("section") == 0, first, second).astype(BF16)
 
 
 def per_device(
@@ -257,7 +304,6 @@
     query_cols, kv_cols, units = w_query.shape[2], w_key.shape[2], w_gate.shape[2]
     kv_heads = kv_cols // HD
     me = lax.axis_index("mem")
-    section = lax.axis_index("section").astype(jnp.int32).reshape(1)
 
     group = jnp.arange(requests, dtype=jnp.int32) // slots
     slot_index = (group ^ me) * slots + jnp.arange(requests, dtype=jnp.int32) % slots
@@ -269,6 +315,7 @@
     perm = here.astype(BF16)
     perm_back = (request_of[None, :] == every[:, None]).astype(BF16)
     slot_lengths = jnp.sum(jnp.where(here[:slots], lengths[None, :], 0), axis=1)
+    wide_lengths = jnp.broadcast_to(slot_lengths[:, None], (slots, LANES))
     freqs = ROPE_BASE ** (-(jnp.arange(HD // 2, dtype=F32) * 2.0) / HD)
     angles = slot_lengths.astype(F32)[:, None] * freqs[None, :]
     cosine = jnp.concatenate([jnp.cos(angles)] * 2, axis=-1)
@@ -277,24 +324,64 @@
     head_cols = query_cols + 2 * kv_cols
     term_cols = 2 * units + 3 * LANES
 
-    def layer(x, tag):
-        heads = run(
+    def first_heads():
+        pieces = 8
+        return run(
+            functools.partial(first_heads_kernel, mems, pieces),
+            [((slots, head_cols + LANES), F32)] * mems,
+            [
+                pltpu.with_memory_space_constraint(source, pltpu.HBM)
+                for source in (hidden_in, attn_gain, owner_order, w_query[0], w_key[0], w_value[0])
+            ],
+            specs=[pl.BlockSpec(memory_space=pltpu.HBM)] * 6,
+            scratch=[
+                pltpu.VMEM((requests, local_width), BF16),
+                pltpu.VMEM((1, local_width), BF16),
+                pltpu.SMEM((requests,), jnp.int32),
+                pltpu.VMEM((local_width, query_cols), BF16),
+                pltpu.VMEM((local_width, kv_cols), BF16),
+                pltpu.VMEM((local_width, kv_cols), BF16),
+                pltpu.VMEM((requests, head_cols + LANES), F32),
+                pltpu.SemaphoreType.DMA((5 + pieces,)),
+            ],
+            grant=12,
+            name="heads_0",
+        )
+
+    def heads_of(x, tag):
+        return run(
             functools.partial(heads_kernel, mems),
             [((slots, head_cols + LANES), F32)] * mems,
             [x, attn_gain, perm, w_query[0], w_key[0], w_value[0]],
             scratch=[pltpu.VMEM((requests, head_cols + LANES), F32)],
             name="heads" + tag,
         )
+
+    def window(value, after):
+        def kernel(value_ref, after_ref, out_ref):
+            out_ref[...] = value_ref[...]
+
+        return run(kernel, (value.shape, value.dtype), [value, after], name="window")
+
+    def layer(x, heads, tag):
         attended = run(
             functools.partial(attention_kernel, mems, width, kv_heads),
             ((slots, query_cols), BF16),
-            [slot_lengths, cosine, sine, heads[0], *partners(heads, "mem"), key_cache[0], value_cache[0]],
-            specs=[IN_SMEM] + [IN_VMEM] * (mems + 4),
+            [
+                wide_lengths,
+                window(cosine, heads[0]) if tag == "_0" else cosine,
+                sine,
+                heads[0],
+                *partners(heads, "mem"),
+                key_cache[0],
+                value_cache[0],
+            ],
             scratch=[
-                pltpu.VMEM((-(-head_cols // HD // 8) * 8, HD), F32),
-                pltpu.VMEM((query_cols // HD, key_cache.shape[2]), F32),
+                pltpu.VMEM((slots, -(-head_cols // HD // 8) * 8, HD), F32),
+                pltpu.VMEM((slots, query_cols // HD, key_cache.shape[2]), F32),
                 pltpu.VMEM((slots, query_cols), F32),
             ],
+            grant=3,
             name="attention" + tag,
         )
         projected = run(
@@ -315,11 +402,12 @@
             ((requests, local_width), BF16),
             [w_down[0], terms, *partners([terms] * mems, "mem")],
             scratch=[pltpu.VMEM((requests, units), BF16)],
+            keep=[window(cosine, terms)] if tag == "_1" else (),
             name="down" + tag,
         )
         return after, [down, *partners([down] * tps, "tp")]
 
-    after, downs = layer(hidden_in, "_0")
+    after, downs = layer(hidden_in, first_heads(), "_0")
     first = run(
         functools.partial(finish_kernel, tps),
         ((requests, local_width), BF16),
@@ -328,12 +416,11 @@
     )
     sections = lax.axis_size("section")
     passed = lax.ppermute(first, "section", [(i, (i + 1) % sections) for i in range(sections)])
-    after, downs = layer(passed, "_1")
+    after, downs = layer(passed, heads_of(passed, "_1"), "_1")
     result = run(
         functools.partial(choose_kernel, tps),
         ((requests, local_width), BF16),
-        [section, after, first, *downs],
-        specs=[IN_SMEM] + [IN_VMEM] * (tps + 2),
+        [after, first, *downs],
         name="choose",
     )
     return result[None]

time: 135 us -> 101 us (0.75); the launches traced: 137 us -> 101 us
  local copies, waits for them, and re-layouts: 23.7 us -> 0.24 us
  Pallas kernels: 39.2 us -> 25.4 us
    unnamed x56 -> x62, local copies, waits for them, and re-layouts: 23.7 us -> 0.17 us
    pallas_call x12 -> x14, Pallas kernels: 39.2 us -> 25.4 us  [run(): pl.pallas_call(without_kept, out_shape=[jax.ShapeDtypeStruct(shape, dtype...]
  transfers between devices with their start and end apart: 31 -> 31, of which waited for: 26 -> 27; matrix products, arithmetic and copies ran while one was open for 0% -> 1% of each run, Pallas kernels for 0% -> 0%
where the time goes in v2:
time: 101 us
  starting transfers between devices  40.1 us (40%)
  waiting for transfers between devices  33.8 us (33%)
  Pallas kernels  25.4 us (25%)
    ppermute x30, starting transfers between devices, partners(): lax.ppermute(values[s], axis, [(i, i ^ s) for i in range(count)])  40.1 us
    ppermute x30, waiting for transfers between devices, partners(): lax.ppermute(values[s], axis, [(i, i ^ s) for i in range(count)])  32.6 us
    pallas_call x14, Pallas kernels, run(): pl.pallas_call(without_kept, out_shape=[jax.ShapeDtypeStruct(shape, dtype...  25.4 us
  transfers between devices with their start and end apart: 31, of which 27 were waited for; matrix products, arithmetic and copies ran while one was open for 1% of the time, Pallas kernels for 0%

profile of v2, /device:TPU:0, one launch (start us, length us, event | category | flops | bytes accessed | tf_op | source)
XLA Modules:
  0.0 100.6 jit_solution(10472276624624602861)
XLA Ops:
  0.0 4.7 %heads_0.1 = (f32[2,2688]{1,0:T(2,128)S(1)}, f32[2,2688]{1,0:T(2,128)S(1)}, f32[2,2688]{1,0:T(2,128)S(1)}, f32[2,2688]{1,0:T(2,128)S(1)}) custom-call(bf16[8,2048]{1,0:T(8,128)(2,1)} %refs_0_.3, bf16[1,2048]{1,0:T(2,128)(2,1)} %refs_1_.6, s32[8]{0:T(128)} %refs_2_.1, bf16[2048,2048]{1,0:T(8,128)(2,1)} %bitcast.24, bf16[2048,256]{1,0:T(8,128)(2,1)} %bitcast.38, ...), custom_call_target="tpu_custom_call" | custom-call | flops 23000000512 | tf_op jit(solution)/shard_map/heads_0/pallas_call | solution.py:33
  4.7 3.0 %collective-permute-start = (f32[2,2688]{1,0:T(2,128)S(1)}, f32[2,2688]{1,0:T(2,128)S(1)}, u32[]{:S(2)}, u32[]{:S(2)}) collective-permute-start(f32[2,2688]{1,0:T(2,128)S(1)} %get-tuple-element.18), channel_id=1, source_target_pairs={{0,1},{1,0},{2,3},{3,2},{4,5},{5,4},{6,7},{7,6},{8,9},{9,8},{10,11... | collective-permute-start | bytes 64520 | tf_op jit(solution)/shard_map/ppermute | solution.py:49
  7.7 1.5 %collective-permute-start.1 = (f32[2,2688]{1,0:T(2,128)S(1)}, f32[2,2688]{1,0:T(2,128)S(1)}, u32[]{:S(2)}, u32[]{:S(2)}) collective-permute-start(f32[2,2688]{1,0:T(2,128)S(1)} %get-tuple-element.19), channel_id=1, source_target_pairs={{0,2},{1,3},{2,0},{3,1},{4,6},{5,7},{6,4},{7,5},{8,10},{9,11},{10,... | collective-permute-start | bytes 64520 | tf_op jit(solution)/shard_map/ppermute | solution.py:49
  9.9 1.6 %collective-permute-done.1.refs_5_ = f32[2,2688]{1,0:T(2,128)S(1)} collective-permute-done((f32[2,2688]{1,0:T(2,128)S(1)}, f32[2,2688]{1,0:T(2,128)S(1)}, u32[]{:S(2)}, u32[]{:S(2)}) %collective-permute-start.1) | collective-permute-done | bytes 21536 | tf_op jit(solution)/shard_map/ppermute | solution.py:49
  11.5 2.4 %collective-permute-done.2.refs_6_ = f32[2,2688]{1,0:T(2,128)S(1)} collective-permute-done((f32[2,2688]{1,0:T(2,128)S(1)}, f32[2,2688]{1,0:T(2,128)S(1)}, u32[]{:S(2)}, u32[]{:S(2)}) %collective-permute-start.2) | collective-permute-done | bytes 21536 | tf_op jit(solution)/shard_map/ppermute | solution.py:49
  14.0 1.9 %attention_0.1.refs_2_ = bf16[2,2048]{1,0:T(2,128)(2,1)S(1)} custom-call(s32[2,128]{1,0:T(2,128)S(1)} %broadcast_in_dim.47.refs_0_, f32[2,128]{1,0:T(2,128)S(1)} %window.2.refs_1_, f32[2,128]{1,0:T(2,128)S(1)} %get-tuple-element.35.refs_2_, f32[2,2688]{1,0:T(2,128)S(1)} %get-tuple-element.17.refs_1_.refs_3_, f32[2,2688]{1,0:T(2,128)S(1)} %collective-permute-done.refs_4_, ...), custom_call_target="tpu_custom_call" | custom-call | flops 23000000512 | tf_op jit(solution)/shard_map/attention_0/pallas_call | solution.py:33
  16.0 2.3 %collective-permute-start.5 = (bf16[2,2048]{1,0:T(2,128)(2,1)S(1)}, bf16[2,2048]{1,0:T(2,128)(2,1)S(1)}, u32[]{:S(2)}, u32[]{:S(2)}) collective-permute-start(bf16[2,2048]{1,0:T(2,128)(2,1)S(1)} %attention_0.1.refs_2_), channel_id=1, source_target_pairs={{0,3},{1,2},{2,1},{3,0},{4,7},{5,6},{6,5},{7,4},{8,11},{9,10},{10,... | collective-permute-start | bytes 24584 | tf_op jit(solution)/shard_map/ppermute | solution.py:49
  19.5 1.1 %collective-permute-done.5.refs_5_ = bf16[2,2048]{1,0:T(2,128)(2,1)S(1)} collective-permute-done((bf16[2,2048]{1,0:T(2,128)(2,1)S(1)}, bf16[2,2048]{1,0:T(2,128)(2,1)S(1)}, u32[]{:S(2)}, u32[]{:S(2)}) %collective-permute-start.5) | collective-permute-done | bytes 8224 | tf_op jit(solution)/shard_map/ppermute | solution.py:49
  20.6 1.3 %collective-permute-done.4.refs_4_ = bf16[2,2048]{1,0:T(2,128)(2,1)S(1)} collective-permute-done((bf16[2,2048]{1,0:T(2,128)(2,1)S(1)}, bf16[2,2048]{1,0:T(2,128)(2,1)S(1)}, u32[]{:S(2)}, u32[]{:S(2)}) %collective-permute-start.4) | collective-permute-done | bytes 8224 | tf_op jit(solution)/shard_map/ppermute | solution.py:49
  22.5 1.3 %project_0.1.refs_4_ = bf16[8,2048]{1,0:T(8,128)(2,1)S(1)} custom-call(bf16[8,8]{1,0:T(8,128)(2,1)S(1)} %get-tuple-element.33.refs_0_, bf16[2048,2048]{1,0:T(8,128)(2,1)S(1)} %bitcast.30, bf16[2,2048]{1,0:T(2,128)(2,1)S(1)} %attention_0.1.refs_2_, bf16[2,2048]{1,0:T(2,128)(2,1)S(1)} %collective-permute-done.3.refs_3_, ...), custom_call_target="tpu_custom_call" | custom-call | flops 23000000512 | tf_op jit(solution)/shard_map/project_0/pallas_call | solution.py:33
  23.8 3.6 %collective-permute-start.8 = (bf16[8,2048]{1,0:T(8,128)(2,1)S(1)}, bf16[8,2048]{1,0:T(8,128)(2,1)S(1)}, u32[]{:S(2)}, u32[]{:S(2)}) collective-permute-start(bf16[8,2048]{1,0:T(8,128)(2,1)S(1)} %project_0.1.refs_4_), channel_id=1, source_target_pairs={{0,12},{4,8},{8,4},{12,0},{1,13},{5,9},{9,5},{13,1},{2,14},{6,10},... | collective-permute-start | bytes 98312 | tf_op jit(solution)/shard_map/ppermute | solution.py:49
  28.2 1.6 %collective-permute-done.8.refs_7_ = bf16[8,2048]{1,0:T(8,128)(2,1)S(1)} collective-permute-done((bf16[8,2048]{1,0:T(8,128)(2,1)S(1)}, bf16[8,2048]{1,0:T(8,128)(2,1)S(1)}, u32[]{:S(2)}, u32[]{:S(2)}) %collective-permute-start.8) | collective-permute-done | bytes 32800 | tf_op jit(solution)/shard_map/ppermute | solution.py:49
  29.8 2.4 %collective-permute-done.7.refs_6_ = bf16[8,2048]{1,0:T(8,128)(2,1)S(1)} collective-permute-done((bf16[8,2048]{1,0:T(8,128)(2,1)S(1)}, bf16[8,2048]{1,0:T(8,128)(2,1)S(1)}, u32[]{:S(2)}, u32[]{:S(2)}) %collective-permute-start.7) | collective-permute-done | bytes 32800 | tf_op jit(solution)/shard_map/ppermute | solution.py:49
  32.4 3.9 %terms_0.1 = (bf16[8,2048]{1,0:T(8,128)(2,1)S(1)}, bf16[8,7552]{1,0:T(8,128)(2,1)S(1)}) custom-call(bf16[8,2048]{1,0:T(8,128)(2,1)S(1)} %copy-done.4, bf16[1,2048]{1,0:T(2,128)(2,1)S(1)} %copy-done.6, bf16[2048,3584]{1,0:T(8,128)(2,1)S(1)} %bitcast.12, bf16[2048,3584]{1,0:T(8,128)(2,1)S(1)} %bitcast.16, bf16[8,2048]{1,0:T(8,128)(2,1)S(1)} %project_0.1.refs_4_, ...), custom_call_target="tpu_custom_call" | custom-call | flops 23000000512 | tf_op jit(solution)/shard_map/terms_0/pallas_call | solution.py:33
  36.3 1.5 %collective-permute-start.11 = (bf16[8,7552]{1,0:T(8,128)(2,1)S(1)}, bf16[8,7552]{1,0:T(8,128)(2,1)S(1)}, u32[]{:S(2)}, u32[]{:S(2)}) collective-permute-start(bf16[8,7552]{1,0:T(8,128)(2,1)S(1)} %get-tuple-element.22.refs_1_), channel_id=1, source_target_pairs={{0,3},{1,2},{2,1},{3,0},{4,7},{5,6},{6,5},{7,4},{8,11},{9,10},{10,... | collective-permute-start | bytes 362504 | tf_op jit(solution)/shard_map/ppermute | solution.py:49
  38.5 1.3 %collective-permute-start.9 = (bf16[8,7552]{1,0:T(8,128)(2,1)S(1)}, bf16[8,7552]{1,0:T(8,128)(2,1)S(1)}, u32[]{:S(2)}, u32[]{:S(2)}) collective-permute-start(bf16[8,7552]{1,0:T(8,128)(2,1)S(1)} %get-tuple-element.22.refs_1_), channel_id=1, source_target_pairs={{0,1},{1,0},{2,3},{3,2},{4,5},{5,4},{6,7},{7,6},{8,9},{9,8},{10,11... | collective-permute-start | bytes 362504 | tf_op jit(solution)/shard_map/ppermute | solution.py:49
  39.8 2.3 %collective-permute-done.11.refs_4_ = bf16[8,7552]{1,0:T(8,128)(2,1)S(1)} collective-permute-done((bf16[8,7552]{1,0:T(8,128)(2,1)S(1)}, bf16[8,7552]{1,0:T(8,128)(2,1)S(1)}, u32[]{:S(2)}, u32[]{:S(2)}) %collective-permute-start.11) | collective-permute-done | bytes 120864 | tf_op jit(solution)/shard_map/ppermute | solution.py:49
  42.1 1.2 %collective-permute-done.10.refs_3_ = bf16[8,7552]{1,0:T(8,128)(2,1)S(1)} collective-permute-done((bf16[8,7552]{1,0:T(8,128)(2,1)S(1)}, bf16[8,7552]{1,0:T(8,128)(2,1)S(1)}, u32[]{:S(2)}, u32[]{:S(2)}) %collective-permute-start.10) | collective-permute-done | bytes 120864 | tf_op jit(solution)/shard_map/ppermute | solution.py:49
  43.5 2.1 %down_0.1.refs_1_ = bf16[8,2048]{1,0:T(8,128)(2,1)S(1)} custom-call(bf16[3584,2048]{1,0:T(8,128)(2,1)S(1)} %bitcast.20, bf16[8,7552]{1,0:T(8,128)(2,1)S(1)} %get-tuple-element.22.refs_1_, bf16[8,7552]{1,0:T(8,128)(2,1)S(1)} %collective-permute-done.9.refs_2_, bf16[8,7552]{1,0:T(8,128)(2,1)S(1)} %collective-permute-done.10.refs_3_, ...), custom_call_target="tpu_custom_call" | custom-call | flops 23000000512 | tf_op jit(solution)/shard_map/down_0/pallas_call | solution.py:33
  45.6 1.5 %collective-permute-start.14 = (bf16[8,2048]{1,0:T(8,128)(2,1)S(1)}, bf16[8,2048]{1,0:T(8,128)(2,1)S(1)}, u32[]{:S(2)}, u32[]{:S(2)}) collective-permute-start(bf16[8,2048]{1,0:T(8,128)(2,1)S(1)} %down_0.1.refs_1_), channel_id=1, source_target_pairs={{0,12},{4,8},{8,4},{12,0},{1,13},{5,9},{9,5},{13,1},{2,14},{6,10},... | collective-permute-start | bytes 98312 | tf_op jit(solution)/shard_map/ppermute | solution.py:49
  47.7 2.3 %collective-permute-start.12 = (bf16[8,2048]{1,0:T(8,128)(2,1)S(1)}, bf16[8,2048]{1,0:T(8,128)(2,1)S(1)}, u32[]{:S(2)}, u32[]{:S(2)}) collective-permute-start(bf16[8,2048]{1,0:T(8,128)(2,1)S(1)} %down_0.1.refs_1_), channel_id=1, source_target_pairs={{0,4},{4,0},{8,12},{12,8},{1,5},{5,1},{9,13},{13,9},{2,6},{6,2},{1... | collective-permute-start | bytes 98312 | tf_op jit(solution)/shard_map/ppermute | solution.py:49
  50.0 1.3 %collective-permute-done.14.refs_4_ = bf16[8,2048]{1,0:T(8,128)(2,1)S(1)} collective-permute-done((bf16[8,2048]{1,0:T(8,128)(2,1)S(1)}, bf16[8,2048]{1,0:T(8,128)(2,1)S(1)}, u32[]{:S(2)}, u32[]{:S(2)}) %collective-permute-start.14) | collective-permute-done | bytes 32800 | tf_op jit(solution)/shard_map/ppermute | solution.py:49
  52.4 1.2 %collective-permute-done.15.refs_0_ = bf16[8,2048]{1,0:T(8,128)(2,1)S(1)} collective-permute-done((bf16[8,2048]{1,0:T(8,128)(2,1)S(1)}, bf16[8,2048]{1,0:T(8,128)(2,1)S(1)}, u32[]{:S(2)}, u32[]{:S(2)}) %collective-permute-start.15) | collective-permute-done | bytes 32800 | tf_op jit(solution)/shard_map/ppermute | solution.py:418
  53.6 1.6 %heads_1.1 = (f32[2,2688]{1,0:T(2,128)S(1)}, f32[2,2688]{1,0:T(2,128)S(1)}, f32[2,2688]{1,0:T(2,128)S(1)}, f32[2,2688]{1,0:T(2,128)S(1)}) custom-call(bf16[8,2048]{1,0:T(8,128)(2,1)S(1)} %collective-permute-done.15.refs_0_, bf16[1,2048]{1,0:T(2,128)(2,1)S(1)} %copy-done.5, bf16[8,8]{1,0:T(8,128)(2,1)S(1)} %get-tuple-element.31.refs_2_, ...), custom_call_target="tpu_custom_call" | custom-call | flops 23000000512 | tf_op jit(solution)/shard_map/heads_1/pallas_call | solution.py:33
  55.2 1.3 %collective-permute-start.16 = (f32[2,2688]{1,0:T(2,128)S(1)}, f32[2,2688]{1,0:T(2,128)S(1)}, u32[]{:S(2)}, u32[]{:S(2)}) collective-permute-start(f32[2,2688]{1,0:T(2,128)S(1)} %get-tuple-element.24), channel_id=1, source_target_pairs={{0,1},{1,0},{2,3},{3,2},{4,5},{5,4},{6,7},{7,6},{8,9},{9,8},{10,11... | collective-permute-start | bytes 64520 | tf_op jit(solution)/shard_map/ppermute | solution.py:49
  56.5 1.5 %collective-permute-start.17 = (f32[2,2688]{1,0:T(2,128)S(1)}, f32[2,2688]{1,0:T(2,128)S(1)}, u32[]{:S(2)}, u32[]{:S(2)}) collective-permute-start(f32[2,2688]{1,0:T(2,128)S(1)} %get-tuple-element.25), channel_id=1, source_target_pairs={{0,2},{1,3},{2,0},{3,1},{4,6},{5,7},{6,4},{7,5},{8,10},{9,11},{10,... | collective-permute-start | bytes 64520 | tf_op jit(solution)/shard_map/ppermute | solution.py:49
  59.0 1.2 %collective-permute-done.17.refs_5_ = f32[2,2688]{1,0:T(2,128)S(1)} collective-permute-done((f32[2,2688]{1,0:T(2,128)S(1)}, f32[2,2688]{1,0:T(2,128)S(1)}, u32[]{:S(2)}, u32[]{:S(2)}) %collective-permute-start.17) | collective-permute-done | bytes 21536 | tf_op jit(solution)/shard_map/ppermute | solution.py:49
  60.2 2.4 %collective-permute-done.18.refs_6_ = f32[2,2688]{1,0:T(2,128)S(1)} collective-permute-done((f32[2,2688]{1,0:T(2,128)S(1)}, f32[2,2688]{1,0:T(2,128)S(1)}, u32[]{:S(2)}, u32[]{:S(2)}) %collective-permute-start.18) | collective-permute-done | bytes 21536 | tf_op jit(solution)/shard_map/ppermute | solution.py:49
  62.7 1.9 %attention_1.1.refs_2_ = bf16[2,2048]{1,0:T(2,128)(2,1)S(1)} custom-call(s32[2,128]{1,0:T(2,128)S(1)} %broadcast_in_dim.47.refs_0_, f32[2,128]{1,0:T(2,128)S(1)} %get-tuple-element.34.refs_0_.refs_1_, f32[2,128]{1,0:T(2,128)S(1)} %get-tuple-element.35.refs_2_, f32[2,2688]{1,0:T(2,128)S(1)} %get-tuple-element.23.refs_3_, ...), custom_call_target="tpu_custom_call" | custom-call | flops 23000000512 | tf_op jit(solution)/shard_map/attention_1/pallas_call | solution.py:33
  65.6 1.2 %collective-permute-start.20 = (bf16[2,2048]{1,0:T(2,128)(2,1)S(1)}, bf16[2,2048]{1,0:T(2,128)(2,1)S(1)}, u32[]{:S(2)}, u32[]{:S(2)}) collective-permute-start(bf16[2,2048]{1,0:T(2,128)(2,1)S(1)} %attention_1.1.refs_2_), channel_id=1, source_target_pairs={{0,2},{1,3},{2,0},{3,1},{4,6},{5,7},{6,4},{7,5},{8,10},{9,11},{10,... | collective-permute-start | bytes 24584 | tf_op jit(solution)/shard_map/ppermute | solution.py:49
  66.9 1.5 %collective-permute-start.19 = (bf16[2,2048]{1,0:T(2,128)(2,1)S(1)}, bf16[2,2048]{1,0:T(2,128)(2,1)S(1)}, u32[]{:S(2)}, u32[]{:S(2)}) collective-permute-start(bf16[2,2048]{1,0:T(2,128)(2,1)S(1)} %attention_1.1.refs_2_), channel_id=1, source_target_pairs={{0,1},{1,0},{2,3},{3,2},{4,5},{5,4},{6,7},{7,6},{8,9},{9,8},{10,11... | collective-permute-start | bytes 24584 | tf_op jit(solution)/shard_map/ppermute | solution.py:49
  68.3 1.1 %collective-permute-done.21.refs_5_ = bf16[2,2048]{1,0:T(2,128)(2,1)S(1)} collective-permute-done((bf16[2,2048]{1,0:T(2,128)(2,1)S(1)}, bf16[2,2048]{1,0:T(2,128)(2,1)S(1)}, u32[]{:S(2)}, u32[]{:S(2)}) %collective-permute-start.21) | collective-permute-done | bytes 8224 | tf_op jit(solution)/shard_map/ppermute | solution.py:49
  69.4 1.1 %collective-permute-done.19.refs_3_ = bf16[2,2048]{1,0:T(2,128)(2,1)S(1)} collective-permute-done((bf16[2,2048]{1,0:T(2,128)(2,1)S(1)}, bf16[2,2048]{1,0:T(2,128)(2,1)S(1)}, u32[]{:S(2)}, u32[]{:S(2)}) %collective-permute-start.19) | collective-permute-done | bytes 8224 | tf_op jit(solution)/shard_map/ppermute | solution.py:49
  70.5 1.3 %project_1.1.refs_4_ = bf16[8,2048]{1,0:T(8,128)(2,1)S(1)} custom-call(bf16[8,8]{1,0:T(8,128)(2,1)S(1)} %get-tuple-element.33.refs_0_, bf16[2048,2048]{1,0:T(8,128)(2,1)S(1)} %bitcast.33, bf16[2,2048]{1,0:T(2,128)(2,1)S(1)} %attention_1.1.refs_2_, bf16[2,2048]{1,0:T(2,128)(2,1)S(1)} %collective-permute-done.19.refs_3_, ...), custom_call_target="tpu_custom_call" | custom-call | flops 23000000512 | tf_op jit(solution)/shard_map/project_1/pallas_call | solution.py:33
  71.8 2.4 %collective-permute-start.24 = (bf16[8,2048]{1,0:T(8,128)(2,1)S(1)}, bf16[8,2048]{1,0:T(8,128)(2,1)S(1)}, u32[]{:S(2)}, u32[]{:S(2)}) collective-permute-start(bf16[8,2048]{1,0:T(8,128)(2,1)S(1)} %project_1.1.refs_4_), channel_id=1, source_target_pairs={{0,12},{4,8},{8,4},{12,0},{1,13},{5,9},{9,5},{13,1},{2,14},{6,10},... | collective-permute-start | bytes 98312 | tf_op jit(solution)/shard_map/ppermute | solution.py:49
  75.0 1.2 %collective-permute-start.22 = (bf16[8,2048]{1,0:T(8,128)(2,1)S(1)}, bf16[8,2048]{1,0:T(8,128)(2,1)S(1)}, u32[]{:S(2)}, u32[]{:S(2)}) collective-permute-start(bf16[8,2048]{1,0:T(8,128)(2,1)S(1)} %project_1.1.refs_4_), channel_id=1, source_target_pairs={{0,4},{4,0},{8,12},{12,8},{1,5},{5,1},{9,13},{13,9},{2,6},{6,2},{1... | collective-permute-start | bytes 98312 | tf_op jit(solution)/shard_map/ppermute | solution.py:49
  76.2 1.3 %collective-permute-done.24.refs_7_ = bf16[8,2048]{1,0:T(8,128)(2,1)S(1)} collective-permute-done((bf16[8,2048]{1,0:T(8,128)(2,1)S(1)}, bf16[8,2048]{1,0:T(8,128)(2,1)S(1)}, u32[]{:S(2)}, u32[]{:S(2)}) %collective-permute-start.24) | collective-permute-done | bytes 32800 | tf_op jit(solution)/shard_map/ppermute | solution.py:49
  77.6 1.6 %collective-permute-done.23.refs_6_ = bf16[8,2048]{1,0:T(8,128)(2,1)S(1)} collective-permute-done((bf16[8,2048]{1,0:T(8,128)(2,1)S(1)}, bf16[8,2048]{1,0:T(8,128)(2,1)S(1)}, u32[]{:S(2)}, u32[]{:S(2)}) %collective-permute-start.23) | collective-permute-done | bytes 32800 | tf_op jit(solution)/shard_map/ppermute | solution.py:49
  79.3 3.9 %terms_1.1 = (bf16[8,2048]{1,0:T(8,128)(2,1)S(1)}, bf16[8,7552]{1,0:T(8,128)(2,1)S(1)}) custom-call(bf16[8,2048]{1,0:T(8,128)(2,1)S(1)} %collective-permute-done.15.refs_0_, bf16[1,2048]{1,0:T(2,128)(2,1)S(1)} %copy-done.6, bf16[2048,3584]{1,0:T(8,128)(2,1)S(1)} %bitcast.13, bf16[2048,3584]{1,0:T(8,128)(2,1)S(1)} %bitcast.17, ...), custom_call_target="tpu_custom_call" | custom-call | flops 23000000512 | tf_op jit(solution)/shard_map/terms_1/pallas_call | solution.py:33
  83.2 1.5 %collective-permute-start.27 = (bf16[8,7552]{1,0:T(8,128)(2,1)S(1)}, bf16[8,7552]{1,0:T(8,128)(2,1)S(1)}, u32[]{:S(2)}, u32[]{:S(2)}) collective-permute-start(bf16[8,7552]{1,0:T(8,128)(2,1)S(1)} %get-tuple-element.28.refs_1_), channel_id=1, source_target_pairs={{0,3},{1,2},{2,1},{3,0},{4,7},{5,6},{6,5},{7,4},{8,11},{9,10},{10,... | collective-permute-start | bytes 362504 | tf_op jit(solution)/shard_map/ppermute | solution.py:49
  84.7 1.5 %collective-permute-start.26 = (bf16[8,7552]{1,0:T(8,128)(2,1)S(1)}, bf16[8,7552]{1,0:T(8,128)(2,1)S(1)}, u32[]{:S(2)}, u32[]{:S(2)}) collective-permute-start(bf16[8,7552]{1,0:T(8,128)(2,1)S(1)} %get-tuple-element.28.refs_1_), channel_id=1, source_target_pairs={{0,2},{1,3},{2,0},{3,1},{4,6},{5,7},{6,4},{7,5},{8,10},{9,11},{10,... | collective-permute-start | bytes 362504 | tf_op jit(solution)/shard_map/ppermute | solution.py:49
  86.7 2.3 %collective-permute-done.27.refs_4_ = bf16[8,7552]{1,0:T(8,128)(2,1)S(1)} collective-permute-done((bf16[8,7552]{1,0:T(8,128)(2,1)S(1)}, bf16[8,7552]{1,0:T(8,128)(2,1)S(1)}, u32[]{:S(2)}, u32[]{:S(2)}) %collective-permute-start.27) | collective-permute-done | bytes 120864 | tf_op jit(solution)/shard_map/ppermute | solution.py:49
  89.1 1.2 %collective-permute-done.26.refs_3_ = bf16[8,7552]{1,0:T(8,128)(2,1)S(1)} collective-permute-done((bf16[8,7552]{1,0:T(8,128)(2,1)S(1)}, bf16[8,7552]{1,0:T(8,128)(2,1)S(1)}, u32[]{:S(2)}, u32[]{:S(2)}) %collective-permute-start.26) | collective-permute-done | bytes 120864 | tf_op jit(solution)/shard_map/ppermute | solution.py:49
  91.1 2.1 %down_1.1.refs_2_ = bf16[8,2048]{1,0:T(8,128)(2,1)S(1)} custom-call(bf16[3584,2048]{1,0:T(8,128)(2,1)S(1)} %bitcast.23, bf16[8,7552]{1,0:T(8,128)(2,1)S(1)} %get-tuple-element.28.refs_1_, bf16[8,7552]{1,0:T(8,128)(2,1)S(1)} %collective-permute-done.25.refs_2_, bf16[8,7552]{1,0:T(8,128)(2,1)S(1)} %collective-permute-done.26.refs_3_, ...), custom_call_target="tpu_custom_call" | custom-call | flops 23000000512 | tf_op jit(solution)/shard_map/down_1/pallas_call | solution.py:33
  93.1 1.6 %collective-permute-start.30 = (bf16[8,2048]{1,0:T(8,128)(2,1)S(1)}, bf16[8,2048]{1,0:T(8,128)(2,1)S(1)}, u32[]{:S(2)}, u32[]{:S(2)}) collective-permute-start(bf16[8,2048]{1,0:T(8,128)(2,1)S(1)} %down_1.1.refs_2_), channel_id=1, source_target_pairs={{0,12},{4,8},{8,4},{12,0},{1,13},{5,9},{9,5},{13,1},{2,14},{6,10},... | collective-permute-start | bytes 98312 | tf_op jit(solution)/shard_map/ppermute | solution.py:49
  95.5 2.0 %collective-permute-start.28 = (bf16[8,2048]{1,0:T(8,128)(2,1)S(1)}, bf16[8,2048]{1,0:T(8,128)(2,1)S(1)}, u32[]{:S(2)}, u32[]{:S(2)}) collective-permute-start(bf16[8,2048]{1,0:T(8,128)(2,1)S(1)} %down_1.1.refs_2_), channel_id=1, source_target_pairs={{0,4},{4,0},{8,12},{12,8},{1,5},{5,1},{9,13},{13,9},{2,6},{6,2},{1... | collective-permute-start | bytes 98312 | tf_op jit(solution)/shard_map/ppermute | solution.py:49
  97.5 1.3 %collective-permute-done.30.refs_5_ = bf16[8,2048]{1,0:T(8,128)(2,1)S(1)} collective-permute-done((bf16[8,2048]{1,0:T(8,128)(2,1)S(1)}, bf16[8,2048]{1,0:T(8,128)(2,1)S(1)}, u32[]{:S(2)}, u32[]{:S(2)}) %collective-permute-start.30) | collective-permute-done | bytes 32800 | tf_op jit(solution)/shard_map/ppermute | solution.py:49
  98.9 1.0 %collective-permute-done.29.refs_4_ = bf16[8,2048]{1,0:T(8,128)(2,1)S(1)} collective-permute-done((bf16[8,2048]{1,0:T(8,128)(2,1)S(1)}, bf16[8,2048]{1,0:T(8,128)(2,1)S(1)}, u32[]{:S(2)}, u32[]{:S(2)}) %collective-permute-start.29) | collective-permute-done | bytes 32800 | tf_op jit(solution)/shard_map/ppermute | solution.py:49
  (106 shorter events, 11.6 us)
Async XLA Ops:
  4.7 5.2 %collective-permute-start = (f32[2,2688]{1,0:T(2,128)S(1)}, f32[2,2688]{1,0:T(2,128)S(1)}, u32[]{:S(2)}, u32[]{:S(2)}) collective-permute-start(f32[2,2688]{1,0:T(2,128)S(1)} %get-tuple-element.18), channel_id=1, source_target_pairs={{0,1},{1,0},{2,3},{3,2},{4,5},{5,4},{6,7},{7,6},{8,9},{9,8},{10,11... | collective-permute-start | bytes 64520 | tf_op jit(solution)/shard_map/ppermute | solution.py:49
  7.7 3.8 %collective-permute-start.1 = (f32[2,2688]{1,0:T(2,128)S(1)}, f32[2,2688]{1,0:T(2,128)S(1)}, u32[]{:S(2)}, u32[]{:S(2)}) collective-permute-start(f32[2,2688]{1,0:T(2,128)S(1)} %get-tuple-element.19), channel_id=1, source_target_pairs={{0,2},{1,3},{2,0},{3,1},{4,6},{5,7},{6,4},{7,5},{8,10},{9,11},{10,... | collective-permute-start | bytes 64520 | tf_op jit(solution)/shard_map/ppermute | solution.py:49
  9.2 4.7 %collective-permute-start.2 = (f32[2,2688]{1,0:T(2,128)S(1)}, f32[2,2688]{1,0:T(2,128)S(1)}, u32[]{:S(2)}, u32[]{:S(2)}) collective-permute-start(f32[2,2688]{1,0:T(2,128)S(1)} %get-tuple-element.20), channel_id=1, source_target_pairs={{0,3},{1,2},{2,1},{3,0},{4,7},{5,6},{6,5},{7,4},{8,11},{9,10},{10,... | collective-permute-start | bytes 64520 | tf_op jit(solution)/shard_map/ppermute | solution.py:49
  9.9 12.6 %slice-start.18 = ((s8[8388608]{0:T(1024)(128)(4,1)}), s8[4194304]{0:T(1024)(128)(4,1)S(1)}, s32[]{:S(2)}) async-start(s8[8388608]{0:T(1024)(128)(4,1)} %bitcast.28), calls=%async_computation.18 | async-start | bytes 8388608
  14.0 18.3 %slice-start = ((s8[14680064]{0:T(1024)(128)(4,1)}), s8[4194304]{0:T(1024)(128)(4,1)S(1)}, s32[]{:S(2)}) async-start(s8[14680064]{0:T(1024)(128)(4,1)} %bitcast.10), calls=%async_computation | async-start | bytes 8388608
  14.0 18.3 %slice-start.1 = ((s8[14680064]{0:T(1024)(128)(4,1)}), s8[4194304]{0:T(1024)(128)(4,1)S(1)}, s32[]{:S(2)}) async-start(s8[14680064]{0:T(1024)(128)(4,1)} %bitcast.10), calls=%async_computation.1 | async-start | bytes 8388608
  14.0 18.3 %slice-start.4 = ((s8[14680064]{0:T(1024)(128)(4,1)}), s8[4194304]{0:T(1024)(128)(4,1)S(1)}, s32[]{:S(2)}) async-start(s8[14680064]{0:T(1024)(128)(4,1)} %bitcast.14), calls=%async_computation.4 | async-start | bytes 8388608
  14.0 18.3 %slice-start.5 = ((s8[14680064]{0:T(1024)(128)(4,1)}), s8[4194304]{0:T(1024)(128)(4,1)S(1)}, s32[]{:S(2)}) async-start(s8[14680064]{0:T(1024)(128)(4,1)} %bitcast.14), calls=%async_computation.5 | async-start | bytes 8388608
  16.0 4.6 %collective-permute-start.5 = (bf16[2,2048]{1,0:T(2,128)(2,1)S(1)}, bf16[2,2048]{1,0:T(2,128)(2,1)S(1)}, u32[]{:S(2)}, u32[]{:S(2)}) collective-permute-start(bf16[2,2048]{1,0:T(2,128)(2,1)S(1)} %attention_0.1.refs_2_), channel_id=1, source_target_pairs={{0,3},{1,2},{2,1},{3,0},{4,7},{5,6},{6,5},{7,4},{8,11},{9,10},{10,... | collective-permute-start | bytes 24584 | tf_op jit(solution)/shard_map/ppermute | solution.py:49
  18.3 3.7 %collective-permute-start.4 = (bf16[2,2048]{1,0:T(2,128)(2,1)S(1)}, bf16[2,2048]{1,0:T(2,128)(2,1)S(1)}, u32[]{:S(2)}, u32[]{:S(2)}) collective-permute-start(bf16[2,2048]{1,0:T(2,128)(2,1)S(1)} %attention_0.1.refs_2_), channel_id=1, source_target_pairs={{0,2},{1,3},{2,0},{3,1},{4,6},{5,7},{6,4},{7,5},{8,10},{9,11},{10,... | collective-permute-start | bytes 24584 | tf_op jit(solution)/shard_map/ppermute | solution.py:49
  18.8 3.7 %collective-permute-start.3 = (bf16[2,2048]{1,0:T(2,128)(2,1)S(1)}, bf16[2,2048]{1,0:T(2,128)(2,1)S(1)}, u32[]{:S(2)}, u32[]{:S(2)}) collective-permute-start(bf16[2,2048]{1,0:T(2,128)(2,1)S(1)} %attention_0.1.refs_2_), channel_id=1, source_target_pairs={{0,1},{1,0},{2,3},{3,2},{4,5},{5,4},{6,7},{7,6},{8,9},{9,8},{10,11... | collective-permute-start | bytes 24584 | tf_op jit(solution)/shard_map/ppermute | solution.py:49
  22.4 9.9 %slice-start.3 = ((s8[14680064]{0:T(1024)(128)(4,1)}), s8[2097152]{0:T(1024)(128)(4,1)S(1)}, s32[]{:S(2)}) async-start(s8[14680064]{0:T(1024)(128)(4,1)} %bitcast.10), calls=%async_computation.3 | async-start | bytes 4194304
  22.5 21.0 %slice-start.8 = ((s8[14680064]{0:T(1024)(128)(4,1)}), s8[2097152]{0:T(1024)(128)(4,1)S(1)}, s32[]{:S(2)}) async-start(s8[14680064]{0:T(1024)(128)(4,1)} %bitcast.18), calls=%async_computation.8 | async-start | bytes 4194304
  22.5 21.0 %slice-start.9 = ((s8[14680064]{0:T(1024)(128)(4,1)}), s8[4194304]{0:T(1024)(128)(4,1)S(1)}, s32[]{:S(2)}) async-start(s8[14680064]{0:T(1024)(128)(4,1)} %bitcast.18), calls=%async_computation.9 | async-start | bytes 8388608
  23.8 6.0 %collective-permute-start.8 = (bf16[8,2048]{1,0:T(8,128)(2,1)S(1)}, bf16[8,2048]{1,0:T(8,128)(2,1)S(1)}, u32[]{:S(2)}, u32[]{:S(2)}) collective-permute-start(bf16[8,2048]{1,0:T(8,128)(2,1)S(1)} %project_0.1.refs_4_), channel_id=1, source_target_pairs={{0,12},{4,8},{8,4},{12,0},{1,13},{5,9},{9,5},{13,1},{2,14},{6,10},... | collective-permute-start | bytes 98312 | tf_op jit(solution)/shard_map/ppermute | solution.py:49
  27.4 4.8 %collective-permute-start.7 = (bf16[8,2048]{1,0:T(8,128)(2,1)S(1)}, bf16[8,2048]{1,0:T(8,128)(2,1)S(1)}, u32[]{:S(2)}, u32[]{:S(2)}) collective-permute-start(bf16[8,2048]{1,0:T(8,128)(2,1)S(1)} %project_0.1.refs_4_), channel_id=1, source_target_pairs={{0,8},{4,12},{8,0},{12,4},{1,9},{5,13},{9,1},{13,5},{2,10},{6,14},... | collective-permute-start | bytes 98312 | tf_op jit(solution)/shard_map/ppermute | solution.py:49
  27.4 4.8 %collective-permute-start.6 = (bf16[8,2048]{1,0:T(8,128)(2,1)S(1)}, bf16[8,2048]{1,0:T(8,128)(2,1)S(1)}, u32[]{:S(2)}, u32[]{:S(2)}) collective-permute-start(bf16[8,2048]{1,0:T(8,128)(2,1)S(1)} %project_0.1.refs_4_), channel_id=1, source_target_pairs={{0,4},{4,0},{8,12},{12,8},{1,5},{5,1},{9,13},{13,9},{2,6},{6,2},{1... | collective-permute-start | bytes 98312 | tf_op jit(solution)/shard_map/ppermute | solution.py:49
  32.4 11.1 %slice-start.10 = ((s8[14680064]{0:T(1024)(128)(4,1)}), s8[4194304]{0:T(1024)(128)(4,1)S(1)}, s32[]{:S(2)}) async-start(s8[14680064]{0:T(1024)(128)(4,1)} %bitcast.18), calls=%async_computation.10 | async-start | bytes 8388608
  32.4 11.1 %slice-start.11 = ((s8[14680064]{0:T(1024)(128)(4,1)}), s8[4194304]{0:T(1024)(128)(4,1)S(1)}, s32[]{:S(2)}) async-start(s8[14680064]{0:T(1024)(128)(4,1)} %bitcast.18), calls=%async_computation.11 | async-start | bytes 8388608
  32.4 21.2 %slice-start.16 = ((s8[8388608]{0:T(1024)(128)(4,1)}), s8[4194304]{0:T(1024)(128)(4,1)S(1)}, s32[]{:S(2)}) async-start(s8[8388608]{0:T(1024)(128)(4,1)} %bitcast.25), calls=%async_computation.16 | async-start | bytes 8388608
  36.3 5.8 %collective-permute-start.11 = (bf16[8,7552]{1,0:T(8,128)(2,1)S(1)}, bf16[8,7552]{1,0:T(8,128)(2,1)S(1)}, u32[]{:S(2)}, u32[]{:S(2)}) collective-permute-start(bf16[8,7552]{1,0:T(8,128)(2,1)S(1)} %get-tuple-element.22.refs_1_), channel_id=1, source_target_pairs={{0,3},{1,2},{2,1},{3,0},{4,7},{5,6},{6,5},{7,4},{8,11},{9,10},{10,... | collective-permute-start | bytes 362504 | tf_op jit(solution)/shard_map/ppermute | solution.py:49
  37.8 5.6 %collective-permute-start.10 = (bf16[8,7552]{1,0:T(8,128)(2,1)S(1)}, bf16[8,7552]{1,0:T(8,128)(2,1)S(1)}, u32[]{:S(2)}, u32[]{:S(2)}) collective-permute-start(bf16[8,7552]{1,0:T(8,128)(2,1)S(1)} %get-tuple-element.22.refs_1_), channel_id=1, source_target_pairs={{0,2},{1,3},{2,0},{3,1},{4,6},{5,7},{6,4},{7,5},{8,10},{9,11},{10,... | collective-permute-start | bytes 362504 | tf_op jit(solution)/shard_map/ppermute | solution.py:49
  38.5 4.9 %collective-permute-start.9 = (bf16[8,7552]{1,0:T(8,128)(2,1)S(1)}, bf16[8,7552]{1,0:T(8,128)(2,1)S(1)}, u32[]{:S(2)}, u32[]{:S(2)}) collective-permute-start(bf16[8,7552]{1,0:T(8,128)(2,1)S(1)} %get-tuple-element.22.refs_1_), channel_id=1, source_target_pairs={{0,1},{1,0},{2,3},{3,2},{4,5},{5,4},{6,7},{7,6},{8,9},{9,8},{10,11... | collective-permute-start | bytes 362504 | tf_op jit(solution)/shard_map/ppermute | solution.py:49
  43.5 10.1 %slice-start.17 = ((s8[8388608]{0:T(1024)(128)(4,1)}), s8[4194304]{0:T(1024)(128)(4,1)S(1)}, s32[]{:S(2)}) async-start(s8[8388608]{0:T(1024)(128)(4,1)} %bitcast.25), calls=%async_computation.17 | async-start | bytes 8388608
  43.5 10.0 %copy-start.2 = (bf16[1,2048,256]{2,1,0:T(8,128)(2,1)S(1)}, bf16[1,2048,256]{2,1,0:T(8,128)(2,1)}, u32[]{:S(2)}) copy-start(bf16[1,2048,256]{2,1,0:T(8,128)(2,1)} %param.19) | copy-start | bytes 3145732
  43.5 10.0 %copy-start.3 = (bf16[1,2048,256]{2,1,0:T(8,128)(2,1)S(1)}, bf16[1,2048,256]{2,1,0:T(8,128)(2,1)}, u32[]{:S(2)}) copy-start(bf16[1,2048,256]{2,1,0:T(8,128)(2,1)} %param.20) | copy-start | bytes 3145732
  43.5 10.0 %copy-start.5 = (bf16[1,2048]{1,0:T(2,128)(2,1)S(1)}, bf16[1,2048]{1,0:T(2,128)(2,1)}, u32[]{:S(2)}) copy-start(bf16[1,2048]{1,0:T(2,128)(2,1)} %refs_1_.6) | copy-start | bytes 12292
  45.6 5.7 %collective-permute-start.14 = (bf16[8,2048]{1,0:T(8,128)(2,1)S(1)}, bf16[8,2048]{1,0:T(8,128)(2,1)S(1)}, u32[]{:S(2)}, u32[]{:S(2)}) collective-permute-start(bf16[8,2048]{1,0:T(8,128)(2,1)S(1)} %down_0.1.refs_1_), channel_id=1, source_target_pairs={{0,12},{4,8},{8,4},{12,0},{1,13},{5,9},{9,5},{13,1},{2,14},{6,10},... | collective-permute-start | bytes 98312 | tf_op jit(solution)/shard_map/ppermute | solution.py:49
  47.1 4.8 %collective-permute-start.13 = (bf16[8,2048]{1,0:T(8,128)(2,1)S(1)}, bf16[8,2048]{1,0:T(8,128)(2,1)S(1)}, u32[]{:S(2)}, u32[]{:S(2)}) collective-permute-start(bf16[8,2048]{1,0:T(8,128)(2,1)S(1)} %down_0.1.refs_1_), channel_id=1, source_target_pairs={{0,8},{4,12},{8,0},{12,4},{1,9},{5,13},{9,1},{13,5},{2,10},{6,14},... | collective-permute-start | bytes 98312 | tf_op jit(solution)/shard_map/ppermute | solution.py:49
  47.7 4.6 %collective-permute-start.12 = (bf16[8,2048]{1,0:T(8,128)(2,1)S(1)}, bf16[8,2048]{1,0:T(8,128)(2,1)S(1)}, u32[]{:S(2)}, u32[]{:S(2)}) collective-permute-start(bf16[8,2048]{1,0:T(8,128)(2,1)S(1)} %down_0.1.refs_1_), channel_id=1, source_target_pairs={{0,4},{4,0},{8,12},{12,8},{1,5},{5,1},{9,13},{13,9},{2,6},{6,2},{1... | collective-permute-start | bytes 98312 | tf_op jit(solution)/shard_map/ppermute | solution.py:49
  52.3 1.3 %collective-permute-start.15 = (bf16[8,2048]{1,0:T(8,128)(2,1)S(1)}, bf16[8,2048]{1,0:T(8,128)(2,1)S(1)}, u32[]{:S(2)}, u32[]{:S(2)}) collective-permute-start(bf16[8,2048]{1,0:T(8,128)(2,1)S(1)} %finish.1.refs_1_), channel_id=1, source_target_pairs={{0,16},{16,0},{1,17},{17,1},{2,18},{18,2},{3,19},{19,3},{4,20},{20... | collective-permute-start | bytes 98312 | tf_op jit(solution)/shard_map/ppermute | solution.py:418
  53.6 16.9 %slice-start.20 = ((s8[8388608]{0:T(1024)(128)(4,1)}), s8[4194304]{0:T(1024)(128)(4,1)S(1)}, s32[]{:S(2)}) async-start(s8[8388608]{0:T(1024)(128)(4,1)} %bitcast.31), calls=%async_computation.20 | async-start | bytes 8388608
  55.2 3.9 %collective-permute-start.16 = (f32[2,2688]{1,0:T(2,128)S(1)}, f32[2,2688]{1,0:T(2,128)S(1)}, u32[]{:S(2)}, u32[]{:S(2)}) collective-permute-start(f32[2,2688]{1,0:T(2,128)S(1)} %get-tuple-element.24), channel_id=1, source_target_pairs={{0,1},{1,0},{2,3},{3,2},{4,5},{5,4},{6,7},{7,6},{8,9},{9,8},{10,11... | collective-permute-start | bytes 64520 | tf_op jit(solution)/shard_map/ppermute | solution.py:49
  56.4 14.1 %slice-start.21 = ((s8[8388608]{0:T(1024)(128)(4,1)}), s8[4194304]{0:T(1024)(128)(4,1)S(1)}, s32[]{:S(2)}) async-start(s8[8388608]{0:T(1024)(128)(4,1)} %bitcast.31), calls=%async_computation.21 | async-start | bytes 8388608
  56.5 3.8 %collective-permute-start.17 = (f32[2,2688]{1,0:T(2,128)S(1)}, f32[2,2688]{1,0:T(2,128)S(1)}, u32[]{:S(2)}, u32[]{:S(2)}) collective-permute-start(f32[2,2688]{1,0:T(2,128)S(1)} %get-tuple-element.25), channel_id=1, source_target_pairs={{0,2},{1,3},{2,0},{3,1},{4,6},{5,7},{6,4},{7,5},{8,10},{9,11},{10,... | collective-permute-start | bytes 64520 | tf_op jit(solution)/shard_map/ppermute | solution.py:49
  58.0 4.7 %collective-permute-start.18 = (f32[2,2688]{1,0:T(2,128)S(1)}, f32[2,2688]{1,0:T(2,128)S(1)}, u32[]{:S(2)}, u32[]{:S(2)}) collective-permute-start(f32[2,2688]{1,0:T(2,128)S(1)} %get-tuple-element.26), channel_id=1, source_target_pairs={{0,3},{1,2},{2,1},{3,0},{4,7},{5,6},{6,5},{7,4},{8,11},{9,10},{10,... | collective-permute-start | bytes 64520 | tf_op jit(solution)/shard_map/ppermute | solution.py:49
  64.6 4.8 %collective-permute-start.21 = (bf16[2,2048]{1,0:T(2,128)(2,1)S(1)}, bf16[2,2048]{1,0:T(2,128)(2,1)S(1)}, u32[]{:S(2)}, u32[]{:S(2)}) collective-permute-start(bf16[2,2048]{1,0:T(2,128)(2,1)S(1)} %attention_1.1.refs_2_), channel_id=1, source_target_pairs={{0,3},{1,2},{2,1},{3,0},{4,7},{5,6},{6,5},{7,4},{8,11},{9,10},{10,... | collective-permute-start | bytes 24584 | tf_op jit(solution)/shard_map/ppermute | solution.py:49
  65.6 3.8 %collective-permute-start.20 = (bf16[2,2048]{1,0:T(2,128)(2,1)S(1)}, bf16[2,2048]{1,0:T(2,128)(2,1)S(1)}, u32[]{:S(2)}, u32[]{:S(2)}) collective-permute-start(bf16[2,2048]{1,0:T(2,128)(2,1)S(1)} %attention_1.1.refs_2_), channel_id=1, source_target_pairs={{0,2},{1,3},{2,0},{3,1},{4,6},{5,7},{6,4},{7,5},{8,10},{9,11},{10,... | collective-permute-start | bytes 24584 | tf_op jit(solution)/shard_map/ppermute | solution.py:49
  66.9 3.7 %collective-permute-start.19 = (bf16[2,2048]{1,0:T(2,128)(2,1)S(1)}, bf16[2,2048]{1,0:T(2,128)(2,1)S(1)}, u32[]{:S(2)}, u32[]{:S(2)}) collective-permute-start(bf16[2,2048]{1,0:T(2,128)(2,1)S(1)} %attention_1.1.refs_2_), channel_id=1, source_target_pairs={{0,1},{1,0},{2,3},{3,2},{4,5},{5,4},{6,7},{7,6},{8,9},{9,8},{10,11... | collective-permute-start | bytes 24584 | tf_op jit(solution)/shard_map/ppermute | solution.py:49
  71.8 5.7 %collective-permute-start.24 = (bf16[8,2048]{1,0:T(8,128)(2,1)S(1)}, bf16[8,2048]{1,0:T(8,128)(2,1)S(1)}, u32[]{:S(2)}, u32[]{:S(2)}) collective-permute-start(bf16[8,2048]{1,0:T(8,128)(2,1)S(1)} %project_1.1.refs_4_), channel_id=1, source_target_pairs={{0,12},{4,8},{8,4},{12,0},{1,13},{5,9},{9,5},{13,1},{2,14},{6,10},... | collective-permute-start | bytes 98312 | tf_op jit(solution)/shard_map/ppermute | solution.py:49
  74.2 4.9 %collective-permute-start.23 = (bf16[8,2048]{1,0:T(8,128)(2,1)S(1)}, bf16[8,2048]{1,0:T(8,128)(2,1)S(1)}, u32[]{:S(2)}, u32[]{:S(2)}) collective-permute-start(bf16[8,2048]{1,0:T(8,128)(2,1)S(1)} %project_1.1.refs_4_), channel_id=1, source_target_pairs={{0,8},{4,12},{8,0},{12,4},{1,9},{5,13},{9,1},{13,5},{2,10},{6,14},... | collective-permute-start | bytes 98312 | tf_op jit(solution)/shard_map/ppermute | solution.py:49
  75.0 4.3 %collective-permute-start.22 = (bf16[8,2048]{1,0:T(8,128)(2,1)S(1)}, bf16[8,2048]{1,0:T(8,128)(2,1)S(1)}, u32[]{:S(2)}, u32[]{:S(2)}) collective-permute-start(bf16[8,2048]{1,0:T(8,128)(2,1)S(1)} %project_1.1.refs_4_), channel_id=1, source_target_pairs={{0,4},{4,0},{8,12},{12,8},{1,5},{5,1},{9,13},{13,9},{2,6},{6,2},{1... | collective-permute-start | bytes 98312 | tf_op jit(solution)/shard_map/ppermute | solution.py:49
  83.2 5.9 %collective-permute-start.27 = (bf16[8,7552]{1,0:T(8,128)(2,1)S(1)}, bf16[8,7552]{1,0:T(8,128)(2,1)S(1)}, u32[]{:S(2)}, u32[]{:S(2)}) collective-permute-start(bf16[8,7552]{1,0:T(8,128)(2,1)S(1)} %get-tuple-element.28.refs_1_), channel_id=1, source_target_pairs={{0,3},{1,2},{2,1},{3,0},{4,7},{5,6},{6,5},{7,4},{8,11},{9,10},{10,... | collective-permute-start | bytes 362504 | tf_op jit(solution)/shard_map/ppermute | solution.py:49
  84.7 5.6 %collective-permute-start.26 = (bf16[8,7552]{1,0:T(8,128)(2,1)S(1)}, bf16[8,7552]{1,0:T(8,128)(2,1)S(1)}, u32[]{:S(2)}, u32[]{:S(2)}) collective-permute-start(bf16[8,7552]{1,0:T(8,128)(2,1)S(1)} %get-tuple-element.28.refs_1_), channel_id=1, source_target_pairs={{0,2},{1,3},{2,0},{3,1},{4,6},{5,7},{6,4},{7,5},{8,10},{9,11},{10,... | collective-permute-start | bytes 362504 | tf_op jit(solution)/shard_map/ppermute | solution.py:49
  86.2 4.9 %collective-permute-start.25 = (bf16[8,7552]{1,0:T(8,128)(2,1)S(1)}, bf16[8,7552]{1,0:T(8,128)(2,1)S(1)}, u32[]{:S(2)}, u32[]{:S(2)}) collective-permute-start(bf16[8,7552]{1,0:T(8,128)(2,1)S(1)} %get-tuple-element.28.refs_1_), channel_id=1, source_target_pairs={{0,1},{1,0},{2,3},{3,2},{4,5},{5,4},{6,7},{7,6},{8,9},{9,8},{10,11... | collective-permute-start | bytes 362504 | tf_op jit(solution)/shard_map/ppermute | solution.py:49
  93.1 5.7 %collective-permute-start.30 = (bf16[8,2048]{1,0:T(8,128)(2,1)S(1)}, bf16[8,2048]{1,0:T(8,128)(2,1)S(1)}, u32[]{:S(2)}, u32[]{:S(2)}) collective-permute-start(bf16[8,2048]{1,0:T(8,128)(2,1)S(1)} %down_1.1.refs_2_), channel_id=1, source_target_pairs={{0,12},{4,8},{8,4},{12,0},{1,13},{5,9},{9,5},{13,1},{2,14},{6,10},... | collective-permute-start | bytes 98312 | tf_op jit(solution)/shard_map/ppermute | solution.py:49
  94.7 5.2 %collective-permute-start.29 = (bf16[8,2048]{1,0:T(8,128)(2,1)S(1)}, bf16[8,2048]{1,0:T(8,128)(2,1)S(1)}, u32[]{:S(2)}, u32[]{:S(2)}) collective-permute-start(bf16[8,2048]{1,0:T(8,128)(2,1)S(1)} %down_1.1.refs_2_), channel_id=1, source_target_pairs={{0,8},{4,12},{8,0},{12,4},{1,9},{5,13},{9,1},{13,5},{2,10},{6,14},... | collective-permute-start | bytes 98312 | tf_op jit(solution)/shard_map/ppermute | solution.py:49
  95.5 4.4 %collective-permute-start.28 = (bf16[8,2048]{1,0:T(8,128)(2,1)S(1)}, bf16[8,2048]{1,0:T(8,128)(2,1)S(1)}, u32[]{:S(2)}, u32[]{:S(2)}) collective-permute-start(bf16[8,2048]{1,0:T(8,128)(2,1)S(1)} %down_1.1.refs_2_), channel_id=1, source_target_pairs={{0,4},{4,0},{8,12},{12,8},{1,5},{5,1},{9,13},{13,9},{2,6},{6,2},{1... | collective-permute-start | bytes 98312 | tf_op jit(solution)/shard_map/ppermute | solution.py:49
  (14 other events, 116.5 us)

commit v3 on v2

--- a/solution.py
+++ b/solution.py
@@ -21,17 +21,29 @@
 STAGE_US = dict.fromkeys(("heads", "attention", "project", "terms", "down", "window"), 20)
 
 
-def run(kernel, outs, args, specs=None, scratch=(), grant=2, name=None, keep=()):
+def run(kernel, outs, args, specs=None, scratch=(), grant=2, name=None, keep=(), section=None):
     single = isinstance(outs, tuple)
     out_list = [outs] if single else list(outs)
     flops = STAGE_US.get(name.split("_")[0], 0) * 1150000000
     args, held = list(args), len(args)
-
-    def without_kept(*refs):
-        kernel(*refs[:held], *refs[held + len(keep) :])
+    first_out = held + len(keep)
+
+    def in_section(*refs):
+        def work():
+            kernel(*refs[:held], *refs[first_out:])
+
+        if section is None:
+            return work()
+        here = lax.axis_index("section") == section
+        pl.when(here)(work)
+
+        @pl.when(jnp.logical_not(here))
+        def _():
+            for out_ref in refs[first_out : first_out + len(out_list)]:
+                out_ref[...] = jnp.zeros_like(out_ref)
 
     result = pl.pallas_call(
-        without_kept,
+        in_section,
         out_shape=[jax.ShapeDtypeStruct(shape, dtype) for shape, dtype in out_list],
         in_specs=(specs or [IN_VMEM] * held) + [IN_VMEM] * len(keep),
         out_specs=[IN_VMEM] * len(out_list),
@@ -131,7 +143,7 @@
 
 
 def attention_kernel(count, width, kv_heads, lengths_ref, cos_ref, sin_ref, *rest):
-    pieces = rest[:count]
+    pieces = [rest[0], *rest[count - 1 : 0 : -1]]
     key_ref, value_ref = rest[count : count + 2]
     out_ref, head_scr, score_scr, row_scr = rest[count + 2 :]
     slots, context = key_ref.shape[:2]
@@ -345,6 +357,7 @@
                 pltpu.SemaphoreType.DMA((5 + pieces,)),
             ],
             grant=12,
+            section=0,
             name="heads_0",
         )
 
@@ -354,6 +367,7 @@
             [((slots, head_cols + LANES), F32)] * mems,
             [x, attn_gain, perm, w_query[0], w_key[0], w_value[0]],
             scratch=[pltpu.VMEM((requests, head_cols + LANES), F32)],
+            section=int(tag[1:]),
             name="heads" + tag,
         )
 
@@ -372,7 +386,7 @@
                 window(cosine, heads[0]) if tag == "_0" else cosine,
                 sine,
                 heads[0],
-                *partners(heads, "mem"),
+                *partners(heads, "mem")[::-1],
                 key_cache[0],
                 value_cache[0],
             ],
@@ -382,6 +396,7 @@
                 pltpu.VMEM((slots, query_cols), F32),
             ],
             grant=3,
+            section=int(tag[1:]),
             name="attention" + tag,
         )
         projected = run(
@@ -389,12 +404,14 @@
             ((requests, local_width), BF16),
             [perm_back, w_out[0], attended, *partners([attended] * mems, "mem")],
             scratch=[pltpu.VMEM((requests, query_cols), F32)],
+            section=int(tag[1:]),
             name="project" + tag,
         )
         after, terms = run(
             functools.partial(hidden_terms_kernel, tps),
             [((requests, local_width), BF16), ((requests, term_cols), BF16)],
             [x, ffn_gain, w_gate[0], w_up[0], projected, *partners([projected] * tps, "tp")],
+            section=int(tag[1:]),
             name="terms" + tag,
         )
         down = run(
@@ -403,6 +420,7 @@
             [w_down[0], terms, *partners([terms] * mems, "mem")],
             scratch=[pltpu.VMEM((requests, units), BF16)],
             keep=[window(cosine, terms)] if tag == "_1" else (),
+            section=int(tag[1:]),
             name="down" + tag,
         )
         return after, [down, *partners([down] * tps, "tp")]

time: 101 us -> 93.1 us (0.922)
  the two profiles are of different devices: /device:TPU:0 before, /device:TPU:1 now
where the time goes in v3:
time: 93.1 us; the launch traced here: 92.9 us
  starting transfers between devices  52.6 us (56%)
  waiting for transfers between devices  25.8 us (28%)
  Pallas kernels  11.7 us (13%)
  local copies, waits for them, and re-layouts  1.73 us (2%)
    ppermute x30, starting transfers between devices, partners(): lax.ppermute(values[s], axis, [(i, i ^ s) for i in range(count)])  31.6 us
    ppermute x30, waiting for transfers between devices, partners(): lax.ppermute(values[s], axis, [(i, i ^ s) for i in range(count)])  25 us
    ppermute x1, starting transfers between devices, per_device(): lax.ppermute(first, 'section', [(i, (i + 1) % sections) for i in range(se...  21 us
    pallas_call x14, Pallas kernels, run(): pl.pallas_call(in_section, out_shape=[jax.ShapeDtypeStruct(shape, dtype)...  11.7 us
  transfers between devices with their start and end apart: 31, of which 25 were waited for; matrix products, arithmetic and copies ran while one was open for 1% of the time, Pallas kernels for 0%

profile of v3, /device:TPU:1, one launch (start us, length us, event | category | flops | bytes accessed | tf_op | source)
XLA Modules:
  0.0 92.9 jit_solution(18202776684592660266)
XLA Ops:
  0.1 3.0 %collective-permute-start = (f32[2,2688]{1,0:T(2,128)S(1)}, f32[2,2688]{1,0:T(2,128)S(1)}, u32[]{:S(2)}, u32[]{:S(2)}) collective-permute-start(f32[2,2688]{1,0:T(2,128)S(1)} %get-tuple-element.18), channel_id=1, source_target_pairs={{0,3},{1,2},{2,1},{3,0},{4,7},{5,6},{6,5},{7,4},{8,11},{9,10},{10,... | collective-permute-start | bytes 64520 | tf_op jit(solution)/shard_map/ppermute | solution.py:61
  4.4 1.5 %collective-permute-done.1.refs_5_ = f32[2,2688]{1,0:T(2,128)S(1)} collective-permute-done((f32[2,2688]{1,0:T(2,128)S(1)}, f32[2,2688]{1,0:T(2,128)S(1)}, u32[]{:S(2)}, u32[]{:S(2)}) %collective-permute-start.1) | collective-permute-done | bytes 21536 | tf_op jit(solution)/shard_map/ppermute | solution.py:61
  6.3 1.3 %copy-done.1 = bf16[1,2,4096,256]{3,2,1,0:T(8,128)(2,1)S(1)} copy-done((bf16[1,2,4096,256]{3,2,1,0:T(8,128)(2,1)S(1)}, bf16[1,2,4096,256]{3,2,1,0:T(8,128)(2,1)}, u32[]{:S(2)}) %copy-start.1) | copy-done | bytes 4194328
  7.7 2.4 %collective-permute-start.5 = (bf16[2,2048]{1,0:T(2,128)(2,1)S(1)}, bf16[2,2048]{1,0:T(2,128)(2,1)S(1)}, u32[]{:S(2)}, u32[]{:S(2)}) collective-permute-start(bf16[2,2048]{1,0:T(2,128)(2,1)S(1)} %attention_0.1.refs_2_), channel_id=1, source_target_pairs={{0,3},{1,2},{2,1},{3,0},{4,7},{5,6},{6,5},{7,4},{8,11},{9,10},{10,... | collective-permute-start | bytes 24584 | tf_op jit(solution)/shard_map/ppermute | solution.py:61
  10.4 0.8 collective-permute-done.5.refs_5_
  11.1 1.5 %collective-permute-done.4.refs_4_ = bf16[2,2048]{1,0:T(2,128)(2,1)S(1)} collective-permute-done((bf16[2,2048]{1,0:T(2,128)(2,1)S(1)}, bf16[2,2048]{1,0:T(2,128)(2,1)S(1)}, u32[]{:S(2)}, u32[]{:S(2)}) %collective-permute-start.4) | collective-permute-done | bytes 8224 | tf_op jit(solution)/shard_map/ppermute | solution.py:61
  12.9 3.4 %collective-permute-start.8 = (bf16[8,2048]{1,0:T(8,128)(2,1)S(1)}, bf16[8,2048]{1,0:T(8,128)(2,1)S(1)}, u32[]{:S(2)}, u32[]{:S(2)}) collective-permute-start(bf16[8,2048]{1,0:T(8,128)(2,1)S(1)} %project_0.1.refs_4_), channel_id=1, source_target_pairs={{0,12},{4,8},{8,4},{12,0},{1,13},{5,9},{9,5},{13,1},{2,14},{6,10},... | collective-permute-start | bytes 98312 | tf_op jit(solution)/shard_map/ppermute | solution.py:61
  16.3 0.4 collective-permute-start.6
  16.6 0.9 %collective-permute-done.8.refs_7_ = bf16[8,2048]{1,0:T(8,128)(2,1)S(1)} collective-permute-done((bf16[8,2048]{1,0:T(8,128)(2,1)S(1)}, bf16[8,2048]{1,0:T(8,128)(2,1)S(1)}, u32[]{:S(2)}, u32[]{:S(2)}) %collective-permute-start.8) | collective-permute-done | bytes 32800 | tf_op jit(solution)/shard_map/ppermute | solution.py:61
  17.6 2.4 %collective-permute-done.7.refs_6_ = bf16[8,2048]{1,0:T(8,128)(2,1)S(1)} collective-permute-done((bf16[8,2048]{1,0:T(8,128)(2,1)S(1)}, bf16[8,2048]{1,0:T(8,128)(2,1)S(1)}, u32[]{:S(2)}, u32[]{:S(2)}) %collective-permute-start.7) | collective-permute-done | bytes 32800 | tf_op jit(solution)/shard_map/ppermute | solution.py:61
  20.1 1.3 %collective-permute-start.11 = (bf16[8,7552]{1,0:T(8,128)(2,1)S(1)}, bf16[8,7552]{1,0:T(8,128)(2,1)S(1)}, u32[]{:S(2)}, u32[]{:S(2)}) collective-permute-start(bf16[8,7552]{1,0:T(8,128)(2,1)S(1)} %get-tuple-element.22.refs_1_), channel_id=1, source_target_pairs={{0,3},{1,2},{2,1},{3,0},{4,7},{5,6},{6,5},{7,4},{8,11},{9,10},{10,... | collective-permute-start | bytes 362504 | tf_op jit(solution)/shard_map/ppermute | solution.py:61
  21.6 1.2 %collective-permute-start.9 = (bf16[8,7552]{1,0:T(8,128)(2,1)S(1)}, bf16[8,7552]{1,0:T(8,128)(2,1)S(1)}, u32[]{:S(2)}, u32[]{:S(2)}) collective-permute-start(bf16[8,7552]{1,0:T(8,128)(2,1)S(1)} %get-tuple-element.22.refs_1_), channel_id=1, source_target_pairs={{0,1},{1,0},{2,3},{3,2},{4,5},{5,4},{6,7},{7,6},{8,9},{9,8},{10,11... | collective-permute-start | bytes 362504 | tf_op jit(solution)/shard_map/ppermute | solution.py:61
  22.8 2.1 %collective-permute-done.11.refs_4_ = bf16[8,7552]{1,0:T(8,128)(2,1)S(1)} collective-permute-done((bf16[8,7552]{1,0:T(8,128)(2,1)S(1)}, bf16[8,7552]{1,0:T(8,128)(2,1)S(1)}, u32[]{:S(2)}, u32[]{:S(2)}) %collective-permute-start.11) | collective-permute-done | bytes 120864 | tf_op jit(solution)/shard_map/ppermute | solution.py:61
  24.9 1.2 %collective-permute-done.10.refs_3_ = bf16[8,7552]{1,0:T(8,128)(2,1)S(1)} collective-permute-done((bf16[8,7552]{1,0:T(8,128)(2,1)S(1)}, bf16[8,7552]{1,0:T(8,128)(2,1)S(1)}, u32[]{:S(2)}, u32[]{:S(2)}) %collective-permute-start.10) | collective-permute-done | bytes 120864 | tf_op jit(solution)/shard_map/ppermute | solution.py:61
  26.4 2.1 %collective-permute-start.14 = (bf16[8,2048]{1,0:T(8,128)(2,1)S(1)}, bf16[8,2048]{1,0:T(8,128)(2,1)S(1)}, u32[]{:S(2)}, u32[]{:S(2)}) collective-permute-start(bf16[8,2048]{1,0:T(8,128)(2,1)S(1)} %down_0.1.refs_1_), channel_id=1, source_target_pairs={{0,12},{4,8},{8,4},{12,0},{1,13},{5,9},{9,5},{13,1},{2,14},{6,10},... | collective-permute-start | bytes 98312 | tf_op jit(solution)/shard_map/ppermute | solution.py:61
  28.5 1.5 %collective-permute-start.12 = (bf16[8,2048]{1,0:T(8,128)(2,1)S(1)}, bf16[8,2048]{1,0:T(8,128)(2,1)S(1)}, u32[]{:S(2)}, u32[]{:S(2)}) collective-permute-start(bf16[8,2048]{1,0:T(8,128)(2,1)S(1)} %down_0.1.refs_1_), channel_id=1, source_target_pairs={{0,4},{4,0},{8,12},{12,8},{1,5},{5,1},{9,13},{13,9},{2,6},{6,2},{1... | collective-permute-start | bytes 98312 | tf_op jit(solution)/shard_map/ppermute | solution.py:61
  30.0 1.1 %collective-permute-done.14.refs_4_ = bf16[8,2048]{1,0:T(8,128)(2,1)S(1)} collective-permute-done((bf16[8,2048]{1,0:T(8,128)(2,1)S(1)}, bf16[8,2048]{1,0:T(8,128)(2,1)S(1)}, u32[]{:S(2)}, u32[]{:S(2)}) %collective-permute-start.14) | collective-permute-done | bytes 32800 | tf_op jit(solution)/shard_map/ppermute | solution.py:61
  31.1 1.1 %collective-permute-done.13.refs_3_ = bf16[8,2048]{1,0:T(8,128)(2,1)S(1)} collective-permute-done((bf16[8,2048]{1,0:T(8,128)(2,1)S(1)}, bf16[8,2048]{1,0:T(8,128)(2,1)S(1)}, u32[]{:S(2)}, u32[]{:S(2)}) %collective-permute-start.13) | collective-permute-done | bytes 32800 | tf_op jit(solution)/shard_map/ppermute | solution.py:61
  32.2 21.0 %collective-permute-start.15 = (bf16[8,2048]{1,0:T(8,128)(2,1)S(1)}, bf16[8,2048]{1,0:T(8,128)(2,1)S(1)}, u32[]{:S(2)}, u32[]{:S(2)}) collective-permute-start(bf16[8,2048]{1,0:T(8,128)(2,1)S(1)} %finish.1.refs_1_), channel_id=1, source_target_pairs={{0,16},{16,0},{1,17},{17,1},{2,18},{18,2},{3,19},{19,3},{4,20},{20... | collective-permute-start | bytes 98312 | tf_op jit(solution)/shard_map/ppermute | solution.py:436
  53.2 0.9 collective-permute-done.15.refs_0_
  54.1 1.6 %heads_1.1 = (f32[2,2688]{1,0:T(2,128)S(1)}, f32[2,2688]{1,0:T(2,128)S(1)}, f32[2,2688]{1,0:T(2,128)S(1)}, f32[2,2688]{1,0:T(2,128)S(1)}) custom-call(bf16[8,2048]{1,0:T(8,128)(2,1)S(1)} %collective-permute-done.15.refs_0_, bf16[1,2048]{1,0:T(2,128)(2,1)S(1)} %copy-done.5, bf16[8,8]{1,0:T(8,128)(2,1)S(1)} %get-tuple-element.31.refs_2_, ...), custom_call_target="tpu_custom_call" | custom-call | flops 23000000512 | tf_op jit(solution)/shard_map/heads_1/pallas_call | solution.py:45
  55.7 1.9 %collective-permute-start.16 = (f32[2,2688]{1,0:T(2,128)S(1)}, f32[2,2688]{1,0:T(2,128)S(1)}, u32[]{:S(2)}, u32[]{:S(2)}) collective-permute-start(f32[2,2688]{1,0:T(2,128)S(1)} %get-tuple-element.24), channel_id=1, source_target_pairs={{0,3},{1,2},{2,1},{3,0},{4,7},{5,6},{6,5},{7,4},{8,11},{9,10},{10,... | collective-permute-start | bytes 64520 | tf_op jit(solution)/shard_map/ppermute | solution.py:61
  57.7 0.8 collective-permute-start.18
  58.5 0.9 collective-permute-done.16.refs_4_
  59.4 1.0 %collective-permute-done.17.refs_5_ = f32[2,2688]{1,0:T(2,128)S(1)} collective-permute-done((f32[2,2688]{1,0:T(2,128)S(1)}, f32[2,2688]{1,0:T(2,128)S(1)}, u32[]{:S(2)}, u32[]{:S(2)}) %collective-permute-start.17) | collective-permute-done | bytes 21536 | tf_op jit(solution)/shard_map/ppermute | solution.py:61
  60.3 2.0 %attention_1.1.refs_2_ = bf16[2,2048]{1,0:T(2,128)(2,1)S(1)} custom-call(s32[2,128]{1,0:T(2,128)S(1)} %broadcast_in_dim.47.refs_0_, f32[2,128]{1,0:T(2,128)S(1)} %get-tuple-element.34.refs_0_.refs_1_, f32[2,128]{1,0:T(2,128)S(1)} %get-tuple-element.35.refs_2_, f32[2,2688]{1,0:T(2,128)S(1)} %get-tuple-element.23.refs_3_, ...), custom_call_target="tpu_custom_call" | custom-call | flops 23000000512 | tf_op jit(solution)/shard_map/attention_1/pallas_call | solution.py:45
  62.3 1.2 %collective-permute-start.21 = (bf16[2,2048]{1,0:T(2,128)(2,1)S(1)}, bf16[2,2048]{1,0:T(2,128)(2,1)S(1)}, u32[]{:S(2)}, u32[]{:S(2)}) collective-permute-start(bf16[2,2048]{1,0:T(2,128)(2,1)S(1)} %attention_1.1.refs_2_), channel_id=1, source_target_pairs={{0,3},{1,2},{2,1},{3,0},{4,7},{5,6},{6,5},{7,4},{8,11},{9,10},{10,... | collective-permute-start | bytes 24584 | tf_op jit(solution)/shard_map/ppermute | solution.py:61
  63.5 0.9 collective-permute-start.20
  64.5 0.7 collective-permute-start.19
  65.2 0.6 collective-permute-done.21.refs_5_
  66.0 0.9 collective-permute-done.19.refs_3_
  67.0 1.3 %project_1.1.refs_4_ = bf16[8,2048]{1,0:T(8,128)(2,1)S(1)} custom-call(bf16[8,8]{1,0:T(8,128)(2,1)S(1)} %get-tuple-element.33.refs_0_, bf16[2048,2048]{1,0:T(8,128)(2,1)S(1)} %bitcast.33, bf16[2,2048]{1,0:T(2,128)(2,1)S(1)} %attention_1.1.refs_2_, bf16[2,2048]{1,0:T(2,128)(2,1)S(1)} %collective-permute-done.19.refs_3_, ...), custom_call_target="tpu_custom_call" | custom-call | flops 23000000512 | tf_op jit(solution)/shard_map/project_1/pallas_call | solution.py:45
  68.3 1.4 %collective-permute-start.24 = (bf16[8,2048]{1,0:T(8,128)(2,1)S(1)}, bf16[8,2048]{1,0:T(8,128)(2,1)S(1)}, u32[]{:S(2)}, u32[]{:S(2)}) collective-permute-start(bf16[8,2048]{1,0:T(8,128)(2,1)S(1)} %project_1.1.refs_4_), channel_id=1, source_target_pairs={{0,12},{4,8},{8,4},{12,0},{1,13},{5,9},{9,5},{13,1},{2,14},{6,10},... | collective-permute-start | bytes 98312 | tf_op jit(solution)/shard_map/ppermute | solution.py:61
  69.7 0.5 collective-permute-start.23
  70.2 1.6 %collective-permute-start.22 = (bf16[8,2048]{1,0:T(8,128)(2,1)S(1)}, bf16[8,2048]{1,0:T(8,128)(2,1)S(1)}, u32[]{:S(2)}, u32[]{:S(2)}) collective-permute-start(bf16[8,2048]{1,0:T(8,128)(2,1)S(1)} %project_1.1.refs_4_), channel_id=1, source_target_pairs={{0,4},{4,0},{8,12},{12,8},{1,5},{5,1},{9,13},{13,9},{2,6},{6,2},{1... | collective-permute-start | bytes 98312 | tf_op jit(solution)/shard_map/ppermute | solution.py:61
  71.8 1.3 %collective-permute-done.24.refs_7_ = bf16[8,2048]{1,0:T(8,128)(2,1)S(1)} collective-permute-done((bf16[8,2048]{1,0:T(8,128)(2,1)S(1)}, bf16[8,2048]{1,0:T(8,128)(2,1)S(1)}, u32[]{:S(2)}, u32[]{:S(2)}) %collective-permute-start.24) | collective-permute-done | bytes 32800 | tf_op jit(solution)/shard_map/ppermute | solution.py:61
  73.2 1.3 %collective-permute-done.23.refs_6_ = bf16[8,2048]{1,0:T(8,128)(2,1)S(1)} collective-permute-done((bf16[8,2048]{1,0:T(8,128)(2,1)S(1)}, bf16[8,2048]{1,0:T(8,128)(2,1)S(1)}, u32[]{:S(2)}, u32[]{:S(2)}) %collective-permute-start.23) | collective-permute-done | bytes 32800 | tf_op jit(solution)/shard_map/ppermute | solution.py:61
  74.5 3.9 %terms_1.1 = (bf16[8,2048]{1,0:T(8,128)(2,1)S(1)}, bf16[8,7552]{1,0:T(8,128)(2,1)S(1)}) custom-call(bf16[8,2048]{1,0:T(8,128)(2,1)S(1)} %collective-permute-done.15.refs_0_, bf16[1,2048]{1,0:T(2,128)(2,1)S(1)} %copy-done.6, bf16[2048,3584]{1,0:T(8,128)(2,1)S(1)} %bitcast.13, bf16[2048,3584]{1,0:T(8,128)(2,1)S(1)} %bitcast.17, ...), custom_call_target="tpu_custom_call" | custom-call | flops 23000000512 | tf_op jit(solution)/shard_map/terms_1/pallas_call | solution.py:45
  78.4 1.9 %collective-permute-start.27 = (bf16[8,7552]{1,0:T(8,128)(2,1)S(1)}, bf16[8,7552]{1,0:T(8,128)(2,1)S(1)}, u32[]{:S(2)}, u32[]{:S(2)}) collective-permute-start(bf16[8,7552]{1,0:T(8,128)(2,1)S(1)} %get-tuple-element.28.refs_1_), channel_id=1, source_target_pairs={{0,3},{1,2},{2,1},{3,0},{4,7},{5,6},{6,5},{7,4},{8,11},{9,10},{10,... | collective-permute-start | bytes 362504 | tf_op jit(solution)/shard_map/ppermute | solution.py:61
  80.5 0.7 collective-permute-start.25
  81.2 3.1 %collective-permute-done.27.refs_4_ = bf16[8,7552]{1,0:T(8,128)(2,1)S(1)} collective-permute-done((bf16[8,7552]{1,0:T(8,128)(2,1)S(1)}, bf16[8,7552]{1,0:T(8,128)(2,1)S(1)}, u32[]{:S(2)}, u32[]{:S(2)}) %collective-permute-start.27) | collective-permute-done | bytes 120864 | tf_op jit(solution)/shard_map/ppermute | solution.py:61
  84.2 0.7 collective-permute-done.26.refs_3_
  84.9 2.1 %down_1.1.refs_2_ = bf16[8,2048]{1,0:T(8,128)(2,1)S(1)} custom-call(bf16[3584,2048]{1,0:T(8,128)(2,1)S(1)} %bitcast.23, bf16[8,7552]{1,0:T(8,128)(2,1)S(1)} %get-tuple-element.28.refs_1_, bf16[8,7552]{1,0:T(8,128)(2,1)S(1)} %collective-permute-done.25.refs_2_, bf16[8,7552]{1,0:T(8,128)(2,1)S(1)} %collective-permute-done.26.refs_3_, ...), custom_call_target="tpu_custom_call" | custom-call | flops 23000000512 | tf_op jit(solution)/shard_map/down_1/pallas_call | solution.py:45
  87.0 1.5 %collective-permute-start.30 = (bf16[8,2048]{1,0:T(8,128)(2,1)S(1)}, bf16[8,2048]{1,0:T(8,128)(2,1)S(1)}, u32[]{:S(2)}, u32[]{:S(2)}) collective-permute-start(bf16[8,2048]{1,0:T(8,128)(2,1)S(1)} %down_1.1.refs_2_), channel_id=1, source_target_pairs={{0,12},{4,8},{8,4},{12,0},{1,13},{5,9},{9,5},{13,1},{2,14},{6,10},... | collective-permute-start | bytes 98312 | tf_op jit(solution)/shard_map/ppermute | solution.py:61
  88.7 1.9 %collective-permute-start.28 = (bf16[8,2048]{1,0:T(8,128)(2,1)S(1)}, bf16[8,2048]{1,0:T(8,128)(2,1)S(1)}, u32[]{:S(2)}, u32[]{:S(2)}) collective-permute-start(bf16[8,2048]{1,0:T(8,128)(2,1)S(1)} %down_1.1.refs_2_), channel_id=1, source_target_pairs={{0,4},{4,0},{8,12},{12,8},{1,5},{5,1},{9,13},{13,9},{2,6},{6,2},{1... | collective-permute-start | bytes 98312 | tf_op jit(solution)/shard_map/ppermute | solution.py:61
  90.6 1.0 %collective-permute-done.30.refs_5_ = bf16[8,2048]{1,0:T(8,128)(2,1)S(1)} collective-permute-done((bf16[8,2048]{1,0:T(8,128)(2,1)S(1)}, bf16[8,2048]{1,0:T(8,128)(2,1)S(1)}, u32[]{:S(2)}, u32[]{:S(2)}) %collective-permute-start.30) | collective-permute-done | bytes 32800 | tf_op jit(solution)/shard_map/ppermute | solution.py:61
  91.6 0.7 collective-permute-done.29.refs_4_
  92.3 0.6 choose.1
  (106 shorter events, 3.5 us)
Async XLA Ops:
  0.1 4.2 %collective-permute-start = (f32[2,2688]{1,0:T(2,128)S(1)}, f32[2,2688]{1,0:T(2,128)S(1)}, u32[]{:S(2)}, u32[]{:S(2)}) collective-permute-start(f32[2,2688]{1,0:T(2,128)S(1)} %get-tuple-element.18), channel_id=1, source_target_pairs={{0,3},{1,2},{2,1},{3,0},{4,7},{5,6},{6,5},{7,4},{8,11},{9,10},{10,... | collective-permute-start | bytes 64520 | tf_op jit(solution)/shard_map/ppermute | solution.py:61
  3.2 2.6 %collective-permute-start.1 = (f32[2,2688]{1,0:T(2,128)S(1)}, f32[2,2688]{1,0:T(2,128)S(1)}, u32[]{:S(2)}, u32[]{:S(2)}) collective-permute-start(f32[2,2688]{1,0:T(2,128)S(1)} %get-tuple-element.19), channel_id=1, source_target_pairs={{0,2},{1,3},{2,0},{3,1},{4,6},{5,7},{6,4},{7,5},{8,10},{9,11},{10,... | collective-permute-start | bytes 64520 | tf_op jit(solution)/shard_map/ppermute | solution.py:61
  3.4 2.6 %collective-permute-start.2 = (f32[2,2688]{1,0:T(2,128)S(1)}, f32[2,2688]{1,0:T(2,128)S(1)}, u32[]{:S(2)}, u32[]{:S(2)}) collective-permute-start(f32[2,2688]{1,0:T(2,128)S(1)} %get-tuple-element.20), channel_id=1, source_target_pairs={{0,1},{1,0},{2,3},{3,2},{4,5},{5,4},{6,7},{7,6},{8,9},{9,8},{10,11... | collective-permute-start | bytes 64520 | tf_op jit(solution)/shard_map/ppermute | solution.py:61
  4.2 8.6 %slice-start.18 = ((s8[8388608]{0:T(1024)(128)(4,1)}), s8[4194304]{0:T(1024)(128)(4,1)S(1)}, s32[]{:S(2)}) async-start(s8[8388608]{0:T(1024)(128)(4,1)} %bitcast.28), calls=%async_computation.18 | async-start | bytes 8388608
  7.6 12.3 %slice-start = ((s8[14680064]{0:T(1024)(128)(4,1)}), s8[4194304]{0:T(1024)(128)(4,1)S(1)}, s32[]{:S(2)}) async-start(s8[14680064]{0:T(1024)(128)(4,1)} %bitcast.10), calls=%async_computation | async-start | bytes 8388608
  7.6 12.3 %slice-start.1 = ((s8[14680064]{0:T(1024)(128)(4,1)}), s8[4194304]{0:T(1024)(128)(4,1)S(1)}, s32[]{:S(2)}) async-start(s8[14680064]{0:T(1024)(128)(4,1)} %bitcast.10), calls=%async_computation.1 | async-start | bytes 8388608
  7.6 12.3 %slice-start.4 = ((s8[14680064]{0:T(1024)(128)(4,1)}), s8[4194304]{0:T(1024)(128)(4,1)S(1)}, s32[]{:S(2)}) async-start(s8[14680064]{0:T(1024)(128)(4,1)} %bitcast.14), calls=%async_computation.4 | async-start | bytes 8388608
  7.6 12.3 %slice-start.5 = ((s8[14680064]{0:T(1024)(128)(4,1)}), s8[4194304]{0:T(1024)(128)(4,1)S(1)}, s32[]{:S(2)}) async-start(s8[14680064]{0:T(1024)(128)(4,1)} %bitcast.14), calls=%async_computation.5 | async-start | bytes 8388608
  7.7 3.5 %collective-permute-start.5 = (bf16[2,2048]{1,0:T(2,128)(2,1)S(1)}, bf16[2,2048]{1,0:T(2,128)(2,1)S(1)}, u32[]{:S(2)}, u32[]{:S(2)}) collective-permute-start(bf16[2,2048]{1,0:T(2,128)(2,1)S(1)} %attention_0.1.refs_2_), channel_id=1, source_target_pairs={{0,3},{1,2},{2,1},{3,0},{4,7},{5,6},{6,5},{7,4},{8,11},{9,10},{10,... | collective-permute-start | bytes 24584 | tf_op jit(solution)/shard_map/ppermute | solution.py:61
  10.0 2.6 %collective-permute-start.4 = (bf16[2,2048]{1,0:T(2,128)(2,1)S(1)}, bf16[2,2048]{1,0:T(2,128)(2,1)S(1)}, u32[]{:S(2)}, u32[]{:S(2)}) collective-permute-start(bf16[2,2048]{1,0:T(2,128)(2,1)S(1)} %attention_0.1.refs_2_), channel_id=1, source_target_pairs={{0,2},{1,3},{2,0},{3,1},{4,6},{5,7},{6,4},{7,5},{8,10},{9,11},{10,... | collective-permute-start | bytes 24584 | tf_op jit(solution)/shard_map/ppermute | solution.py:61
  10.2 2.5 %collective-permute-start.3 = (bf16[2,2048]{1,0:T(2,128)(2,1)S(1)}, bf16[2,2048]{1,0:T(2,128)(2,1)S(1)}, u32[]{:S(2)}, u32[]{:S(2)}) collective-permute-start(bf16[2,2048]{1,0:T(2,128)(2,1)S(1)} %attention_0.1.refs_2_), channel_id=1, source_target_pairs={{0,1},{1,0},{2,3},{3,2},{4,5},{5,4},{6,7},{7,6},{8,9},{9,8},{10,11... | collective-permute-start | bytes 24584 | tf_op jit(solution)/shard_map/ppermute | solution.py:61
  12.8 7.2 %slice-start.3 = ((s8[14680064]{0:T(1024)(128)(4,1)}), s8[2097152]{0:T(1024)(128)(4,1)S(1)}, s32[]{:S(2)}) async-start(s8[14680064]{0:T(1024)(128)(4,1)} %bitcast.10), calls=%async_computation.3 | async-start | bytes 4194304
  12.8 7.2 %slice-start.6 = ((s8[14680064]{0:T(1024)(128)(4,1)}), s8[4194304]{0:T(1024)(128)(4,1)S(1)}, s32[]{:S(2)}) async-start(s8[14680064]{0:T(1024)(128)(4,1)} %bitcast.14), calls=%async_computation.6 | async-start | bytes 8388608
  12.8 7.2 %slice-start.7 = ((s8[14680064]{0:T(1024)(128)(4,1)}), s8[2097152]{0:T(1024)(128)(4,1)S(1)}, s32[]{:S(2)}) async-start(s8[14680064]{0:T(1024)(128)(4,1)} %bitcast.14), calls=%async_computation.7 | async-start | bytes 4194304
  12.8 13.4 %slice-start.8 = ((s8[14680064]{0:T(1024)(128)(4,1)}), s8[2097152]{0:T(1024)(128)(4,1)S(1)}, s32[]{:S(2)}) async-start(s8[14680064]{0:T(1024)(128)(4,1)} %bitcast.18), calls=%async_computation.8 | async-start | bytes 4194304
  12.8 13.4 %slice-start.9 = ((s8[14680064]{0:T(1024)(128)(4,1)}), s8[4194304]{0:T(1024)(128)(4,1)S(1)}, s32[]{:S(2)}) async-start(s8[14680064]{0:T(1024)(128)(4,1)} %bitcast.18), calls=%async_computation.9 | async-start | bytes 8388608
  12.9 4.7 %collective-permute-start.8 = (bf16[8,2048]{1,0:T(8,128)(2,1)S(1)}, bf16[8,2048]{1,0:T(8,128)(2,1)S(1)}, u32[]{:S(2)}, u32[]{:S(2)}) collective-permute-start(bf16[8,2048]{1,0:T(8,128)(2,1)S(1)} %project_0.1.refs_4_), channel_id=1, source_target_pairs={{0,12},{4,8},{8,4},{12,0},{1,13},{5,9},{9,5},{13,1},{2,14},{6,10},... | collective-permute-start | bytes 98312 | tf_op jit(solution)/shard_map/ppermute | solution.py:61
  16.3 3.7 %collective-permute-start.7 = (bf16[8,2048]{1,0:T(8,128)(2,1)S(1)}, bf16[8,2048]{1,0:T(8,128)(2,1)S(1)}, u32[]{:S(2)}, u32[]{:S(2)}) collective-permute-start(bf16[8,2048]{1,0:T(8,128)(2,1)S(1)} %project_0.1.refs_4_), channel_id=1, source_target_pairs={{0,8},{4,12},{8,0},{12,4},{1,9},{5,13},{9,1},{13,5},{2,10},{6,14},... | collective-permute-start | bytes 98312 | tf_op jit(solution)/shard_map/ppermute | solution.py:61
  16.3 3.7 %collective-permute-start.6 = (bf16[8,2048]{1,0:T(8,128)(2,1)S(1)}, bf16[8,2048]{1,0:T(8,128)(2,1)S(1)}, u32[]{:S(2)}, u32[]{:S(2)}) collective-permute-start(bf16[8,2048]{1,0:T(8,128)(2,1)S(1)} %project_0.1.refs_4_), channel_id=1, source_target_pairs={{0,4},{4,0},{8,12},{12,8},{1,5},{5,1},{9,13},{13,9},{2,6},{6,2},{1... | collective-permute-start | bytes 98312 | tf_op jit(solution)/shard_map/ppermute | solution.py:61
  20.1 34.0 %slice-start.16 = ((s8[8388608]{0:T(1024)(128)(4,1)}), s8[4194304]{0:T(1024)(128)(4,1)S(1)}, s32[]{:S(2)}) async-start(s8[8388608]{0:T(1024)(128)(4,1)} %bitcast.25), calls=%async_computation.16 | async-start | bytes 8388608
  20.1 4.8 %collective-permute-start.11 = (bf16[8,7552]{1,0:T(8,128)(2,1)S(1)}, bf16[8,7552]{1,0:T(8,128)(2,1)S(1)}, u32[]{:S(2)}, u32[]{:S(2)}) collective-permute-start(bf16[8,7552]{1,0:T(8,128)(2,1)S(1)} %get-tuple-element.22.refs_1_), channel_id=1, source_target_pairs={{0,3},{1,2},{2,1},{3,0},{4,7},{5,6},{6,5},{7,4},{8,11},{9,10},{10,... | collective-permute-start | bytes 362504 | tf_op jit(solution)/shard_map/ppermute | solution.py:61
  21.4 4.7 %collective-permute-start.10 = (bf16[8,7552]{1,0:T(8,128)(2,1)S(1)}, bf16[8,7552]{1,0:T(8,128)(2,1)S(1)}, u32[]{:S(2)}, u32[]{:S(2)}) collective-permute-start(bf16[8,7552]{1,0:T(8,128)(2,1)S(1)} %get-tuple-element.22.refs_1_), channel_id=1, source_target_pairs={{0,2},{1,3},{2,0},{3,1},{4,6},{5,7},{6,4},{7,5},{8,10},{9,11},{10,... | collective-permute-start | bytes 362504 | tf_op jit(solution)/shard_map/ppermute | solution.py:61
  21.6 4.7 %collective-permute-start.9 = (bf16[8,7552]{1,0:T(8,128)(2,1)S(1)}, bf16[8,7552]{1,0:T(8,128)(2,1)S(1)}, u32[]{:S(2)}, u32[]{:S(2)}) collective-permute-start(bf16[8,7552]{1,0:T(8,128)(2,1)S(1)} %get-tuple-element.22.refs_1_), channel_id=1, source_target_pairs={{0,1},{1,0},{2,3},{3,2},{4,5},{5,4},{6,7},{7,6},{8,9},{9,8},{10,11... | collective-permute-start | bytes 362504 | tf_op jit(solution)/shard_map/ppermute | solution.py:61
  26.3 27.8 %slice-start.17 = ((s8[8388608]{0:T(1024)(128)(4,1)}), s8[4194304]{0:T(1024)(128)(4,1)S(1)}, s32[]{:S(2)}) async-start(s8[8388608]{0:T(1024)(128)(4,1)} %bitcast.25), calls=%async_computation.17 | async-start | bytes 8388608
  26.3 27.8 %copy-start.2 = (bf16[1,2048,256]{2,1,0:T(8,128)(2,1)S(1)}, bf16[1,2048,256]{2,1,0:T(8,128)(2,1)}, u32[]{:S(2)}) copy-start(bf16[1,2048,256]{2,1,0:T(8,128)(2,1)} %param.19) | copy-start | bytes 3145732
  26.3 27.8 %copy-start.3 = (bf16[1,2048,256]{2,1,0:T(8,128)(2,1)S(1)}, bf16[1,2048,256]{2,1,0:T(8,128)(2,1)}, u32[]{:S(2)}) copy-start(bf16[1,2048,256]{2,1,0:T(8,128)(2,1)} %param.20) | copy-start | bytes 3145732
  26.3 27.8 %copy-start.5 = (bf16[1,2048]{1,0:T(2,128)(2,1)S(1)}, bf16[1,2048]{1,0:T(2,128)(2,1)}, u32[]{:S(2)}) copy-start(bf16[1,2048]{1,0:T(2,128)(2,1)} %refs_1_.6) | copy-start | bytes 12292
  26.4 4.7 %collective-permute-start.14 = (bf16[8,2048]{1,0:T(8,128)(2,1)S(1)}, bf16[8,2048]{1,0:T(8,128)(2,1)S(1)}, u32[]{:S(2)}, u32[]{:S(2)}) collective-permute-start(bf16[8,2048]{1,0:T(8,128)(2,1)S(1)} %down_0.1.refs_1_), channel_id=1, source_target_pairs={{0,12},{4,8},{8,4},{12,0},{1,13},{5,9},{9,5},{13,1},{2,14},{6,10},... | collective-permute-start | bytes 98312 | tf_op jit(solution)/shard_map/ppermute | solution.py:61
  28.5 3.7 %collective-permute-start.13 = (bf16[8,2048]{1,0:T(8,128)(2,1)S(1)}, bf16[8,2048]{1,0:T(8,128)(2,1)S(1)}, u32[]{:S(2)}, u32[]{:S(2)}) collective-permute-start(bf16[8,2048]{1,0:T(8,128)(2,1)S(1)} %down_0.1.refs_1_), channel_id=1, source_target_pairs={{0,8},{4,12},{8,0},{12,4},{1,9},{5,13},{9,1},{13,5},{2,10},{6,14},... | collective-permute-start | bytes 98312 | tf_op jit(solution)/shard_map/ppermute | solution.py:61
  28.5 3.7 %collective-permute-start.12 = (bf16[8,2048]{1,0:T(8,128)(2,1)S(1)}, bf16[8,2048]{1,0:T(8,128)(2,1)S(1)}, u32[]{:S(2)}, u32[]{:S(2)}) collective-permute-start(bf16[8,2048]{1,0:T(8,128)(2,1)S(1)} %down_0.1.refs_1_), channel_id=1, source_target_pairs={{0,4},{4,0},{8,12},{12,8},{1,5},{5,1},{9,13},{13,9},{2,6},{6,2},{1... | collective-permute-start | bytes 98312 | tf_op jit(solution)/shard_map/ppermute | solution.py:61
  32.2 21.9 %collective-permute-start.15 = (bf16[8,2048]{1,0:T(8,128)(2,1)S(1)}, bf16[8,2048]{1,0:T(8,128)(2,1)S(1)}, u32[]{:S(2)}, u32[]{:S(2)}) collective-permute-start(bf16[8,2048]{1,0:T(8,128)(2,1)S(1)} %finish.1.refs_1_), channel_id=1, source_target_pairs={{0,16},{16,0},{1,17},{17,1},{2,18},{18,2},{3,19},{19,3},{4,20},{20... | collective-permute-start | bytes 98312 | tf_op jit(solution)/shard_map/ppermute | solution.py:436
  54.1 12.8 %slice-start.20 = ((s8[8388608]{0:T(1024)(128)(4,1)}), s8[4194304]{0:T(1024)(128)(4,1)S(1)}, s32[]{:S(2)}) async-start(s8[8388608]{0:T(1024)(128)(4,1)} %bitcast.31), calls=%async_computation.20 | async-start | bytes 8388608
  55.7 3.6 %collective-permute-start.16 = (f32[2,2688]{1,0:T(2,128)S(1)}, f32[2,2688]{1,0:T(2,128)S(1)}, u32[]{:S(2)}, u32[]{:S(2)}) collective-permute-start(f32[2,2688]{1,0:T(2,128)S(1)} %get-tuple-element.24), channel_id=1, source_target_pairs={{0,3},{1,2},{2,1},{3,0},{4,7},{5,6},{6,5},{7,4},{8,11},{9,10},{10,... | collective-permute-start | bytes 64520 | tf_op jit(solution)/shard_map/ppermute | solution.py:61
  57.7 9.3 %slice-start.21 = ((s8[8388608]{0:T(1024)(128)(4,1)}), s8[4194304]{0:T(1024)(128)(4,1)S(1)}, s32[]{:S(2)}) async-start(s8[8388608]{0:T(1024)(128)(4,1)} %bitcast.31), calls=%async_computation.21 | async-start | bytes 8388608
  57.7 2.6 %collective-permute-start.17 = (f32[2,2688]{1,0:T(2,128)S(1)}, f32[2,2688]{1,0:T(2,128)S(1)}, u32[]{:S(2)}, u32[]{:S(2)}) collective-permute-start(f32[2,2688]{1,0:T(2,128)S(1)} %get-tuple-element.25), channel_id=1, source_target_pairs={{0,2},{1,3},{2,0},{3,1},{4,6},{5,7},{6,4},{7,5},{8,10},{9,11},{10,... | collective-permute-start | bytes 64520 | tf_op jit(solution)/shard_map/ppermute | solution.py:61
  57.7 2.6 %collective-permute-start.18 = (f32[2,2688]{1,0:T(2,128)S(1)}, f32[2,2688]{1,0:T(2,128)S(1)}, u32[]{:S(2)}, u32[]{:S(2)}) collective-permute-start(f32[2,2688]{1,0:T(2,128)S(1)} %get-tuple-element.26), channel_id=1, source_target_pairs={{0,1},{1,0},{2,3},{3,2},{4,5},{5,4},{6,7},{7,6},{8,9},{9,8},{10,11... | collective-permute-start | bytes 64520 | tf_op jit(solution)/shard_map/ppermute | solution.py:61
  62.3 3.5 %collective-permute-start.21 = (bf16[2,2048]{1,0:T(2,128)(2,1)S(1)}, bf16[2,2048]{1,0:T(2,128)(2,1)S(1)}, u32[]{:S(2)}, u32[]{:S(2)}) collective-permute-start(bf16[2,2048]{1,0:T(2,128)(2,1)S(1)} %attention_1.1.refs_2_), channel_id=1, source_target_pairs={{0,3},{1,2},{2,1},{3,0},{4,7},{5,6},{6,5},{7,4},{8,11},{9,10},{10,... | collective-permute-start | bytes 24584 | tf_op jit(solution)/shard_map/ppermute | solution.py:61
  63.5 2.5 %collective-permute-start.20 = (bf16[2,2048]{1,0:T(2,128)(2,1)S(1)}, bf16[2,2048]{1,0:T(2,128)(2,1)S(1)}, u32[]{:S(2)}, u32[]{:S(2)}) collective-permute-start(bf16[2,2048]{1,0:T(2,128)(2,1)S(1)} %attention_1.1.refs_2_), channel_id=1, source_target_pairs={{0,2},{1,3},{2,0},{3,1},{4,6},{5,7},{6,4},{7,5},{8,10},{9,11},{10,... | collective-permute-start | bytes 24584 | tf_op jit(solution)/shard_map/ppermute | solution.py:61
  64.5 2.5 %collective-permute-start.19 = (bf16[2,2048]{1,0:T(2,128)(2,1)S(1)}, bf16[2,2048]{1,0:T(2,128)(2,1)S(1)}, u32[]{:S(2)}, u32[]{:S(2)}) collective-permute-start(bf16[2,2048]{1,0:T(2,128)(2,1)S(1)} %attention_1.1.refs_2_), channel_id=1, source_target_pairs={{0,1},{1,0},{2,3},{3,2},{4,5},{5,4},{6,7},{7,6},{8,9},{9,8},{10,11... | collective-permute-start | bytes 24584 | tf_op jit(solution)/shard_map/ppermute | solution.py:61
  68.3 4.9 %collective-permute-start.24 = (bf16[8,2048]{1,0:T(8,128)(2,1)S(1)}, bf16[8,2048]{1,0:T(8,128)(2,1)S(1)}, u32[]{:S(2)}, u32[]{:S(2)}) collective-permute-start(bf16[8,2048]{1,0:T(8,128)(2,1)S(1)} %project_1.1.refs_4_), channel_id=1, source_target_pairs={{0,12},{4,8},{8,4},{12,0},{1,13},{5,9},{9,5},{13,1},{2,14},{6,10},... | collective-permute-start | bytes 98312 | tf_op jit(solution)/shard_map/ppermute | solution.py:61
  69.7 4.8 %collective-permute-start.23 = (bf16[8,2048]{1,0:T(8,128)(2,1)S(1)}, bf16[8,2048]{1,0:T(8,128)(2,1)S(1)}, u32[]{:S(2)}, u32[]{:S(2)}) collective-permute-start(bf16[8,2048]{1,0:T(8,128)(2,1)S(1)} %project_1.1.refs_4_), channel_id=1, source_target_pairs={{0,8},{4,12},{8,0},{12,4},{1,9},{5,13},{9,1},{13,5},{2,10},{6,14},... | collective-permute-start | bytes 98312 | tf_op jit(solution)/shard_map/ppermute | solution.py:61
  70.2 4.3 %collective-permute-start.22 = (bf16[8,2048]{1,0:T(8,128)(2,1)S(1)}, bf16[8,2048]{1,0:T(8,128)(2,1)S(1)}, u32[]{:S(2)}, u32[]{:S(2)}) collective-permute-start(bf16[8,2048]{1,0:T(8,128)(2,1)S(1)} %project_1.1.refs_4_), channel_id=1, source_target_pairs={{0,4},{4,0},{8,12},{12,8},{1,5},{5,1},{9,13},{13,9},{2,6},{6,2},{1... | collective-permute-start | bytes 98312 | tf_op jit(solution)/shard_map/ppermute | solution.py:61
  78.4 5.8 %collective-permute-start.27 = (bf16[8,7552]{1,0:T(8,128)(2,1)S(1)}, bf16[8,7552]{1,0:T(8,128)(2,1)S(1)}, u32[]{:S(2)}, u32[]{:S(2)}) collective-permute-start(bf16[8,7552]{1,0:T(8,128)(2,1)S(1)} %get-tuple-element.28.refs_1_), channel_id=1, source_target_pairs={{0,3},{1,2},{2,1},{3,0},{4,7},{5,6},{6,5},{7,4},{8,11},{9,10},{10,... | collective-permute-start | bytes 362504 | tf_op jit(solution)/shard_map/ppermute | solution.py:61
  80.4 4.5 %collective-permute-start.26 = (bf16[8,7552]{1,0:T(8,128)(2,1)S(1)}, bf16[8,7552]{1,0:T(8,128)(2,1)S(1)}, u32[]{:S(2)}, u32[]{:S(2)}) collective-permute-start(bf16[8,7552]{1,0:T(8,128)(2,1)S(1)} %get-tuple-element.28.refs_1_), channel_id=1, source_target_pairs={{0,2},{1,3},{2,0},{3,1},{4,6},{5,7},{6,4},{7,5},{8,10},{9,11},{10,... | collective-permute-start | bytes 362504 | tf_op jit(solution)/shard_map/ppermute | solution.py:61
  80.5 4.4 %collective-permute-start.25 = (bf16[8,7552]{1,0:T(8,128)(2,1)S(1)}, bf16[8,7552]{1,0:T(8,128)(2,1)S(1)}, u32[]{:S(2)}, u32[]{:S(2)}) collective-permute-start(bf16[8,7552]{1,0:T(8,128)(2,1)S(1)} %get-tuple-element.28.refs_1_), channel_id=1, source_target_pairs={{0,1},{1,0},{2,3},{3,2},{4,5},{5,4},{6,7},{7,6},{8,9},{9,8},{10,11... | collective-permute-start | bytes 362504 | tf_op jit(solution)/shard_map/ppermute | solution.py:61
  87.0 4.6 %collective-permute-start.30 = (bf16[8,2048]{1,0:T(8,128)(2,1)S(1)}, bf16[8,2048]{1,0:T(8,128)(2,1)S(1)}, u32[]{:S(2)}, u32[]{:S(2)}) collective-permute-start(bf16[8,2048]{1,0:T(8,128)(2,1)S(1)} %down_1.1.refs_2_), channel_id=1, source_target_pairs={{0,12},{4,8},{8,4},{12,0},{1,13},{5,9},{9,5},{13,1},{2,14},{6,10},... | collective-permute-start | bytes 98312 | tf_op jit(solution)/shard_map/ppermute | solution.py:61
  88.5 3.7 %collective-permute-start.29 = (bf16[8,2048]{1,0:T(8,128)(2,1)S(1)}, bf16[8,2048]{1,0:T(8,128)(2,1)S(1)}, u32[]{:S(2)}, u32[]{:S(2)}) collective-permute-start(bf16[8,2048]{1,0:T(8,128)(2,1)S(1)} %down_1.1.refs_2_), channel_id=1, source_target_pairs={{0,8},{4,12},{8,0},{12,4},{1,9},{5,13},{9,1},{13,5},{2,10},{6,14},... | collective-permute-start | bytes 98312 | tf_op jit(solution)/shard_map/ppermute | solution.py:61
  88.7 3.6 %collective-permute-start.28 = (bf16[8,2048]{1,0:T(8,128)(2,1)S(1)}, bf16[8,2048]{1,0:T(8,128)(2,1)S(1)}, u32[]{:S(2)}, u32[]{:S(2)}) collective-permute-start(bf16[8,2048]{1,0:T(8,128)(2,1)S(1)} %down_1.1.refs_2_), channel_id=1, source_target_pairs={{0,4},{4,0},{8,12},{12,8},{1,5},{5,1},{9,13},{13,9},{2,6},{6,2},{1... | collective-permute-start | bytes 98312 | tf_op jit(solution)/shard_map/ppermute | solution.py:61
  (14 other events, 79.8 us)

commit v4 on v3

--- a/solution.py
+++ b/solution.py
@@ -55,11 +55,38 @@
     return result[0] if single else result
 
 
-def partners(values, axis):
-    count = lax.axis_size(axis)
+def partners(values, axis, active):
+    axes = ("section", "tp", "mem")
+    sections, tps, mems = (lax.axis_size(name) for name in axes)
+
+    def pairs(s):
+        for section in range(sections):
+            for tp in range(tps):
+                for mem in range(mems):
+                    if section == active:
+                        there = (tp ^ s, mem) if axis == "tp" else (tp, mem ^ s)
+                    else:
+                        there = (tp, mem ^ 1) if axis == "tp" else (tp ^ 1, mem)
+                    yield (
+                        (section * tps + tp) * mems + mem,
+                        (section * tps + there[0]) * mems + there[1],
+                    )
+
     return [
-        lax.ppermute(values[s], axis, [(i, i ^ s) for i in range(count)]) for s in range(1, count)
+        lax.ppermute(values[s], axes, list(pairs(s))) for s in range(1, lax.axis_size(axis))
     ]
+
+
+def across(value, s=0):
+    axes = ("section", "tp", "mem")
+    sections, tps, mems = (lax.axis_size(name) for name in axes)
+    pairs = [
+        ((section * tps + tp) * mems + mem, ((section ^ 1) * tps + (tp ^ s)) * mems + mem)
+        for section in range(sections)
+        for tp in range(tps)
+        for mem in range(mems)
+    ]
+    return lax.ppermute(value, axes, pairs)
 
 
 def tree_sum(pieces):
@@ -81,9 +108,10 @@
     return tree_sum([ref[rows, cols].astype(F32) for ref in refs])
 
 
-def heads_kernel(count, x_ref, gain_ref, perm_ref, wq_ref, wk_ref, wv_ref, *rest):
-    out_refs, sums = rest[:count], rest[count]
-    slots = x_ref.shape[0] // count
+def heads_kernel(count, pieces, after_ref, gain_ref, perm_ref, wq_ref, wk_ref, wv_ref, *rest):
+    out_refs, x_ref, sums = rest[pieces : pieces + count], *rest[pieces + count :]
+    slots = after_ref.shape[0] // count
+    x_ref[...] = (after_ref[...].astype(F32) + total_of(rest[:pieces])).astype(BF16)
     x = jnp.dot(perm_ref[...], x_ref[...], preferred_element_type=F32)
     scaled = (x * gain_ref[...].astype(F32)).astype(BF16)
     squares = jnp.sum(x * x, axis=1, keepdims=True)
@@ -279,12 +307,6 @@
     matmul_into(out_ref, 0, hidden_scr[...], w_ref, 512)
 
 
-def finish_kernel(count, x_ref, *rest):
-    pieces = rest[:count]
-    out_ref = rest[count]
-    out_ref[...] = (x_ref[...].astype(F32) + total_of(pieces)).astype(BF16)
-
-
 def choose_kernel(count, x_ref, first_ref, *rest):
     pieces = rest[:count]
     out_ref = rest[count]
@@ -361,15 +383,16 @@
             name="heads_0",
         )
 
-    def heads_of(x, tag):
-        return run(
-            functools.partial(heads_kernel, mems),
-            [((slots, head_cols + LANES), F32)] * mems,
-            [x, attn_gain, perm, w_query[0], w_key[0], w_value[0]],
+    def second_heads(after, downs):
+        *heads, x = run(
+            functools.partial(heads_kernel, mems, len(downs)),
+            [((slots, head_cols + LANES), F32)] * mems + [((requests, local_width), BF16)],
+            [after, attn_gain, perm, w_query[0], w_key[0], w_value[0], *downs],
             scratch=[pltpu.VMEM((requests, head_cols + LANES), F32)],
-            section=int(tag[1:]),
-            name="heads" + tag,
-        )
+            section=1,
+            name="heads_1",
+        )
+        return x, heads
 
     def window(value, after):
         def kernel(value_ref, after_ref, out_ref):
@@ -386,7 +409,7 @@
                 window(cosine, heads[0]) if tag == "_0" else cosine,
                 sine,
                 heads[0],
-                *partners(heads, "mem")[::-1],
+                *partners(heads, "mem", int(tag[1:]))[::-1],
                 key_cache[0],
                 value_cache[0],
             ],
@@ -402,7 +425,7 @@
         projected = run(
             functools.partial(project_kernel, mems),
             ((requests, local_width), BF16),
-            [perm_back, w_out[0], attended, *partners([attended] * mems, "mem")],
+            [perm_back, w_out[0], attended, *partners([attended] * mems, "mem", int(tag[1:]))],
             scratch=[pltpu.VMEM((requests, query_cols), F32)],
             section=int(tag[1:]),
             name="project" + tag,
@@ -410,35 +433,30 @@
         after, terms = run(
             functools.partial(hidden_terms_kernel, tps),
             [((requests, local_width), BF16), ((requests, term_cols), BF16)],
-            [x, ffn_gain, w_gate[0], w_up[0], projected, *partners([projected] * tps, "tp")],
+            [x, ffn_gain, w_gate[0], w_up[0], projected, *partners([projected] * tps, "tp", int(tag[1:]))],
             section=int(tag[1:]),
             name="terms" + tag,
         )
         down = run(
             functools.partial(down_kernel, mems, width),
             ((requests, local_width), BF16),
-            [w_down[0], terms, *partners([terms] * mems, "mem")],
+            [w_down[0], terms, *partners([terms] * mems, "mem", int(tag[1:]))],
             scratch=[pltpu.VMEM((requests, units), BF16)],
             keep=[window(cosine, terms)] if tag == "_1" else (),
             section=int(tag[1:]),
             name="down" + tag,
         )
-        return after, [down, *partners([down] * tps, "tp")]
-
-    after, downs = layer(hidden_in, first_heads(), "_0")
-    first = run(
-        functools.partial(finish_kernel, tps),
-        ((requests, local_width), BF16),
-        [after, *downs],
-        name="finish",
-    )
-    sections = lax.axis_size("section")
-    passed = lax.ppermute(first, "section", [(i, (i + 1) % sections) for i in range(sections)])
-    after, downs = layer(passed, heads_of(passed, "_1"), "_1")
+        return after, down
+
+    after, down = layer(hidden_in, first_heads(), "_0")
+    downs = [across(down, s) for s in range(tps)]
+    passed, heads = second_heads(across(after), downs)
+    first = across(passed)
+    after, down = layer(passed, heads, "_1")
     result = run(
         functools.partial(choose_kernel, tps),
         ((requests, local_width), BF16),
-        [after, first, *downs],
+        [after, first, down, *partners([down] * tps, "tp", 1)],
         name="choose",
     )
     return result[None]

time: 93.1 us -> 89.6 us (0.962)
  waiting for transfers between devices: 25.8 us -> 18.2 us
  local copies, waits for them, and re-layouts: 1.73 us -> 5.11 us
    ppermute x31 -> x33, waiting for transfers between devices: 25.8 us -> 18.2 us  [the longest x27 16.3 us: partners(): lax.ppermute(values[s], axes, list(pairs(s)))]
    unnamed x62, local copies, waits for them, and re-layouts: 1.66 us -> 5.04 us
    ppermute x31 -> x33, starting transfers between devices: 52.6 us -> 53.5 us  [the longest x6 28.8 us: across(): return lax.ppermute(value, axes, pairs)]
    pallas_call x14 -> x13, Pallas kernels: 11.7 us -> 11.7 us  [run(): pl.pallas_call(in_section, out_shape=[jax.ShapeDtypeStruct(shape, dtype)...]
  transfers between devices with their start and end apart: 31 -> 33, of which waited for: 25 -> 22; matrix products, arithmetic and copies ran while one was open for 1% -> 1% of each run, Pallas kernels for 0% -> 7%
where the time goes in v4:
time: 89.6 us; the launch traced here: 89.5 us
  starting transfers between devices  53.5 us (60%)
  waiting for transfers between devices  18.2 us (20%)
  Pallas kernels  11.7 us (13%)
  local copies, waits for them, and re-layouts  5.11 us (6%)
    ppermute x6, starting transfers between devices, across(): return lax.ppermute(value, axes, pairs)  28.8 us
    ppermute x27, starting transfers between devices, partners(): lax.ppermute(values[s], axes, list(pairs(s)))  24.7 us
    ppermute x27, waiting for transfers between devices, partners(): lax.ppermute(values[s], axes, list(pairs(s)))  16.3 us
    pallas_call x13, Pallas kernels, run(): pl.pallas_call(in_section, out_shape=[jax.ShapeDtypeStruct(shape, dtype)...  11.7 us
    unnamed x62, local copies, waits for them, and re-layouts  5.04 us
    ppermute x6, waiting for transfers between devices, across(): return lax.ppermute(value, axes, pairs)  1.93 us
  transfers between devices with their start and end apart: 33, of which 22 were waited for; matrix products, arithmetic and copies ran while one was open for 1% of the time, Pallas kernels for 7%

profile of v4, /device:TPU:1, one launch (start us, length us, event | category | flops | bytes accessed | tf_op | source)
XLA Modules:
  0.0 89.5 jit_solution(112700998170461991)
XLA Ops:
  0.1 2.2 %collective-permute-start = (f32[2,2688]{1,0:T(2,128)S(1)}, f32[2,2688]{1,0:T(2,128)S(1)}, u32[]{:S(2)}, u32[]{:S(2)}) collective-permute-start(f32[2,2688]{1,0:T(2,128)S(1)} %get-tuple-element.19), channel_id=1, source_target_pairs={{0,3},{1,2},{2,1},{3,0},{4,7},{5,6},{6,5},{7,4},{8,11},{9,10},{10,... | collective-permute-start | bytes 64520 | tf_op jit(solution)/shard_map/ppermute | solution.py:76
  2.4 1.4 %collective-permute-start.2 = (f32[2,2688]{1,0:T(2,128)S(1)}, f32[2,2688]{1,0:T(2,128)S(1)}, u32[]{:S(2)}, u32[]{:S(2)}) collective-permute-start(f32[2,2688]{1,0:T(2,128)S(1)} %get-tuple-element.21), channel_id=1, source_target_pairs={{0,1},{1,0},{2,3},{3,2},{4,5},{5,4},{6,7},{7,6},{8,9},{9,8},{10,11... | collective-permute-start | bytes 64520 | tf_op jit(solution)/shard_map/ppermute | solution.py:76
  4.4 0.5 collective-permute-done.1.refs_5_
  5.3 1.3 %copy-done = bf16[1,2,4096,256]{3,2,1,0:T(8,128)(2,1)S(1)} copy-done((bf16[1,2,4096,256]{3,2,1,0:T(8,128)(2,1)S(1)}, bf16[1,2,4096,256]{3,2,1,0:T(8,128)(2,1)}, u32[]{:S(2)}) %copy-start) | copy-done | bytes 4194328
  6.6 1.3 %copy-done.1 = bf16[1,2,4096,256]{3,2,1,0:T(8,128)(2,1)S(1)} copy-done((bf16[1,2,4096,256]{3,2,1,0:T(8,128)(2,1)S(1)}, bf16[1,2,4096,256]{3,2,1,0:T(8,128)(2,1)}, u32[]{:S(2)}) %copy-start.1) | copy-done | bytes 4194328
  8.0 1.4 %collective-permute-start.4 = (bf16[2,2048]{1,0:T(2,128)(2,1)S(1)}, bf16[2,2048]{1,0:T(2,128)(2,1)S(1)}, u32[]{:S(2)}, u32[]{:S(2)}) collective-permute-start(bf16[2,2048]{1,0:T(2,128)(2,1)S(1)} %attention_0.1.refs_2_), channel_id=1, source_target_pairs={{0,2},{1,3},{2,0},{3,1},{4,6},{5,7},{6,4},{7,5},{8,10},{9,11},{10,... | collective-permute-start | bytes 24584 | tf_op jit(solution)/shard_map/ppermute | solution.py:76
  9.5 1.0 %collective-permute-done.5.refs_5_ = bf16[2,2048]{1,0:T(2,128)(2,1)S(1)} collective-permute-done((bf16[2,2048]{1,0:T(2,128)(2,1)S(1)}, bf16[2,2048]{1,0:T(2,128)(2,1)S(1)}, u32[]{:S(2)}, u32[]{:S(2)}) %collective-permute-start.5) | collective-permute-done | bytes 8224 | tf_op jit(solution)/shard_map/ppermute | solution.py:76
  10.6 1.5 %collective-permute-done.3.refs_3_ = bf16[2,2048]{1,0:T(2,128)(2,1)S(1)} collective-permute-done((bf16[2,2048]{1,0:T(2,128)(2,1)S(1)}, bf16[2,2048]{1,0:T(2,128)(2,1)S(1)}, u32[]{:S(2)}, u32[]{:S(2)}) %collective-permute-start.3) | collective-permute-done | bytes 8224 | tf_op jit(solution)/shard_map/ppermute | solution.py:76
  12.2 1.1 %collective-permute-start.8 = (bf16[8,2048]{1,0:T(8,128)(2,1)S(1)}, bf16[8,2048]{1,0:T(8,128)(2,1)S(1)}, u32[]{:S(2)}, u32[]{:S(2)}) collective-permute-start(bf16[8,2048]{1,0:T(8,128)(2,1)S(1)} %project_0.1.refs_4_), channel_id=1, source_target_pairs={{0,12},{1,13},{2,14},{3,15},{4,8},{5,9},{6,10},{7,11},{8,4},{9,5},... | collective-permute-start | bytes 98312 | tf_op jit(solution)/shard_map/ppermute | solution.py:76
  13.3 0.4 collective-permute-start.7
  13.7 1.1 %collective-permute-start.6 = (bf16[8,2048]{1,0:T(8,128)(2,1)S(1)}, bf16[8,2048]{1,0:T(8,128)(2,1)S(1)}, u32[]{:S(2)}, u32[]{:S(2)}) collective-permute-start(bf16[8,2048]{1,0:T(8,128)(2,1)S(1)} %project_0.1.refs_4_), channel_id=1, source_target_pairs={{0,4},{1,5},{2,6},{3,7},{4,0},{5,1},{6,2},{7,3},{8,12},{9,13},{10,... | collective-permute-start | bytes 98312 | tf_op jit(solution)/shard_map/ppermute | solution.py:76
  15.0 1.1 %collective-permute-done.7.refs_6_ = bf16[8,2048]{1,0:T(8,128)(2,1)S(1)} collective-permute-done((bf16[8,2048]{1,0:T(8,128)(2,1)S(1)}, bf16[8,2048]{1,0:T(8,128)(2,1)S(1)}, u32[]{:S(2)}, u32[]{:S(2)}) %collective-permute-start.7) | collective-permute-done | bytes 32800 | tf_op jit(solution)/shard_map/ppermute | solution.py:76
  16.5 0.5 slice-done.3
  17.0 1.2 %slice-done.6 = s8[4194304]{0:T(1024)(128)(4,1)S(1)} async-done(((s8[14680064]{0:T(1024)(128)(4,1)}), s8[4194304]{0:T(1024)(128)(4,1)S(1)}, s32[]{:S(2)}) %slice-start.6) | async-done | bytes 4194328
  18.2 0.6 slice-done.7
  19.1 1.4 %collective-permute-start.11 = (bf16[8,7552]{1,0:T(8,128)(2,1)S(1)}, bf16[8,7552]{1,0:T(8,128)(2,1)S(1)}, u32[]{:S(2)}, u32[]{:S(2)}) collective-permute-start(bf16[8,7552]{1,0:T(8,128)(2,1)S(1)} %get-tuple-element.23.refs_1_), channel_id=1, source_target_pairs={{0,2},{1,3},{2,0},{3,1},{4,6},{5,7},{6,4},{7,5},{8,10},{9,11},{10,... | collective-permute-start | bytes 362504 | tf_op jit(solution)/shard_map/ppermute | solution.py:76
  20.5 19.3 %collective-permute-start.9 = (bf16[8,2048]{1,0:T(8,128)(2,1)S(1)}, bf16[8,2048]{1,0:T(8,128)(2,1)S(1)}, u32[]{:S(2)}, u32[]{:S(2)}) collective-permute-start(bf16[8,2048]{1,0:T(8,128)(2,1)S(1)} %get-tuple-element.22), channel_id=1, source_target_pairs={{0,16},{1,17},{2,18},{3,19},{4,20},{5,21},{6,22},{7,23},{8,24},{9,... | collective-permute-start | bytes 98312 | tf_op jit(solution)/shard_map/ppermute | solution.py:89
  40.0 6.8 %collective-permute-start.16 = (bf16[8,2048]{1,0:T(8,128)(2,1)S(1)}, bf16[8,2048]{1,0:T(8,128)(2,1)S(1)}, u32[]{:S(2)}, u32[]{:S(2)}) collective-permute-start(bf16[8,2048]{1,0:T(8,128)(2,1)S(1)} %down_0.1), channel_id=1, source_target_pairs={{0,28},{1,29},{2,30},{3,31},{4,24},{5,25},{6,26},{7,27},{8,20},{9,... | collective-permute-start | bytes 98312 | tf_op jit(solution)/shard_map/ppermute | solution.py:89
  46.8 0.6 collective-permute-start.15
  47.4 2.1 %collective-permute-start.14 = (bf16[8,2048]{1,0:T(8,128)(2,1)S(1)}, bf16[8,2048]{1,0:T(8,128)(2,1)S(1)}, u32[]{:S(2)}, u32[]{:S(2)}) collective-permute-start(bf16[8,2048]{1,0:T(8,128)(2,1)S(1)} %down_0.1), channel_id=1, source_target_pairs={{0,20},{1,21},{2,22},{3,23},{4,16},{5,17},{6,18},{7,19},{8,28},{9,... | collective-permute-start | bytes 98312 | tf_op jit(solution)/shard_map/ppermute | solution.py:89
  49.4 1.6 %collective-permute-done.15.refs_8_ = bf16[8,2048]{1,0:T(8,128)(2,1)S(1)} collective-permute-done((bf16[8,2048]{1,0:T(8,128)(2,1)S(1)}, bf16[8,2048]{1,0:T(8,128)(2,1)S(1)}, u32[]{:S(2)}, u32[]{:S(2)}) %collective-permute-start.15) | collective-permute-done | bytes 32800 | tf_op jit(solution)/shard_map/ppermute | solution.py:89
  51.4 1.6 %heads_1.1 = (f32[2,2688]{1,0:T(2,128)S(1)}, f32[2,2688]{1,0:T(2,128)S(1)}, f32[2,2688]{1,0:T(2,128)S(1)}, f32[2,2688]{1,0:T(2,128)S(1)}, bf16[8,2048]{1,0:T(8,128)(2,1)S(1)}) custom-call(bf16[8,2048]{1,0:T(8,128)(2,1)S(1)} %collective-permute-done.9.refs_0_, bf16[1,2048]{1,0:T(2,128)(2,1)S(1)} %copy-done.5, bf16[8,8]{1,0:T(8,128)(2,1)S(1)} %get-tuple-element.33.refs_2_, ...), custom_call_target="tpu_custom_call" | custom-call | flops 23000000512 | tf_op jit(solution)/shard_map/heads_1/pallas_call | solution.py:45
  53.0 1.9 %collective-permute-start.17 = (f32[2,2688]{1,0:T(2,128)S(1)}, f32[2,2688]{1,0:T(2,128)S(1)}, u32[]{:S(2)}, u32[]{:S(2)}) collective-permute-start(f32[2,2688]{1,0:T(2,128)S(1)} %get-tuple-element.26), channel_id=1, source_target_pairs={{0,4},{1,5},{2,6},{3,7},{4,0},{5,1},{6,2},{7,3},{8,12},{9,13},{10,... | collective-permute-start | bytes 64520 | tf_op jit(solution)/shard_map/ppermute | solution.py:76
  55.2 0.6 collective-permute-start.19
  55.7 0.9 collective-permute-done.17.refs_4_
  56.6 1.0 %collective-permute-done.18.refs_5_ = f32[2,2688]{1,0:T(2,128)S(1)} collective-permute-done((f32[2,2688]{1,0:T(2,128)S(1)}, f32[2,2688]{1,0:T(2,128)S(1)}, u32[]{:S(2)}, u32[]{:S(2)}) %collective-permute-start.18) | collective-permute-done | bytes 21536 | tf_op jit(solution)/shard_map/ppermute | solution.py:76
  57.8 2.0 %attention_1.1.refs_2_ = bf16[2,2048]{1,0:T(2,128)(2,1)S(1)} custom-call(s32[2,128]{1,0:T(2,128)S(1)} %broadcast_in_dim.47.refs_0_, f32[2,128]{1,0:T(2,128)S(1)} %get-tuple-element.36.refs_0_.refs_1_, f32[2,128]{1,0:T(2,128)S(1)} %get-tuple-element.37.refs_2_, f32[2,2688]{1,0:T(2,128)S(1)} %get-tuple-element.25.refs_3_, ...), custom_call_target="tpu_custom_call" | custom-call | flops 23000000512 | tf_op jit(solution)/shard_map/attention_1/pallas_call | solution.py:45
  59.8 1.3 %collective-permute-start.22 = (bf16[2,2048]{1,0:T(2,128)(2,1)S(1)}, bf16[2,2048]{1,0:T(2,128)(2,1)S(1)}, u32[]{:S(2)}, u32[]{:S(2)}) collective-permute-start(bf16[2,2048]{1,0:T(2,128)(2,1)S(1)} %attention_1.1.refs_2_), channel_id=1, source_target_pairs={{0,4},{1,5},{2,6},{3,7},{4,0},{5,1},{6,2},{7,3},{8,12},{9,13},{10,... | collective-permute-start | bytes 24584 | tf_op jit(solution)/shard_map/ppermute | solution.py:76
  61.1 0.5 collective-permute-start.21
  61.6 0.9 %collective-permute-start.20 = (bf16[2,2048]{1,0:T(2,128)(2,1)S(1)}, bf16[2,2048]{1,0:T(2,128)(2,1)S(1)}, u32[]{:S(2)}, u32[]{:S(2)}) collective-permute-start(bf16[2,2048]{1,0:T(2,128)(2,1)S(1)} %attention_1.1.refs_2_), channel_id=1, source_target_pairs={{0,4},{1,5},{2,6},{3,7},{4,0},{5,1},{6,2},{7,3},{8,12},{9,13},{10,... | collective-permute-start | bytes 24584 | tf_op jit(solution)/shard_map/ppermute | solution.py:76
  62.5 0.8 collective-permute-done.22.refs_5_
  63.6 0.5 collective-permute-done.20.refs_3_
  64.1 1.3 %project_1.1.refs_4_ = bf16[8,2048]{1,0:T(8,128)(2,1)S(1)} custom-call(bf16[8,8]{1,0:T(8,128)(2,1)S(1)} %get-tuple-element.35.refs_0_, bf16[2048,2048]{1,0:T(8,128)(2,1)S(1)} %bitcast.33, bf16[2,2048]{1,0:T(2,128)(2,1)S(1)} %attention_1.1.refs_2_, bf16[2,2048]{1,0:T(2,128)(2,1)S(1)} %collective-permute-done.20.refs_3_, ...), custom_call_target="tpu_custom_call" | custom-call | flops 23000000512 | tf_op jit(solution)/shard_map/project_1/pallas_call | solution.py:45
  65.4 2.0 %collective-permute-start.25 = (bf16[8,2048]{1,0:T(8,128)(2,1)S(1)}, bf16[8,2048]{1,0:T(8,128)(2,1)S(1)}, u32[]{:S(2)}, u32[]{:S(2)}) collective-permute-start(bf16[8,2048]{1,0:T(8,128)(2,1)S(1)} %project_1.1.refs_4_), channel_id=1, source_target_pairs={{0,1},{1,0},{2,3},{3,2},{4,5},{5,4},{6,7},{7,6},{8,9},{9,8},{10,11... | collective-permute-start | bytes 98312 | tf_op jit(solution)/shard_map/ppermute | solution.py:76
  67.4 1.5 %collective-permute-start.23 = (bf16[8,2048]{1,0:T(8,128)(2,1)S(1)}, bf16[8,2048]{1,0:T(8,128)(2,1)S(1)}, u32[]{:S(2)}, u32[]{:S(2)}) collective-permute-start(bf16[8,2048]{1,0:T(8,128)(2,1)S(1)} %project_1.1.refs_4_), channel_id=1, source_target_pairs={{0,1},{1,0},{2,3},{3,2},{4,5},{5,4},{6,7},{7,6},{8,9},{9,8},{10,11... | collective-permute-start | bytes 98312 | tf_op jit(solution)/shard_map/ppermute | solution.py:76
  69.0 1.0 %collective-permute-done.25.refs_7_ = bf16[8,2048]{1,0:T(8,128)(2,1)S(1)} collective-permute-done((bf16[8,2048]{1,0:T(8,128)(2,1)S(1)}, bf16[8,2048]{1,0:T(8,128)(2,1)S(1)}, u32[]{:S(2)}, u32[]{:S(2)}) %collective-permute-start.25) | collective-permute-done | bytes 32800 | tf_op jit(solution)/shard_map/ppermute | solution.py:76
  70.0 1.1 %collective-permute-done.24.refs_6_ = bf16[8,2048]{1,0:T(8,128)(2,1)S(1)} collective-permute-done((bf16[8,2048]{1,0:T(8,128)(2,1)S(1)}, bf16[8,2048]{1,0:T(8,128)(2,1)S(1)}, u32[]{:S(2)}, u32[]{:S(2)}) %collective-permute-start.24) | collective-permute-done | bytes 32800 | tf_op jit(solution)/shard_map/ppermute | solution.py:76
  71.0 3.9 %terms_1.1 = (bf16[8,2048]{1,0:T(8,128)(2,1)S(1)}, bf16[8,7552]{1,0:T(8,128)(2,1)S(1)}) custom-call(bf16[8,2048]{1,0:T(8,128)(2,1)S(1)} %get-tuple-element.24.refs_0_, bf16[1,2048]{1,0:T(2,128)(2,1)S(1)} %copy-done.6, bf16[2048,3584]{1,0:T(8,128)(2,1)S(1)} %bitcast.13, bf16[2048,3584]{1,0:T(8,128)(2,1)S(1)} %bitcast.17, ...), custom_call_target="tpu_custom_call" | custom-call | flops 23000000512 | tf_op jit(solution)/shard_map/terms_1/pallas_call | solution.py:45
  75.0 1.8 %collective-permute-start.29 = (bf16[8,7552]{1,0:T(8,128)(2,1)S(1)}, bf16[8,7552]{1,0:T(8,128)(2,1)S(1)}, u32[]{:S(2)}, u32[]{:S(2)}) collective-permute-start(bf16[8,7552]{1,0:T(8,128)(2,1)S(1)} %get-tuple-element.30.refs_1_), channel_id=1, source_target_pairs={{0,4},{1,5},{2,6},{3,7},{4,0},{5,1},{6,2},{7,3},{8,12},{9,13},{10,... | collective-permute-start | bytes 362504 | tf_op jit(solution)/shard_map/ppermute | solution.py:76
  77.0 0.7 collective-permute-start.27
  77.7 2.0 %collective-permute-done.29.refs_4_ = bf16[8,7552]{1,0:T(8,128)(2,1)S(1)} collective-permute-done((bf16[8,7552]{1,0:T(8,128)(2,1)S(1)}, bf16[8,7552]{1,0:T(8,128)(2,1)S(1)}, u32[]{:S(2)}, u32[]{:S(2)}) %collective-permute-start.29) | collective-permute-done | bytes 120864 | tf_op jit(solution)/shard_map/ppermute | solution.py:76
  79.7 1.4 %collective-permute-done.28.refs_3_ = bf16[8,7552]{1,0:T(8,128)(2,1)S(1)} collective-permute-done((bf16[8,7552]{1,0:T(8,128)(2,1)S(1)}, bf16[8,7552]{1,0:T(8,128)(2,1)S(1)}, u32[]{:S(2)}, u32[]{:S(2)}) %collective-permute-start.28) | collective-permute-done | bytes 120864 | tf_op jit(solution)/shard_map/ppermute | solution.py:76
  81.2 2.1 %down_1.1.refs_2_ = bf16[8,2048]{1,0:T(8,128)(2,1)S(1)} custom-call(bf16[3584,2048]{1,0:T(8,128)(2,1)S(1)} %bitcast.23, bf16[8,7552]{1,0:T(8,128)(2,1)S(1)} %get-tuple-element.30.refs_1_, bf16[8,7552]{1,0:T(8,128)(2,1)S(1)} %collective-permute-done.27.refs_2_, bf16[8,7552]{1,0:T(8,128)(2,1)S(1)} %collective-permute-done.28.refs_3_, ...), custom_call_target="tpu_custom_call" | custom-call | flops 23000000512 | tf_op jit(solution)/shard_map/down_1/pallas_call | solution.py:45
  83.2 1.9 %collective-permute-start.32 = (bf16[8,2048]{1,0:T(8,128)(2,1)S(1)}, bf16[8,2048]{1,0:T(8,128)(2,1)S(1)}, u32[]{:S(2)}, u32[]{:S(2)}) collective-permute-start(bf16[8,2048]{1,0:T(8,128)(2,1)S(1)} %down_1.1.refs_2_), channel_id=1, source_target_pairs={{0,1},{1,0},{2,3},{3,2},{4,5},{5,4},{6,7},{7,6},{8,9},{9,8},{10,11... | collective-permute-start | bytes 98312 | tf_op jit(solution)/shard_map/ppermute | solution.py:76
  85.4 1.4 %collective-permute-start.30 = (bf16[8,2048]{1,0:T(8,128)(2,1)S(1)}, bf16[8,2048]{1,0:T(8,128)(2,1)S(1)}, u32[]{:S(2)}, u32[]{:S(2)}) collective-permute-start(bf16[8,2048]{1,0:T(8,128)(2,1)S(1)} %down_1.1.refs_2_), channel_id=1, source_target_pairs={{0,1},{1,0},{2,3},{3,2},{4,5},{5,4},{6,7},{7,6},{8,9},{9,8},{10,11... | collective-permute-start | bytes 98312 | tf_op jit(solution)/shard_map/ppermute | solution.py:76
  86.8 1.0 %collective-permute-done.32.refs_5_ = bf16[8,2048]{1,0:T(8,128)(2,1)S(1)} collective-permute-done((bf16[8,2048]{1,0:T(8,128)(2,1)S(1)}, bf16[8,2048]{1,0:T(8,128)(2,1)S(1)}, u32[]{:S(2)}, u32[]{:S(2)}) %collective-permute-start.32) | collective-permute-done | bytes 32800 | tf_op jit(solution)/shard_map/ppermute | solution.py:76
  87.8 1.0 %collective-permute-done.31.refs_4_ = bf16[8,2048]{1,0:T(8,128)(2,1)S(1)} collective-permute-done((bf16[8,2048]{1,0:T(8,128)(2,1)S(1)}, bf16[8,2048]{1,0:T(8,128)(2,1)S(1)}, u32[]{:S(2)}, u32[]{:S(2)}) %collective-permute-start.31) | collective-permute-done | bytes 32800 | tf_op jit(solution)/shard_map/ppermute | solution.py:76
  88.8 0.6 choose.1
  (109 shorter events, 4.2 us)
Async XLA Ops:
  0.1 4.3 %collective-permute-start = (f32[2,2688]{1,0:T(2,128)S(1)}, f32[2,2688]{1,0:T(2,128)S(1)}, u32[]{:S(2)}, u32[]{:S(2)}) collective-permute-start(f32[2,2688]{1,0:T(2,128)S(1)} %get-tuple-element.19), channel_id=1, source_target_pairs={{0,3},{1,2},{2,1},{3,0},{4,7},{5,6},{6,5},{7,4},{8,11},{9,10},{10,... | collective-permute-start | bytes 64520 | tf_op jit(solution)/shard_map/ppermute | solution.py:76
  2.3 2.6 %collective-permute-start.1 = (f32[2,2688]{1,0:T(2,128)S(1)}, f32[2,2688]{1,0:T(2,128)S(1)}, u32[]{:S(2)}, u32[]{:S(2)}) collective-permute-start(f32[2,2688]{1,0:T(2,128)S(1)} %get-tuple-element.20), channel_id=1, source_target_pairs={{0,2},{1,3},{2,0},{3,1},{4,6},{5,7},{6,4},{7,5},{8,10},{9,11},{10,... | collective-permute-start | bytes 64520 | tf_op jit(solution)/shard_map/ppermute | solution.py:76
  2.4 2.8 %collective-permute-start.2 = (f32[2,2688]{1,0:T(2,128)S(1)}, f32[2,2688]{1,0:T(2,128)S(1)}, u32[]{:S(2)}, u32[]{:S(2)}) collective-permute-start(f32[2,2688]{1,0:T(2,128)S(1)} %get-tuple-element.21), channel_id=1, source_target_pairs={{0,1},{1,0},{2,3},{3,2},{4,5},{5,4},{6,7},{7,6},{8,9},{9,8},{10,11... | collective-permute-start | bytes 64520 | tf_op jit(solution)/shard_map/ppermute | solution.py:76
  7.9 8.7 %slice-start = ((s8[14680064]{0:T(1024)(128)(4,1)}), s8[4194304]{0:T(1024)(128)(4,1)S(1)}, s32[]{:S(2)}) async-start(s8[14680064]{0:T(1024)(128)(4,1)} %bitcast.10), calls=%async_computation | async-start | bytes 8388608
  7.9 8.7 %slice-start.1 = ((s8[14680064]{0:T(1024)(128)(4,1)}), s8[4194304]{0:T(1024)(128)(4,1)S(1)}, s32[]{:S(2)}) async-start(s8[14680064]{0:T(1024)(128)(4,1)} %bitcast.10), calls=%async_computation.1 | async-start | bytes 8388608
  7.9 8.7 %slice-start.4 = ((s8[14680064]{0:T(1024)(128)(4,1)}), s8[4194304]{0:T(1024)(128)(4,1)S(1)}, s32[]{:S(2)}) async-start(s8[14680064]{0:T(1024)(128)(4,1)} %bitcast.14), calls=%async_computation.4 | async-start | bytes 8388608
  7.9 8.7 %slice-start.5 = ((s8[14680064]{0:T(1024)(128)(4,1)}), s8[4194304]{0:T(1024)(128)(4,1)S(1)}, s32[]{:S(2)}) async-start(s8[14680064]{0:T(1024)(128)(4,1)} %bitcast.14), calls=%async_computation.5 | async-start | bytes 8388608
  7.9 2.6 %collective-permute-start.5 = (bf16[2,2048]{1,0:T(2,128)(2,1)S(1)}, bf16[2,2048]{1,0:T(2,128)(2,1)S(1)}, u32[]{:S(2)}, u32[]{:S(2)}) collective-permute-start(bf16[2,2048]{1,0:T(2,128)(2,1)S(1)} %attention_0.1.refs_2_), channel_id=1, source_target_pairs={{0,3},{1,2},{2,1},{3,0},{4,7},{5,6},{6,5},{7,4},{8,11},{9,10},{10,... | collective-permute-start | bytes 24584 | tf_op jit(solution)/shard_map/ppermute | solution.py:76
  8.0 2.5 %collective-permute-start.4 = (bf16[2,2048]{1,0:T(2,128)(2,1)S(1)}, bf16[2,2048]{1,0:T(2,128)(2,1)S(1)}, u32[]{:S(2)}, u32[]{:S(2)}) collective-permute-start(bf16[2,2048]{1,0:T(2,128)(2,1)S(1)} %attention_0.1.refs_2_), channel_id=1, source_target_pairs={{0,2},{1,3},{2,0},{3,1},{4,6},{5,7},{6,4},{7,5},{8,10},{9,11},{10,... | collective-permute-start | bytes 24584 | tf_op jit(solution)/shard_map/ppermute | solution.py:76
  9.4 2.7 %collective-permute-start.3 = (bf16[2,2048]{1,0:T(2,128)(2,1)S(1)}, bf16[2,2048]{1,0:T(2,128)(2,1)S(1)}, u32[]{:S(2)}, u32[]{:S(2)}) collective-permute-start(bf16[2,2048]{1,0:T(2,128)(2,1)S(1)} %attention_0.1.refs_2_), channel_id=1, source_target_pairs={{0,1},{1,0},{2,3},{3,2},{4,5},{5,4},{6,7},{7,6},{8,9},{9,8},{10,11... | collective-permute-start | bytes 24584 | tf_op jit(solution)/shard_map/ppermute | solution.py:76
  12.2 27.7 %slice-start.8 = ((s8[14680064]{0:T(1024)(128)(4,1)}), s8[2097152]{0:T(1024)(128)(4,1)S(1)}, s32[]{:S(2)}) async-start(s8[14680064]{0:T(1024)(128)(4,1)} %bitcast.18), calls=%async_computation.8 | async-start | bytes 4194304
  12.2 27.7 %slice-start.9 = ((s8[14680064]{0:T(1024)(128)(4,1)}), s8[4194304]{0:T(1024)(128)(4,1)S(1)}, s32[]{:S(2)}) async-start(s8[14680064]{0:T(1024)(128)(4,1)} %bitcast.18), calls=%async_computation.9 | async-start | bytes 8388608
  12.2 2.8 %collective-permute-start.8 = (bf16[8,2048]{1,0:T(8,128)(2,1)S(1)}, bf16[8,2048]{1,0:T(8,128)(2,1)S(1)}, u32[]{:S(2)}, u32[]{:S(2)}) collective-permute-start(bf16[8,2048]{1,0:T(8,128)(2,1)S(1)} %project_0.1.refs_4_), channel_id=1, source_target_pairs={{0,12},{1,13},{2,14},{3,15},{4,8},{5,9},{6,10},{7,11},{8,4},{9,5},... | collective-permute-start | bytes 98312 | tf_op jit(solution)/shard_map/ppermute | solution.py:76
  13.3 2.8 %collective-permute-start.7 = (bf16[8,2048]{1,0:T(8,128)(2,1)S(1)}, bf16[8,2048]{1,0:T(8,128)(2,1)S(1)}, u32[]{:S(2)}, u32[]{:S(2)}) collective-permute-start(bf16[8,2048]{1,0:T(8,128)(2,1)S(1)} %project_0.1.refs_4_), channel_id=1, source_target_pairs={{0,8},{1,9},{2,10},{3,11},{4,12},{5,13},{6,14},{7,15},{8,0},{9,1},... | collective-permute-start | bytes 98312 | tf_op jit(solution)/shard_map/ppermute | solution.py:76
  13.7 2.8 %collective-permute-start.6 = (bf16[8,2048]{1,0:T(8,128)(2,1)S(1)}, bf16[8,2048]{1,0:T(8,128)(2,1)S(1)}, u32[]{:S(2)}, u32[]{:S(2)}) collective-permute-start(bf16[8,2048]{1,0:T(8,128)(2,1)S(1)} %project_0.1.refs_4_), channel_id=1, source_target_pairs={{0,4},{1,5},{2,6},{3,7},{4,0},{5,1},{6,2},{7,3},{8,12},{9,13},{10,... | collective-permute-start | bytes 98312 | tf_op jit(solution)/shard_map/ppermute | solution.py:76
  18.8 21.1 %slice-start.10 = ((s8[14680064]{0:T(1024)(128)(4,1)}), s8[4194304]{0:T(1024)(128)(4,1)S(1)}, s32[]{:S(2)}) async-start(s8[14680064]{0:T(1024)(128)(4,1)} %bitcast.18), calls=%async_computation.10 | async-start | bytes 8388608
  18.8 21.1 %slice-start.11 = ((s8[14680064]{0:T(1024)(128)(4,1)}), s8[4194304]{0:T(1024)(128)(4,1)S(1)}, s32[]{:S(2)}) async-start(s8[14680064]{0:T(1024)(128)(4,1)} %bitcast.18), calls=%async_computation.11 | async-start | bytes 8388608
  18.9 32.5 %slice-start.16 = ((s8[8388608]{0:T(1024)(128)(4,1)}), s8[4194304]{0:T(1024)(128)(4,1)S(1)}, s32[]{:S(2)}) async-start(s8[8388608]{0:T(1024)(128)(4,1)} %bitcast.25), calls=%async_computation.16 | async-start | bytes 8388608
  18.9 32.4 %slice-start.17 = ((s8[8388608]{0:T(1024)(128)(4,1)}), s8[4194304]{0:T(1024)(128)(4,1)S(1)}, s32[]{:S(2)}) async-start(s8[8388608]{0:T(1024)(128)(4,1)} %bitcast.25), calls=%async_computation.17 | async-start | bytes 8388608
  18.9 21.0 %collective-permute-start.12 = (bf16[8,7552]{1,0:T(8,128)(2,1)S(1)}, bf16[8,7552]{1,0:T(8,128)(2,1)S(1)}, u32[]{:S(2)}, u32[]{:S(2)}) collective-permute-start(bf16[8,7552]{1,0:T(8,128)(2,1)S(1)} %get-tuple-element.23.refs_1_), channel_id=1, source_target_pairs={{0,3},{1,2},{2,1},{3,0},{4,7},{5,6},{6,5},{7,4},{8,11},{9,10},{10,... | collective-permute-start | bytes 362504 | tf_op jit(solution)/shard_map/ppermute | solution.py:76
  19.1 20.8 %collective-permute-start.11 = (bf16[8,7552]{1,0:T(8,128)(2,1)S(1)}, bf16[8,7552]{1,0:T(8,128)(2,1)S(1)}, u32[]{:S(2)}, u32[]{:S(2)}) collective-permute-start(bf16[8,7552]{1,0:T(8,128)(2,1)S(1)} %get-tuple-element.23.refs_1_), channel_id=1, source_target_pairs={{0,2},{1,3},{2,0},{3,1},{4,6},{5,7},{6,4},{7,5},{8,10},{9,11},{10,... | collective-permute-start | bytes 362504 | tf_op jit(solution)/shard_map/ppermute | solution.py:76
  20.5 19.4 %collective-permute-start.10 = (bf16[8,7552]{1,0:T(8,128)(2,1)S(1)}, bf16[8,7552]{1,0:T(8,128)(2,1)S(1)}, u32[]{:S(2)}, u32[]{:S(2)}) collective-permute-start(bf16[8,7552]{1,0:T(8,128)(2,1)S(1)} %get-tuple-element.23.refs_1_), channel_id=1, source_target_pairs={{0,1},{1,0},{2,3},{3,2},{4,5},{5,4},{6,7},{7,6},{8,9},{9,8},{10,11... | collective-permute-start | bytes 362504 | tf_op jit(solution)/shard_map/ppermute | solution.py:76
  20.5 28.9 %collective-permute-start.9 = (bf16[8,2048]{1,0:T(8,128)(2,1)S(1)}, bf16[8,2048]{1,0:T(8,128)(2,1)S(1)}, u32[]{:S(2)}, u32[]{:S(2)}) collective-permute-start(bf16[8,2048]{1,0:T(8,128)(2,1)S(1)} %get-tuple-element.22), channel_id=1, source_target_pairs={{0,16},{1,17},{2,18},{3,19},{4,20},{5,21},{6,22},{7,23},{8,24},{9,... | collective-permute-start | bytes 98312 | tf_op jit(solution)/shard_map/ppermute | solution.py:89
  39.9 11.4 %copy-start.2 = (bf16[1,2048,256]{2,1,0:T(8,128)(2,1)S(1)}, bf16[1,2048,256]{2,1,0:T(8,128)(2,1)}, u32[]{:S(2)}) copy-start(bf16[1,2048,256]{2,1,0:T(8,128)(2,1)} %param.19) | copy-start | bytes 3145732
  39.9 11.4 %copy-start.3 = (bf16[1,2048,256]{2,1,0:T(8,128)(2,1)S(1)}, bf16[1,2048,256]{2,1,0:T(8,128)(2,1)}, u32[]{:S(2)}) copy-start(bf16[1,2048,256]{2,1,0:T(8,128)(2,1)} %param.20) | copy-start | bytes 3145732
  40.0 11.4 %copy-start.5 = (bf16[1,2048]{1,0:T(2,128)(2,1)S(1)}, bf16[1,2048]{1,0:T(2,128)(2,1)}, u32[]{:S(2)}) copy-start(bf16[1,2048]{1,0:T(2,128)(2,1)} %refs_1_.6) | copy-start | bytes 12292
  40.0 9.4 %collective-permute-start.16 = (bf16[8,2048]{1,0:T(8,128)(2,1)S(1)}, bf16[8,2048]{1,0:T(8,128)(2,1)S(1)}, u32[]{:S(2)}, u32[]{:S(2)}) collective-permute-start(bf16[8,2048]{1,0:T(8,128)(2,1)S(1)} %down_0.1), channel_id=1, source_target_pairs={{0,28},{1,29},{2,30},{3,31},{4,24},{5,25},{6,26},{7,27},{8,20},{9,... | collective-permute-start | bytes 98312 | tf_op jit(solution)/shard_map/ppermute | solution.py:89
  46.8 4.3 %collective-permute-start.15 = (bf16[8,2048]{1,0:T(8,128)(2,1)S(1)}, bf16[8,2048]{1,0:T(8,128)(2,1)S(1)}, u32[]{:S(2)}, u32[]{:S(2)}) collective-permute-start(bf16[8,2048]{1,0:T(8,128)(2,1)S(1)} %down_0.1), channel_id=1, source_target_pairs={{0,24},{1,25},{2,26},{3,27},{4,28},{5,29},{6,30},{7,31},{8,16},{9,... | collective-permute-start | bytes 98312 | tf_op jit(solution)/shard_map/ppermute | solution.py:89
  47.4 4.0 %collective-permute-start.14 = (bf16[8,2048]{1,0:T(8,128)(2,1)S(1)}, bf16[8,2048]{1,0:T(8,128)(2,1)S(1)}, u32[]{:S(2)}, u32[]{:S(2)}) collective-permute-start(bf16[8,2048]{1,0:T(8,128)(2,1)S(1)} %down_0.1), channel_id=1, source_target_pairs={{0,20},{1,21},{2,22},{3,23},{4,16},{5,17},{6,18},{7,19},{8,28},{9,... | collective-permute-start | bytes 98312 | tf_op jit(solution)/shard_map/ppermute | solution.py:89
  49.4 1.9 %collective-permute-start.13 = (bf16[8,2048]{1,0:T(8,128)(2,1)S(1)}, bf16[8,2048]{1,0:T(8,128)(2,1)S(1)}, u32[]{:S(2)}, u32[]{:S(2)}) collective-permute-start(bf16[8,2048]{1,0:T(8,128)(2,1)S(1)} %down_0.1), channel_id=1, source_target_pairs={{0,16},{1,17},{2,18},{3,19},{4,20},{5,21},{6,22},{7,23},{8,24},{9,... | collective-permute-start | bytes 98312 | tf_op jit(solution)/shard_map/ppermute | solution.py:89
  51.4 12.7 %slice-start.20 = ((s8[8388608]{0:T(1024)(128)(4,1)}), s8[4194304]{0:T(1024)(128)(4,1)S(1)}, s32[]{:S(2)}) async-start(s8[8388608]{0:T(1024)(128)(4,1)} %bitcast.31), calls=%async_computation.20 | async-start | bytes 8388608
  53.0 3.6 %collective-permute-start.17 = (f32[2,2688]{1,0:T(2,128)S(1)}, f32[2,2688]{1,0:T(2,128)S(1)}, u32[]{:S(2)}, u32[]{:S(2)}) collective-permute-start(f32[2,2688]{1,0:T(2,128)S(1)} %get-tuple-element.26), channel_id=1, source_target_pairs={{0,4},{1,5},{2,6},{3,7},{4,0},{5,1},{6,2},{7,3},{8,12},{9,13},{10,... | collective-permute-start | bytes 64520 | tf_op jit(solution)/shard_map/ppermute | solution.py:76
  54.9 9.1 %slice-start.21 = ((s8[8388608]{0:T(1024)(128)(4,1)}), s8[4194304]{0:T(1024)(128)(4,1)S(1)}, s32[]{:S(2)}) async-start(s8[8388608]{0:T(1024)(128)(4,1)} %bitcast.31), calls=%async_computation.21 | async-start | bytes 8388608
  54.9 2.6 %collective-permute-start.18 = (f32[2,2688]{1,0:T(2,128)S(1)}, f32[2,2688]{1,0:T(2,128)S(1)}, u32[]{:S(2)}, u32[]{:S(2)}) collective-permute-start(f32[2,2688]{1,0:T(2,128)S(1)} %get-tuple-element.27), channel_id=1, source_target_pairs={{0,4},{1,5},{2,6},{3,7},{4,0},{5,1},{6,2},{7,3},{8,12},{9,13},{10,... | collective-permute-start | bytes 64520 | tf_op jit(solution)/shard_map/ppermute | solution.py:76
  55.2 2.6 %collective-permute-start.19 = (f32[2,2688]{1,0:T(2,128)S(1)}, f32[2,2688]{1,0:T(2,128)S(1)}, u32[]{:S(2)}, u32[]{:S(2)}) collective-permute-start(f32[2,2688]{1,0:T(2,128)S(1)} %get-tuple-element.28), channel_id=1, source_target_pairs={{0,4},{1,5},{2,6},{3,7},{4,0},{5,1},{6,2},{7,3},{8,12},{9,13},{10,... | collective-permute-start | bytes 64520 | tf_op jit(solution)/shard_map/ppermute | solution.py:76
  59.8 3.5 %collective-permute-start.22 = (bf16[2,2048]{1,0:T(2,128)(2,1)S(1)}, bf16[2,2048]{1,0:T(2,128)(2,1)S(1)}, u32[]{:S(2)}, u32[]{:S(2)}) collective-permute-start(bf16[2,2048]{1,0:T(2,128)(2,1)S(1)} %attention_1.1.refs_2_), channel_id=1, source_target_pairs={{0,4},{1,5},{2,6},{3,7},{4,0},{5,1},{6,2},{7,3},{8,12},{9,13},{10,... | collective-permute-start | bytes 24584 | tf_op jit(solution)/shard_map/ppermute | solution.py:76
  61.1 2.5 %collective-permute-start.21 = (bf16[2,2048]{1,0:T(2,128)(2,1)S(1)}, bf16[2,2048]{1,0:T(2,128)(2,1)S(1)}, u32[]{:S(2)}, u32[]{:S(2)}) collective-permute-start(bf16[2,2048]{1,0:T(2,128)(2,1)S(1)} %attention_1.1.refs_2_), channel_id=1, source_target_pairs={{0,4},{1,5},{2,6},{3,7},{4,0},{5,1},{6,2},{7,3},{8,12},{9,13},{10,... | collective-permute-start | bytes 24584 | tf_op jit(solution)/shard_map/ppermute | solution.py:76
  61.6 2.5 %collective-permute-start.20 = (bf16[2,2048]{1,0:T(2,128)(2,1)S(1)}, bf16[2,2048]{1,0:T(2,128)(2,1)S(1)}, u32[]{:S(2)}, u32[]{:S(2)}) collective-permute-start(bf16[2,2048]{1,0:T(2,128)(2,1)S(1)} %attention_1.1.refs_2_), channel_id=1, source_target_pairs={{0,4},{1,5},{2,6},{3,7},{4,0},{5,1},{6,2},{7,3},{8,12},{9,13},{10,... | collective-permute-start | bytes 24584 | tf_op jit(solution)/shard_map/ppermute | solution.py:76
  65.4 4.6 %collective-permute-start.25 = (bf16[8,2048]{1,0:T(8,128)(2,1)S(1)}, bf16[8,2048]{1,0:T(8,128)(2,1)S(1)}, u32[]{:S(2)}, u32[]{:S(2)}) collective-permute-start(bf16[8,2048]{1,0:T(8,128)(2,1)S(1)} %project_1.1.refs_4_), channel_id=1, source_target_pairs={{0,1},{1,0},{2,3},{3,2},{4,5},{5,4},{6,7},{7,6},{8,9},{9,8},{10,11... | collective-permute-start | bytes 98312 | tf_op jit(solution)/shard_map/ppermute | solution.py:76
  67.4 3.7 %collective-permute-start.24 = (bf16[8,2048]{1,0:T(8,128)(2,1)S(1)}, bf16[8,2048]{1,0:T(8,128)(2,1)S(1)}, u32[]{:S(2)}, u32[]{:S(2)}) collective-permute-start(bf16[8,2048]{1,0:T(8,128)(2,1)S(1)} %project_1.1.refs_4_), channel_id=1, source_target_pairs={{0,1},{1,0},{2,3},{3,2},{4,5},{5,4},{6,7},{7,6},{8,9},{9,8},{10,11... | collective-permute-start | bytes 98312 | tf_op jit(solution)/shard_map/ppermute | solution.py:76
  67.4 3.6 %collective-permute-start.23 = (bf16[8,2048]{1,0:T(8,128)(2,1)S(1)}, bf16[8,2048]{1,0:T(8,128)(2,1)S(1)}, u32[]{:S(2)}, u32[]{:S(2)}) collective-permute-start(bf16[8,2048]{1,0:T(8,128)(2,1)S(1)} %project_1.1.refs_4_), channel_id=1, source_target_pairs={{0,1},{1,0},{2,3},{3,2},{4,5},{5,4},{6,7},{7,6},{8,9},{9,8},{10,11... | collective-permute-start | bytes 98312 | tf_op jit(solution)/shard_map/ppermute | solution.py:76
  69.0 17.8 %collective-permute-start.26 = (bf16[8,2048]{1,0:T(8,128)(2,1)S(1)}, bf16[8,2048]{1,0:T(8,128)(2,1)S(1)}, u32[]{:S(2)}, u32[]{:S(2)}) collective-permute-start(bf16[8,2048]{1,0:T(8,128)(2,1)S(1)} %get-tuple-element.24.refs_0_), channel_id=1, source_target_pairs={{0,16},{1,17},{2,18},{3,19},{4,20},{5,21},{6,22},{7,23},{8,24},{9,... | collective-permute-start | bytes 98312 | tf_op jit(solution)/shard_map/ppermute | solution.py:89
  75.0 4.7 %collective-permute-start.29 = (bf16[8,7552]{1,0:T(8,128)(2,1)S(1)}, bf16[8,7552]{1,0:T(8,128)(2,1)S(1)}, u32[]{:S(2)}, u32[]{:S(2)}) collective-permute-start(bf16[8,7552]{1,0:T(8,128)(2,1)S(1)} %get-tuple-element.30.refs_1_), channel_id=1, source_target_pairs={{0,4},{1,5},{2,6},{3,7},{4,0},{5,1},{6,2},{7,3},{8,12},{9,13},{10,... | collective-permute-start | bytes 362504 | tf_op jit(solution)/shard_map/ppermute | solution.py:76
  76.8 4.4 %collective-permute-start.28 = (bf16[8,7552]{1,0:T(8,128)(2,1)S(1)}, bf16[8,7552]{1,0:T(8,128)(2,1)S(1)}, u32[]{:S(2)}, u32[]{:S(2)}) collective-permute-start(bf16[8,7552]{1,0:T(8,128)(2,1)S(1)} %get-tuple-element.30.refs_1_), channel_id=1, source_target_pairs={{0,4},{1,5},{2,6},{3,7},{4,0},{5,1},{6,2},{7,3},{8,12},{9,13},{10,... | collective-permute-start | bytes 362504 | tf_op jit(solution)/shard_map/ppermute | solution.py:76
  77.0 4.2 %collective-permute-start.27 = (bf16[8,7552]{1,0:T(8,128)(2,1)S(1)}, bf16[8,7552]{1,0:T(8,128)(2,1)S(1)}, u32[]{:S(2)}, u32[]{:S(2)}) collective-permute-start(bf16[8,7552]{1,0:T(8,128)(2,1)S(1)} %get-tuple-element.30.refs_1_), channel_id=1, source_target_pairs={{0,4},{1,5},{2,6},{3,7},{4,0},{5,1},{6,2},{7,3},{8,12},{9,13},{10,... | collective-permute-start | bytes 362504 | tf_op jit(solution)/shard_map/ppermute | solution.py:76
  83.2 4.6 %collective-permute-start.32 = (bf16[8,2048]{1,0:T(8,128)(2,1)S(1)}, bf16[8,2048]{1,0:T(8,128)(2,1)S(1)}, u32[]{:S(2)}, u32[]{:S(2)}) collective-permute-start(bf16[8,2048]{1,0:T(8,128)(2,1)S(1)} %down_1.1.refs_2_), channel_id=1, source_target_pairs={{0,1},{1,0},{2,3},{3,2},{4,5},{5,4},{6,7},{7,6},{8,9},{9,8},{10,11... | collective-permute-start | bytes 98312 | tf_op jit(solution)/shard_map/ppermute | solution.py:76
  85.2 3.7 %collective-permute-start.31 = (bf16[8,2048]{1,0:T(8,128)(2,1)S(1)}, bf16[8,2048]{1,0:T(8,128)(2,1)S(1)}, u32[]{:S(2)}, u32[]{:S(2)}) collective-permute-start(bf16[8,2048]{1,0:T(8,128)(2,1)S(1)} %down_1.1.refs_2_), channel_id=1, source_target_pairs={{0,1},{1,0},{2,3},{3,2},{4,5},{5,4},{6,7},{7,6},{8,9},{9,8},{10,11... | collective-permute-start | bytes 98312 | tf_op jit(solution)/shard_map/ppermute | solution.py:76
  85.4 3.4 %collective-permute-start.30 = (bf16[8,2048]{1,0:T(8,128)(2,1)S(1)}, bf16[8,2048]{1,0:T(8,128)(2,1)S(1)}, u32[]{:S(2)}, u32[]{:S(2)}) collective-permute-start(bf16[8,2048]{1,0:T(8,128)(2,1)S(1)} %down_1.1.refs_2_), channel_id=1, source_target_pairs={{0,1},{1,0},{2,3},{3,2},{4,5},{5,4},{6,7},{7,6},{8,9},{9,8},{10,11... | collective-permute-start | bytes 98312 | tf_op jit(solution)/shard_map/ppermute | solution.py:76
  (16 other events, 88.5 us)

commit v5 on v4

--- a/solution.py
+++ b/solution.py
@@ -87,6 +87,19 @@
         for mem in range(mems)
     ]
     return lax.ppermute(value, axes, pairs)
+
+
+def tp_order(count):
+    return (1, 3, 2) if count == 4 else tuple(range(1, count))
+
+
+def tp_taken(pieces):
+    return [pieces[s - 1] for s in tp_order(len(pieces) + 1)]
+
+
+def tp_sum(refs):
+    order = (0, *tp_order(len(refs)))
+    return total_of([refs[order.index(s)] for s in range(len(refs))])
 
 
 def tree_sum(pieces):
@@ -265,7 +278,7 @@
 def hidden_terms_kernel(count, x_ref, gain_ref, wg_ref, wu_ref, *rest):
     pieces = rest[:count]
     after_ref, out_ref = rest[count:]
-    after = (x_ref[...].astype(F32) + total_of(pieces)).astype(BF16)
+    after = (x_ref[...].astype(F32) + tp_sum(pieces)).astype(BF16)
     after_ref[...] = after
     after = after.astype(F32)
     scaled = (after * gain_ref[...].astype(F32)).astype(BF16)
@@ -310,7 +323,7 @@
 def choose_kernel(count, x_ref, first_ref, *rest):
     pieces = rest[:count]
     out_ref = rest[count]
-    second = (x_ref[...].astype(F32) + total_of(pieces)).astype(BF16).astype(F32)
+    second = (x_ref[...].astype(F32) + tp_sum(pieces)).astype(BF16).astype(F32)
     first = first_ref[...].astype(F32)
     out_ref[...] = jnp.where(lax.axis_index("section") == 0, first, second).astype(BF16)
 
@@ -433,7 +446,7 @@
         after, terms = run(
             functools.partial(hidden_terms_kernel, tps),
             [((requests, local_width), BF16), ((requests, term_cols), BF16)],
-            [x, ffn_gain, w_gate[0], w_up[0], projected, *partners([projected] * tps, "tp", int(tag[1:]))],
+            [x, ffn_gain, w_gate[0], w_up[0], projected, *tp_taken(partners([projected] * tps, "tp", int(tag[1:])))],
             section=int(tag[1:]),
             name="terms" + tag,
         )
@@ -456,7 +469,7 @@
     result = run(
         functools.partial(choose_kernel, tps),
         ((requests, local_width), BF16),
-        [after, first, down, *partners([down] * tps, "tp", 1)],
+        [after, first, down, *tp_taken(partners([down] * tps, "tp", 1))],
         name="choose",
     )
     return result[None]

time: 89.6 us -> 88.9 us (level)
  starting transfers between devices: 53.5 us -> 51.5 us
  waiting for transfers between devices: 18.2 us -> 19.5 us
    ppermute x27, starting transfers between devices: 24.7 us -> 22.9 us  [partners(): lax.ppermute(values[s], axes, list(pairs(s)))]
    ppermute x27, waiting for transfers between devices: 16.3 us -> 17.3 us  [partners(): lax.ppermute(values[s], axes, list(pairs(s)))]
  transfers between devices with their start and end apart: 33 -> 33, of which waited for: 22 -> 23; matrix products, arithmetic and copies ran while one was open for 1% -> 1% of each run, Pallas kernels for 7% -> 7%
where the time goes in v5:
time: 88.9 us; the launch traced here: 88.8 us
  starting transfers between devices  51.5 us (58%)
  waiting for transfers between devices  19.5 us (22%)
  Pallas kernels  11.7 us (13%)
  local copies, waits for them, and re-layouts  5.11 us (6%)
    ppermute x6, starting transfers between devices, across(): return lax.ppermute(value, axes, pairs)  28.6 us
    ppermute x27, starting transfers between devices, partners(): lax.ppermute(values[s], axes, list(pairs(s)))  22.9 us
    ppermute x27, waiting for transfers between devices, partners(): lax.ppermute(values[s], axes, list(pairs(s)))  17.3 us
    pallas_call x13, Pallas kernels, run(): pl.pallas_call(in_section, out_shape=[jax.ShapeDtypeStruct(shape, dtype)...  11.7 us
    unnamed x62, local copies, waits for them, and re-layouts  5.04 us
    ppermute x6, waiting for transfers between devices, across(): return lax.ppermute(value, axes, pairs)  2.15 us
  transfers between devices with their start and end apart: 33, of which 23 were waited for; matrix products, arithmetic and copies ran while one was open for 1% of the time, Pallas kernels for 7%

profile of v5, /device:TPU:1, one launch (start us, length us, event | category | flops | bytes accessed | tf_op | source)
XLA Modules:
  0.0 88.8 jit_solution(3384087961996909753)
XLA Ops:
  0.1 2.2 %collective-permute-start = (f32[2,2688]{1,0:T(2,128)S(1)}, f32[2,2688]{1,0:T(2,128)S(1)}, u32[]{:S(2)}, u32[]{:S(2)}) collective-permute-start(f32[2,2688]{1,0:T(2,128)S(1)} %get-tuple-element.19), channel_id=1, source_target_pairs={{0,3},{1,2},{2,1},{3,0},{4,7},{5,6},{6,5},{7,4},{8,11},{9,10},{10,... | collective-permute-start | bytes 64520 | tf_op jit(solution)/shard_map/ppermute | solution.py:76
  2.4 1.4 %collective-permute-start.2 = (f32[2,2688]{1,0:T(2,128)S(1)}, f32[2,2688]{1,0:T(2,128)S(1)}, u32[]{:S(2)}, u32[]{:S(2)}) collective-permute-start(f32[2,2688]{1,0:T(2,128)S(1)} %get-tuple-element.21), channel_id=1, source_target_pairs={{0,1},{1,0},{2,3},{3,2},{4,5},{5,4},{6,7},{7,6},{8,9},{9,8},{10,11... | collective-permute-start | bytes 64520 | tf_op jit(solution)/shard_map/ppermute | solution.py:76
  4.4 0.5 collective-permute-done.1.refs_5_
  5.3 1.3 %copy-done = bf16[1,2,4096,256]{3,2,1,0:T(8,128)(2,1)S(1)} copy-done((bf16[1,2,4096,256]{3,2,1,0:T(8,128)(2,1)S(1)}, bf16[1,2,4096,256]{3,2,1,0:T(8,128)(2,1)}, u32[]{:S(2)}) %copy-start) | copy-done | bytes 4194328
  6.6 1.3 %copy-done.1 = bf16[1,2,4096,256]{3,2,1,0:T(8,128)(2,1)S(1)} copy-done((bf16[1,2,4096,256]{3,2,1,0:T(8,128)(2,1)S(1)}, bf16[1,2,4096,256]{3,2,1,0:T(8,128)(2,1)}, u32[]{:S(2)}) %copy-start.1) | copy-done | bytes 4194328
  8.0 1.4 %collective-permute-start.4 = (bf16[2,2048]{1,0:T(2,128)(2,1)S(1)}, bf16[2,2048]{1,0:T(2,128)(2,1)S(1)}, u32[]{:S(2)}, u32[]{:S(2)}) collective-permute-start(bf16[2,2048]{1,0:T(2,128)(2,1)S(1)} %attention_0.1.refs_2_), channel_id=1, source_target_pairs={{0,2},{1,3},{2,0},{3,1},{4,6},{5,7},{6,4},{7,5},{8,10},{9,11},{10,... | collective-permute-start | bytes 24584 | tf_op jit(solution)/shard_map/ppermute | solution.py:76
  9.5 1.0 %collective-permute-done.5.refs_5_ = bf16[2,2048]{1,0:T(2,128)(2,1)S(1)} collective-permute-done((bf16[2,2048]{1,0:T(2,128)(2,1)S(1)}, bf16[2,2048]{1,0:T(2,128)(2,1)S(1)}, u32[]{:S(2)}, u32[]{:S(2)}) %collective-permute-start.5) | collective-permute-done | bytes 8224 | tf_op jit(solution)/shard_map/ppermute | solution.py:76
  10.6 1.5 %collective-permute-done.3.refs_3_ = bf16[2,2048]{1,0:T(2,128)(2,1)S(1)} collective-permute-done((bf16[2,2048]{1,0:T(2,128)(2,1)S(1)}, bf16[2,2048]{1,0:T(2,128)(2,1)S(1)}, u32[]{:S(2)}, u32[]{:S(2)}) %collective-permute-start.3) | collective-permute-done | bytes 8224 | tf_op jit(solution)/shard_map/ppermute | solution.py:76
  12.2 1.1 %collective-permute-start.8 = (bf16[8,2048]{1,0:T(8,128)(2,1)S(1)}, bf16[8,2048]{1,0:T(8,128)(2,1)S(1)}, u32[]{:S(2)}, u32[]{:S(2)}) collective-permute-start(bf16[8,2048]{1,0:T(8,128)(2,1)S(1)} %project_0.1.refs_4_), channel_id=1, source_target_pairs={{0,8},{1,9},{2,10},{3,11},{4,12},{5,13},{6,14},{7,15},{8,0},{9,1},... | collective-permute-start | bytes 98312 | tf_op jit(solution)/shard_map/ppermute | solution.py:76
  13.3 0.4 collective-permute-start.7
  13.7 1.1 %collective-permute-start.6 = (bf16[8,2048]{1,0:T(8,128)(2,1)S(1)}, bf16[8,2048]{1,0:T(8,128)(2,1)S(1)}, u32[]{:S(2)}, u32[]{:S(2)}) collective-permute-start(bf16[8,2048]{1,0:T(8,128)(2,1)S(1)} %project_0.1.refs_4_), channel_id=1, source_target_pairs={{0,4},{1,5},{2,6},{3,7},{4,0},{5,1},{6,2},{7,3},{8,12},{9,13},{10,... | collective-permute-start | bytes 98312 | tf_op jit(solution)/shard_map/ppermute | solution.py:76
  15.0 1.1 %collective-permute-done.7.refs_6_ = bf16[8,2048]{1,0:T(8,128)(2,1)S(1)} collective-permute-done((bf16[8,2048]{1,0:T(8,128)(2,1)S(1)}, bf16[8,2048]{1,0:T(8,128)(2,1)S(1)}, u32[]{:S(2)}, u32[]{:S(2)}) %collective-permute-start.7) | collective-permute-done | bytes 32800 | tf_op jit(solution)/shard_map/ppermute | solution.py:76
  16.1 0.4 collective-permute-done.6.refs_5_
  16.5 0.5 slice-done.3
  17.0 1.2 %slice-done.6 = s8[4194304]{0:T(1024)(128)(4,1)S(1)} async-done(((s8[14680064]{0:T(1024)(128)(4,1)}), s8[4194304]{0:T(1024)(128)(4,1)S(1)}, s32[]{:S(2)}) %slice-start.6) | async-done | bytes 4194328
  18.2 0.6 slice-done.7
  19.1 1.4 %collective-permute-start.11 = (bf16[8,7552]{1,0:T(8,128)(2,1)S(1)}, bf16[8,7552]{1,0:T(8,128)(2,1)S(1)}, u32[]{:S(2)}, u32[]{:S(2)}) collective-permute-start(bf16[8,7552]{1,0:T(8,128)(2,1)S(1)} %get-tuple-element.23.refs_1_), channel_id=1, source_target_pairs={{0,2},{1,3},{2,0},{3,1},{4,6},{5,7},{6,4},{7,5},{8,10},{9,11},{10,... | collective-permute-start | bytes 362504 | tf_op jit(solution)/shard_map/ppermute | solution.py:76
  20.5 19.2 %collective-permute-start.9 = (bf16[8,2048]{1,0:T(8,128)(2,1)S(1)}, bf16[8,2048]{1,0:T(8,128)(2,1)S(1)}, u32[]{:S(2)}, u32[]{:S(2)}) collective-permute-start(bf16[8,2048]{1,0:T(8,128)(2,1)S(1)} %get-tuple-element.22), channel_id=1, source_target_pairs={{0,16},{1,17},{2,18},{3,19},{4,20},{5,21},{6,22},{7,23},{8,24},{9,... | collective-permute-start | bytes 98312 | tf_op jit(solution)/shard_map/ppermute | solution.py:89
  39.9 7.3 %collective-permute-start.16 = (bf16[8,2048]{1,0:T(8,128)(2,1)S(1)}, bf16[8,2048]{1,0:T(8,128)(2,1)S(1)}, u32[]{:S(2)}, u32[]{:S(2)}) collective-permute-start(bf16[8,2048]{1,0:T(8,128)(2,1)S(1)} %down_0.1), channel_id=1, source_target_pairs={{0,28},{1,29},{2,30},{3,31},{4,24},{5,25},{6,26},{7,27},{8,20},{9,... | collective-permute-start | bytes 98312 | tf_op jit(solution)/shard_map/ppermute | solution.py:89
  47.2 2.1 %collective-permute-start.14 = (bf16[8,2048]{1,0:T(8,128)(2,1)S(1)}, bf16[8,2048]{1,0:T(8,128)(2,1)S(1)}, u32[]{:S(2)}, u32[]{:S(2)}) collective-permute-start(bf16[8,2048]{1,0:T(8,128)(2,1)S(1)} %down_0.1), channel_id=1, source_target_pairs={{0,20},{1,21},{2,22},{3,23},{4,16},{5,17},{6,18},{7,19},{8,28},{9,... | collective-permute-start | bytes 98312 | tf_op jit(solution)/shard_map/ppermute | solution.py:89
  49.3 2.1 %collective-permute-done.15.refs_8_ = bf16[8,2048]{1,0:T(8,128)(2,1)S(1)} collective-permute-done((bf16[8,2048]{1,0:T(8,128)(2,1)S(1)}, bf16[8,2048]{1,0:T(8,128)(2,1)S(1)}, u32[]{:S(2)}, u32[]{:S(2)}) %collective-permute-start.15) | collective-permute-done | bytes 32800 | tf_op jit(solution)/shard_map/ppermute | solution.py:89
  51.5 1.6 %heads_1.1 = (f32[2,2688]{1,0:T(2,128)S(1)}, f32[2,2688]{1,0:T(2,128)S(1)}, f32[2,2688]{1,0:T(2,128)S(1)}, f32[2,2688]{1,0:T(2,128)S(1)}, bf16[8,2048]{1,0:T(8,128)(2,1)S(1)}) custom-call(bf16[8,2048]{1,0:T(8,128)(2,1)S(1)} %collective-permute-done.9.refs_0_, bf16[1,2048]{1,0:T(2,128)(2,1)S(1)} %copy-done.5, bf16[8,8]{1,0:T(8,128)(2,1)S(1)} %get-tuple-element.33.refs_2_, ...), custom_call_target="tpu_custom_call" | custom-call | flops 23000000512 | tf_op jit(solution)/shard_map/heads_1/pallas_call | solution.py:45
  53.1 1.9 %collective-permute-start.17 = (f32[2,2688]{1,0:T(2,128)S(1)}, f32[2,2688]{1,0:T(2,128)S(1)}, u32[]{:S(2)}, u32[]{:S(2)}) collective-permute-start(f32[2,2688]{1,0:T(2,128)S(1)} %get-tuple-element.26), channel_id=1, source_target_pairs={{0,4},{1,5},{2,6},{3,7},{4,0},{5,1},{6,2},{7,3},{8,12},{9,13},{10,... | collective-permute-start | bytes 64520 | tf_op jit(solution)/shard_map/ppermute | solution.py:76
  55.3 0.6 collective-permute-start.19
  55.8 0.9 %collective-permute-done.17.refs_4_ = f32[2,2688]{1,0:T(2,128)S(1)} collective-permute-done((f32[2,2688]{1,0:T(2,128)S(1)}, f32[2,2688]{1,0:T(2,128)S(1)}, u32[]{:S(2)}, u32[]{:S(2)}) %collective-permute-start.17) | collective-permute-done | bytes 21536 | tf_op jit(solution)/shard_map/ppermute | solution.py:76
  56.7 1.0 %collective-permute-done.18.refs_5_ = f32[2,2688]{1,0:T(2,128)S(1)} collective-permute-done((f32[2,2688]{1,0:T(2,128)S(1)}, f32[2,2688]{1,0:T(2,128)S(1)}, u32[]{:S(2)}, u32[]{:S(2)}) %collective-permute-start.18) | collective-permute-done | bytes 21536 | tf_op jit(solution)/shard_map/ppermute | solution.py:76
  57.9 2.0 %attention_1.1.refs_2_ = bf16[2,2048]{1,0:T(2,128)(2,1)S(1)} custom-call(s32[2,128]{1,0:T(2,128)S(1)} %broadcast_in_dim.47.refs_0_, f32[2,128]{1,0:T(2,128)S(1)} %get-tuple-element.36.refs_0_.refs_1_, f32[2,128]{1,0:T(2,128)S(1)} %get-tuple-element.37.refs_2_, f32[2,2688]{1,0:T(2,128)S(1)} %get-tuple-element.25.refs_3_, ...), custom_call_target="tpu_custom_call" | custom-call | flops 23000000512 | tf_op jit(solution)/shard_map/attention_1/pallas_call | solution.py:45
  59.9 1.3 %collective-permute-start.22 = (bf16[2,2048]{1,0:T(2,128)(2,1)S(1)}, bf16[2,2048]{1,0:T(2,128)(2,1)S(1)}, u32[]{:S(2)}, u32[]{:S(2)}) collective-permute-start(bf16[2,2048]{1,0:T(2,128)(2,1)S(1)} %attention_1.1.refs_2_), channel_id=1, source_target_pairs={{0,4},{1,5},{2,6},{3,7},{4,0},{5,1},{6,2},{7,3},{8,12},{9,13},{10,... | collective-permute-start | bytes 24584 | tf_op jit(solution)/shard_map/ppermute | solution.py:76
  61.2 0.5 collective-permute-start.21
  61.7 0.9 %collective-permute-start.20 = (bf16[2,2048]{1,0:T(2,128)(2,1)S(1)}, bf16[2,2048]{1,0:T(2,128)(2,1)S(1)}, u32[]{:S(2)}, u32[]{:S(2)}) collective-permute-start(bf16[2,2048]{1,0:T(2,128)(2,1)S(1)} %attention_1.1.refs_2_), channel_id=1, source_target_pairs={{0,4},{1,5},{2,6},{3,7},{4,0},{5,1},{6,2},{7,3},{8,12},{9,13},{10,... | collective-permute-start | bytes 24584 | tf_op jit(solution)/shard_map/ppermute | solution.py:76
  62.6 0.8 collective-permute-done.22.refs_5_
  63.7 0.5 collective-permute-done.20.refs_3_
  64.2 1.3 %project_1.1.refs_4_ = bf16[8,2048]{1,0:T(8,128)(2,1)S(1)} custom-call(bf16[8,8]{1,0:T(8,128)(2,1)S(1)} %get-tuple-element.35.refs_0_, bf16[2048,2048]{1,0:T(8,128)(2,1)S(1)} %bitcast.33, bf16[2,2048]{1,0:T(2,128)(2,1)S(1)} %attention_1.1.refs_2_, bf16[2,2048]{1,0:T(2,128)(2,1)S(1)} %collective-permute-done.20.refs_3_, ...), custom_call_target="tpu_custom_call" | custom-call | flops 23000000512 | tf_op jit(solution)/shard_map/project_1/pallas_call | solution.py:45
  65.9 1.6 %collective-permute-start.24 = (bf16[8,2048]{1,0:T(8,128)(2,1)S(1)}, bf16[8,2048]{1,0:T(8,128)(2,1)S(1)}, u32[]{:S(2)}, u32[]{:S(2)}) collective-permute-start(bf16[8,2048]{1,0:T(8,128)(2,1)S(1)} %project_1.1.refs_4_), channel_id=1, source_target_pairs={{0,1},{1,0},{2,3},{3,2},{4,5},{5,4},{6,7},{7,6},{8,9},{9,8},{10,11... | collective-permute-start | bytes 98312 | tf_op jit(solution)/shard_map/ppermute | solution.py:76
  67.4 0.7 collective-permute-start.23
  68.2 1.0 %collective-permute-done.25.refs_7_ = bf16[8,2048]{1,0:T(8,128)(2,1)S(1)} collective-permute-done((bf16[8,2048]{1,0:T(8,128)(2,1)S(1)}, bf16[8,2048]{1,0:T(8,128)(2,1)S(1)}, u32[]{:S(2)}, u32[]{:S(2)}) %collective-permute-start.25) | collective-permute-done | bytes 32800 | tf_op jit(solution)/shard_map/ppermute | solution.py:76
  69.2 1.4 %collective-permute-done.24.refs_6_ = bf16[8,2048]{1,0:T(8,128)(2,1)S(1)} collective-permute-done((bf16[8,2048]{1,0:T(8,128)(2,1)S(1)}, bf16[8,2048]{1,0:T(8,128)(2,1)S(1)}, u32[]{:S(2)}, u32[]{:S(2)}) %collective-permute-start.24) | collective-permute-done | bytes 32800 | tf_op jit(solution)/shard_map/ppermute | solution.py:76
  70.5 3.9 %terms_1.1 = (bf16[8,2048]{1,0:T(8,128)(2,1)S(1)}, bf16[8,7552]{1,0:T(8,128)(2,1)S(1)}) custom-call(bf16[8,2048]{1,0:T(8,128)(2,1)S(1)} %get-tuple-element.24.refs_0_, bf16[1,2048]{1,0:T(2,128)(2,1)S(1)} %copy-done.6, bf16[2048,3584]{1,0:T(8,128)(2,1)S(1)} %bitcast.13, bf16[2048,3584]{1,0:T(8,128)(2,1)S(1)} %bitcast.17, ...), custom_call_target="tpu_custom_call" | custom-call | flops 23000000512 | tf_op jit(solution)/shard_map/terms_1/pallas_call | solution.py:45
  74.5 1.9 %collective-permute-start.29 = (bf16[8,7552]{1,0:T(8,128)(2,1)S(1)}, bf16[8,7552]{1,0:T(8,128)(2,1)S(1)}, u32[]{:S(2)}, u32[]{:S(2)}) collective-permute-start(bf16[8,7552]{1,0:T(8,128)(2,1)S(1)} %get-tuple-element.30.refs_1_), channel_id=1, source_target_pairs={{0,4},{1,5},{2,6},{3,7},{4,0},{5,1},{6,2},{7,3},{8,12},{9,13},{10,... | collective-permute-start | bytes 362504 | tf_op jit(solution)/shard_map/ppermute | solution.py:76
  76.6 0.6 collective-permute-start.27
  77.2 2.0 %collective-permute-done.29.refs_4_ = bf16[8,7552]{1,0:T(8,128)(2,1)S(1)} collective-permute-done((bf16[8,7552]{1,0:T(8,128)(2,1)S(1)}, bf16[8,7552]{1,0:T(8,128)(2,1)S(1)}, u32[]{:S(2)}, u32[]{:S(2)}) %collective-permute-start.29) | collective-permute-done | bytes 120864 | tf_op jit(solution)/shard_map/ppermute | solution.py:76
  79.2 1.6 %collective-permute-done.28.refs_3_ = bf16[8,7552]{1,0:T(8,128)(2,1)S(1)} collective-permute-done((bf16[8,7552]{1,0:T(8,128)(2,1)S(1)}, bf16[8,7552]{1,0:T(8,128)(2,1)S(1)}, u32[]{:S(2)}, u32[]{:S(2)}) %collective-permute-start.28) | collective-permute-done | bytes 120864 | tf_op jit(solution)/shard_map/ppermute | solution.py:76
  81.0 2.1 %down_1.1.refs_2_ = bf16[8,2048]{1,0:T(8,128)(2,1)S(1)} custom-call(bf16[3584,2048]{1,0:T(8,128)(2,1)S(1)} %bitcast.23, bf16[8,7552]{1,0:T(8,128)(2,1)S(1)} %get-tuple-element.30.refs_1_, bf16[8,7552]{1,0:T(8,128)(2,1)S(1)} %collective-permute-done.27.refs_2_, bf16[8,7552]{1,0:T(8,128)(2,1)S(1)} %collective-permute-done.28.refs_3_, ...), custom_call_target="tpu_custom_call" | custom-call | flops 23000000512 | tf_op jit(solution)/shard_map/down_1/pallas_call | solution.py:45
  83.3 1.7 %collective-permute-start.31 = (bf16[8,2048]{1,0:T(8,128)(2,1)S(1)}, bf16[8,2048]{1,0:T(8,128)(2,1)S(1)}, u32[]{:S(2)}, u32[]{:S(2)}) collective-permute-start(bf16[8,2048]{1,0:T(8,128)(2,1)S(1)} %down_1.1.refs_2_), channel_id=1, source_target_pairs={{0,1},{1,0},{2,3},{3,2},{4,5},{5,4},{6,7},{7,6},{8,9},{9,8},{10,11... | collective-permute-start | bytes 98312 | tf_op jit(solution)/shard_map/ppermute | solution.py:76
  85.0 0.7 collective-permute-start.30
  85.8 1.0 %collective-permute-done.32.refs_5_ = bf16[8,2048]{1,0:T(8,128)(2,1)S(1)} collective-permute-done((bf16[8,2048]{1,0:T(8,128)(2,1)S(1)}, bf16[8,2048]{1,0:T(8,128)(2,1)S(1)}, u32[]{:S(2)}, u32[]{:S(2)}) %collective-permute-start.32) | collective-permute-done | bytes 32800 | tf_op jit(solution)/shard_map/ppermute | solution.py:76
  86.8 1.2 %collective-permute-done.31.refs_4_ = bf16[8,2048]{1,0:T(8,128)(2,1)S(1)} collective-permute-done((bf16[8,2048]{1,0:T(8,128)(2,1)S(1)}, bf16[8,2048]{1,0:T(8,128)(2,1)S(1)}, u32[]{:S(2)}, u32[]{:S(2)}) %collective-permute-start.31) | collective-permute-done | bytes 32800 | tf_op jit(solution)/shard_map/ppermute | solution.py:76
  88.2 0.6 choose.1
  (109 shorter events, 4.1 us)
Async XLA Ops:
  0.1 4.3 %collective-permute-start = (f32[2,2688]{1,0:T(2,128)S(1)}, f32[2,2688]{1,0:T(2,128)S(1)}, u32[]{:S(2)}, u32[]{:S(2)}) collective-permute-start(f32[2,2688]{1,0:T(2,128)S(1)} %get-tuple-element.19), channel_id=1, source_target_pairs={{0,3},{1,2},{2,1},{3,0},{4,7},{5,6},{6,5},{7,4},{8,11},{9,10},{10,... | collective-permute-start | bytes 64520 | tf_op jit(solution)/shard_map/ppermute | solution.py:76
  2.3 2.6 %collective-permute-start.1 = (f32[2,2688]{1,0:T(2,128)S(1)}, f32[2,2688]{1,0:T(2,128)S(1)}, u32[]{:S(2)}, u32[]{:S(2)}) collective-permute-start(f32[2,2688]{1,0:T(2,128)S(1)} %get-tuple-element.20), channel_id=1, source_target_pairs={{0,2},{1,3},{2,0},{3,1},{4,6},{5,7},{6,4},{7,5},{8,10},{9,11},{10,... | collective-permute-start | bytes 64520 | tf_op jit(solution)/shard_map/ppermute | solution.py:76
  2.4 2.8 %collective-permute-start.2 = (f32[2,2688]{1,0:T(2,128)S(1)}, f32[2,2688]{1,0:T(2,128)S(1)}, u32[]{:S(2)}, u32[]{:S(2)}) collective-permute-start(f32[2,2688]{1,0:T(2,128)S(1)} %get-tuple-element.21), channel_id=1, source_target_pairs={{0,1},{1,0},{2,3},{3,2},{4,5},{5,4},{6,7},{7,6},{8,9},{9,8},{10,11... | collective-permute-start | bytes 64520 | tf_op jit(solution)/shard_map/ppermute | solution.py:76
  7.9 8.7 %slice-start = ((s8[14680064]{0:T(1024)(128)(4,1)}), s8[4194304]{0:T(1024)(128)(4,1)S(1)}, s32[]{:S(2)}) async-start(s8[14680064]{0:T(1024)(128)(4,1)} %bitcast.10), calls=%async_computation | async-start | bytes 8388608
  7.9 8.7 %slice-start.1 = ((s8[14680064]{0:T(1024)(128)(4,1)}), s8[4194304]{0:T(1024)(128)(4,1)S(1)}, s32[]{:S(2)}) async-start(s8[14680064]{0:T(1024)(128)(4,1)} %bitcast.10), calls=%async_computation.1 | async-start | bytes 8388608
  7.9 8.7 %slice-start.4 = ((s8[14680064]{0:T(1024)(128)(4,1)}), s8[4194304]{0:T(1024)(128)(4,1)S(1)}, s32[]{:S(2)}) async-start(s8[14680064]{0:T(1024)(128)(4,1)} %bitcast.14), calls=%async_computation.4 | async-start | bytes 8388608
  7.9 8.7 %slice-start.5 = ((s8[14680064]{0:T(1024)(128)(4,1)}), s8[4194304]{0:T(1024)(128)(4,1)S(1)}, s32[]{:S(2)}) async-start(s8[14680064]{0:T(1024)(128)(4,1)} %bitcast.14), calls=%async_computation.5 | async-start | bytes 8388608
  7.9 2.6 %collective-permute-start.5 = (bf16[2,2048]{1,0:T(2,128)(2,1)S(1)}, bf16[2,2048]{1,0:T(2,128)(2,1)S(1)}, u32[]{:S(2)}, u32[]{:S(2)}) collective-permute-start(bf16[2,2048]{1,0:T(2,128)(2,1)S(1)} %attention_0.1.refs_2_), channel_id=1, source_target_pairs={{0,3},{1,2},{2,1},{3,0},{4,7},{5,6},{6,5},{7,4},{8,11},{9,10},{10,... | collective-permute-start | bytes 24584 | tf_op jit(solution)/shard_map/ppermute | solution.py:76
  8.0 2.5 %collective-permute-start.4 = (bf16[2,2048]{1,0:T(2,128)(2,1)S(1)}, bf16[2,2048]{1,0:T(2,128)(2,1)S(1)}, u32[]{:S(2)}, u32[]{:S(2)}) collective-permute-start(bf16[2,2048]{1,0:T(2,128)(2,1)S(1)} %attention_0.1.refs_2_), channel_id=1, source_target_pairs={{0,2},{1,3},{2,0},{3,1},{4,6},{5,7},{6,4},{7,5},{8,10},{9,11},{10,... | collective-permute-start | bytes 24584 | tf_op jit(solution)/shard_map/ppermute | solution.py:76
  9.4 2.7 %collective-permute-start.3 = (bf16[2,2048]{1,0:T(2,128)(2,1)S(1)}, bf16[2,2048]{1,0:T(2,128)(2,1)S(1)}, u32[]{:S(2)}, u32[]{:S(2)}) collective-permute-start(bf16[2,2048]{1,0:T(2,128)(2,1)S(1)} %attention_0.1.refs_2_), channel_id=1, source_target_pairs={{0,1},{1,0},{2,3},{3,2},{4,5},{5,4},{6,7},{7,6},{8,9},{9,8},{10,11... | collective-permute-start | bytes 24584 | tf_op jit(solution)/shard_map/ppermute | solution.py:76
  12.2 27.6 %slice-start.8 = ((s8[14680064]{0:T(1024)(128)(4,1)}), s8[2097152]{0:T(1024)(128)(4,1)S(1)}, s32[]{:S(2)}) async-start(s8[14680064]{0:T(1024)(128)(4,1)} %bitcast.18), calls=%async_computation.8 | async-start | bytes 4194304
  12.2 27.6 %slice-start.9 = ((s8[14680064]{0:T(1024)(128)(4,1)}), s8[4194304]{0:T(1024)(128)(4,1)S(1)}, s32[]{:S(2)}) async-start(s8[14680064]{0:T(1024)(128)(4,1)} %bitcast.18), calls=%async_computation.9 | async-start | bytes 8388608
  12.2 2.8 %collective-permute-start.8 = (bf16[8,2048]{1,0:T(8,128)(2,1)S(1)}, bf16[8,2048]{1,0:T(8,128)(2,1)S(1)}, u32[]{:S(2)}, u32[]{:S(2)}) collective-permute-start(bf16[8,2048]{1,0:T(8,128)(2,1)S(1)} %project_0.1.refs_4_), channel_id=1, source_target_pairs={{0,8},{1,9},{2,10},{3,11},{4,12},{5,13},{6,14},{7,15},{8,0},{9,1},... | collective-permute-start | bytes 98312 | tf_op jit(solution)/shard_map/ppermute | solution.py:76
  13.3 2.8 %collective-permute-start.7 = (bf16[8,2048]{1,0:T(8,128)(2,1)S(1)}, bf16[8,2048]{1,0:T(8,128)(2,1)S(1)}, u32[]{:S(2)}, u32[]{:S(2)}) collective-permute-start(bf16[8,2048]{1,0:T(8,128)(2,1)S(1)} %project_0.1.refs_4_), channel_id=1, source_target_pairs={{0,12},{1,13},{2,14},{3,15},{4,8},{5,9},{6,10},{7,11},{8,4},{9,5},... | collective-permute-start | bytes 98312 | tf_op jit(solution)/shard_map/ppermute | solution.py:76
  13.7 2.8 %collective-permute-start.6 = (bf16[8,2048]{1,0:T(8,128)(2,1)S(1)}, bf16[8,2048]{1,0:T(8,128)(2,1)S(1)}, u32[]{:S(2)}, u32[]{:S(2)}) collective-permute-start(bf16[8,2048]{1,0:T(8,128)(2,1)S(1)} %project_0.1.refs_4_), channel_id=1, source_target_pairs={{0,4},{1,5},{2,6},{3,7},{4,0},{5,1},{6,2},{7,3},{8,12},{9,13},{10,... | collective-permute-start | bytes 98312 | tf_op jit(solution)/shard_map/ppermute | solution.py:76
  18.8 21.0 %slice-start.10 = ((s8[14680064]{0:T(1024)(128)(4,1)}), s8[4194304]{0:T(1024)(128)(4,1)S(1)}, s32[]{:S(2)}) async-start(s8[14680064]{0:T(1024)(128)(4,1)} %bitcast.18), calls=%async_computation.10 | async-start | bytes 8388608
  18.8 21.0 %slice-start.11 = ((s8[14680064]{0:T(1024)(128)(4,1)}), s8[4194304]{0:T(1024)(128)(4,1)S(1)}, s32[]{:S(2)}) async-start(s8[14680064]{0:T(1024)(128)(4,1)} %bitcast.18), calls=%async_computation.11 | async-start | bytes 8388608
  18.9 32.6 %slice-start.16 = ((s8[8388608]{0:T(1024)(128)(4,1)}), s8[4194304]{0:T(1024)(128)(4,1)S(1)}, s32[]{:S(2)}) async-start(s8[8388608]{0:T(1024)(128)(4,1)} %bitcast.25), calls=%async_computation.16 | async-start | bytes 8388608
  18.9 32.5 %slice-start.17 = ((s8[8388608]{0:T(1024)(128)(4,1)}), s8[4194304]{0:T(1024)(128)(4,1)S(1)}, s32[]{:S(2)}) async-start(s8[8388608]{0:T(1024)(128)(4,1)} %bitcast.25), calls=%async_computation.17 | async-start | bytes 8388608
  18.9 20.8 %collective-permute-start.12 = (bf16[8,7552]{1,0:T(8,128)(2,1)S(1)}, bf16[8,7552]{1,0:T(8,128)(2,1)S(1)}, u32[]{:S(2)}, u32[]{:S(2)}) collective-permute-start(bf16[8,7552]{1,0:T(8,128)(2,1)S(1)} %get-tuple-element.23.refs_1_), channel_id=1, source_target_pairs={{0,3},{1,2},{2,1},{3,0},{4,7},{5,6},{6,5},{7,4},{8,11},{9,10},{10,... | collective-permute-start | bytes 362504 | tf_op jit(solution)/shard_map/ppermute | solution.py:76
  19.1 20.7 %collective-permute-start.11 = (bf16[8,7552]{1,0:T(8,128)(2,1)S(1)}, bf16[8,7552]{1,0:T(8,128)(2,1)S(1)}, u32[]{:S(2)}, u32[]{:S(2)}) collective-permute-start(bf16[8,7552]{1,0:T(8,128)(2,1)S(1)} %get-tuple-element.23.refs_1_), channel_id=1, source_target_pairs={{0,2},{1,3},{2,0},{3,1},{4,6},{5,7},{6,4},{7,5},{8,10},{9,11},{10,... | collective-permute-start | bytes 362504 | tf_op jit(solution)/shard_map/ppermute | solution.py:76
  20.5 19.3 %collective-permute-start.10 = (bf16[8,7552]{1,0:T(8,128)(2,1)S(1)}, bf16[8,7552]{1,0:T(8,128)(2,1)S(1)}, u32[]{:S(2)}, u32[]{:S(2)}) collective-permute-start(bf16[8,7552]{1,0:T(8,128)(2,1)S(1)} %get-tuple-element.23.refs_1_), channel_id=1, source_target_pairs={{0,1},{1,0},{2,3},{3,2},{4,5},{5,4},{6,7},{7,6},{8,9},{9,8},{10,11... | collective-permute-start | bytes 362504 | tf_op jit(solution)/shard_map/ppermute | solution.py:76
  20.5 28.8 %collective-permute-start.9 = (bf16[8,2048]{1,0:T(8,128)(2,1)S(1)}, bf16[8,2048]{1,0:T(8,128)(2,1)S(1)}, u32[]{:S(2)}, u32[]{:S(2)}) collective-permute-start(bf16[8,2048]{1,0:T(8,128)(2,1)S(1)} %get-tuple-element.22), channel_id=1, source_target_pairs={{0,16},{1,17},{2,18},{3,19},{4,20},{5,21},{6,22},{7,23},{8,24},{9,... | collective-permute-start | bytes 98312 | tf_op jit(solution)/shard_map/ppermute | solution.py:89
  39.8 11.6 %copy-start.2 = (bf16[1,2048,256]{2,1,0:T(8,128)(2,1)S(1)}, bf16[1,2048,256]{2,1,0:T(8,128)(2,1)}, u32[]{:S(2)}) copy-start(bf16[1,2048,256]{2,1,0:T(8,128)(2,1)} %param.19) | copy-start | bytes 3145732
  39.8 11.6 %copy-start.3 = (bf16[1,2048,256]{2,1,0:T(8,128)(2,1)S(1)}, bf16[1,2048,256]{2,1,0:T(8,128)(2,1)}, u32[]{:S(2)}) copy-start(bf16[1,2048,256]{2,1,0:T(8,128)(2,1)} %param.20) | copy-start | bytes 3145732
  39.8 11.6 %copy-start.5 = (bf16[1,2048]{1,0:T(2,128)(2,1)S(1)}, bf16[1,2048]{1,0:T(2,128)(2,1)}, u32[]{:S(2)}) copy-start(bf16[1,2048]{1,0:T(2,128)(2,1)} %refs_1_.6) | copy-start | bytes 12292
  39.9 9.4 %collective-permute-start.16 = (bf16[8,2048]{1,0:T(8,128)(2,1)S(1)}, bf16[8,2048]{1,0:T(8,128)(2,1)S(1)}, u32[]{:S(2)}, u32[]{:S(2)}) collective-permute-start(bf16[8,2048]{1,0:T(8,128)(2,1)S(1)} %down_0.1), channel_id=1, source_target_pairs={{0,28},{1,29},{2,30},{3,31},{4,24},{5,25},{6,26},{7,27},{8,20},{9,... | collective-permute-start | bytes 98312 | tf_op jit(solution)/shard_map/ppermute | solution.py:89
  47.2 4.2 %collective-permute-start.15 = (bf16[8,2048]{1,0:T(8,128)(2,1)S(1)}, bf16[8,2048]{1,0:T(8,128)(2,1)S(1)}, u32[]{:S(2)}, u32[]{:S(2)}) collective-permute-start(bf16[8,2048]{1,0:T(8,128)(2,1)S(1)} %down_0.1), channel_id=1, source_target_pairs={{0,24},{1,25},{2,26},{3,27},{4,28},{5,29},{6,30},{7,31},{8,16},{9,... | collective-permute-start | bytes 98312 | tf_op jit(solution)/shard_map/ppermute | solution.py:89
  47.2 4.2 %collective-permute-start.14 = (bf16[8,2048]{1,0:T(8,128)(2,1)S(1)}, bf16[8,2048]{1,0:T(8,128)(2,1)S(1)}, u32[]{:S(2)}, u32[]{:S(2)}) collective-permute-start(bf16[8,2048]{1,0:T(8,128)(2,1)S(1)} %down_0.1), channel_id=1, source_target_pairs={{0,20},{1,21},{2,22},{3,23},{4,16},{5,17},{6,18},{7,19},{8,28},{9,... | collective-permute-start | bytes 98312 | tf_op jit(solution)/shard_map/ppermute | solution.py:89
  49.3 2.2 %collective-permute-start.13 = (bf16[8,2048]{1,0:T(8,128)(2,1)S(1)}, bf16[8,2048]{1,0:T(8,128)(2,1)S(1)}, u32[]{:S(2)}, u32[]{:S(2)}) collective-permute-start(bf16[8,2048]{1,0:T(8,128)(2,1)S(1)} %down_0.1), channel_id=1, source_target_pairs={{0,16},{1,17},{2,18},{3,19},{4,20},{5,21},{6,22},{7,23},{8,24},{9,... | collective-permute-start | bytes 98312 | tf_op jit(solution)/shard_map/ppermute | solution.py:89
  51.5 12.7 %slice-start.20 = ((s8[8388608]{0:T(1024)(128)(4,1)}), s8[4194304]{0:T(1024)(128)(4,1)S(1)}, s32[]{:S(2)}) async-start(s8[8388608]{0:T(1024)(128)(4,1)} %bitcast.31), calls=%async_computation.20 | async-start | bytes 8388608
  53.1 3.6 %collective-permute-start.17 = (f32[2,2688]{1,0:T(2,128)S(1)}, f32[2,2688]{1,0:T(2,128)S(1)}, u32[]{:S(2)}, u32[]{:S(2)}) collective-permute-start(f32[2,2688]{1,0:T(2,128)S(1)} %get-tuple-element.26), channel_id=1, source_target_pairs={{0,4},{1,5},{2,6},{3,7},{4,0},{5,1},{6,2},{7,3},{8,12},{9,13},{10,... | collective-permute-start | bytes 64520 | tf_op jit(solution)/shard_map/ppermute | solution.py:76
  55.1 9.1 %slice-start.21 = ((s8[8388608]{0:T(1024)(128)(4,1)}), s8[4194304]{0:T(1024)(128)(4,1)S(1)}, s32[]{:S(2)}) async-start(s8[8388608]{0:T(1024)(128)(4,1)} %bitcast.31), calls=%async_computation.21 | async-start | bytes 8388608
  55.1 2.6 %collective-permute-start.18 = (f32[2,2688]{1,0:T(2,128)S(1)}, f32[2,2688]{1,0:T(2,128)S(1)}, u32[]{:S(2)}, u32[]{:S(2)}) collective-permute-start(f32[2,2688]{1,0:T(2,128)S(1)} %get-tuple-element.27), channel_id=1, source_target_pairs={{0,4},{1,5},{2,6},{3,7},{4,0},{5,1},{6,2},{7,3},{8,12},{9,13},{10,... | collective-permute-start | bytes 64520 | tf_op jit(solution)/shard_map/ppermute | solution.py:76
  55.3 2.6 %collective-permute-start.19 = (f32[2,2688]{1,0:T(2,128)S(1)}, f32[2,2688]{1,0:T(2,128)S(1)}, u32[]{:S(2)}, u32[]{:S(2)}) collective-permute-start(f32[2,2688]{1,0:T(2,128)S(1)} %get-tuple-element.28), channel_id=1, source_target_pairs={{0,4},{1,5},{2,6},{3,7},{4,0},{5,1},{6,2},{7,3},{8,12},{9,13},{10,... | collective-permute-start | bytes 64520 | tf_op jit(solution)/shard_map/ppermute | solution.py:76
  59.9 3.5 %collective-permute-start.22 = (bf16[2,2048]{1,0:T(2,128)(2,1)S(1)}, bf16[2,2048]{1,0:T(2,128)(2,1)S(1)}, u32[]{:S(2)}, u32[]{:S(2)}) collective-permute-start(bf16[2,2048]{1,0:T(2,128)(2,1)S(1)} %attention_1.1.refs_2_), channel_id=1, source_target_pairs={{0,4},{1,5},{2,6},{3,7},{4,0},{5,1},{6,2},{7,3},{8,12},{9,13},{10,... | collective-permute-start | bytes 24584 | tf_op jit(solution)/shard_map/ppermute | solution.py:76
  61.2 2.5 %collective-permute-start.21 = (bf16[2,2048]{1,0:T(2,128)(2,1)S(1)}, bf16[2,2048]{1,0:T(2,128)(2,1)S(1)}, u32[]{:S(2)}, u32[]{:S(2)}) collective-permute-start(bf16[2,2048]{1,0:T(2,128)(2,1)S(1)} %attention_1.1.refs_2_), channel_id=1, source_target_pairs={{0,4},{1,5},{2,6},{3,7},{4,0},{5,1},{6,2},{7,3},{8,12},{9,13},{10,... | collective-permute-start | bytes 24584 | tf_op jit(solution)/shard_map/ppermute | solution.py:76
  61.7 2.5 %collective-permute-start.20 = (bf16[2,2048]{1,0:T(2,128)(2,1)S(1)}, bf16[2,2048]{1,0:T(2,128)(2,1)S(1)}, u32[]{:S(2)}, u32[]{:S(2)}) collective-permute-start(bf16[2,2048]{1,0:T(2,128)(2,1)S(1)} %attention_1.1.refs_2_), channel_id=1, source_target_pairs={{0,4},{1,5},{2,6},{3,7},{4,0},{5,1},{6,2},{7,3},{8,12},{9,13},{10,... | collective-permute-start | bytes 24584 | tf_op jit(solution)/shard_map/ppermute | solution.py:76
  65.5 3.7 %collective-permute-start.25 = (bf16[8,2048]{1,0:T(8,128)(2,1)S(1)}, bf16[8,2048]{1,0:T(8,128)(2,1)S(1)}, u32[]{:S(2)}, u32[]{:S(2)}) collective-permute-start(bf16[8,2048]{1,0:T(8,128)(2,1)S(1)} %project_1.1.refs_4_), channel_id=1, source_target_pairs={{0,1},{1,0},{2,3},{3,2},{4,5},{5,4},{6,7},{7,6},{8,9},{9,8},{10,11... | collective-permute-start | bytes 98312 | tf_op jit(solution)/shard_map/ppermute | solution.py:76
  65.9 4.7 %collective-permute-start.24 = (bf16[8,2048]{1,0:T(8,128)(2,1)S(1)}, bf16[8,2048]{1,0:T(8,128)(2,1)S(1)}, u32[]{:S(2)}, u32[]{:S(2)}) collective-permute-start(bf16[8,2048]{1,0:T(8,128)(2,1)S(1)} %project_1.1.refs_4_), channel_id=1, source_target_pairs={{0,1},{1,0},{2,3},{3,2},{4,5},{5,4},{6,7},{7,6},{8,9},{9,8},{10,11... | collective-permute-start | bytes 98312 | tf_op jit(solution)/shard_map/ppermute | solution.py:76
  67.4 3.1 %collective-permute-start.23 = (bf16[8,2048]{1,0:T(8,128)(2,1)S(1)}, bf16[8,2048]{1,0:T(8,128)(2,1)S(1)}, u32[]{:S(2)}, u32[]{:S(2)}) collective-permute-start(bf16[8,2048]{1,0:T(8,128)(2,1)S(1)} %project_1.1.refs_4_), channel_id=1, source_target_pairs={{0,1},{1,0},{2,3},{3,2},{4,5},{5,4},{6,7},{7,6},{8,9},{9,8},{10,11... | collective-permute-start | bytes 98312 | tf_op jit(solution)/shard_map/ppermute | solution.py:76
  68.2 17.6 %collective-permute-start.26 = (bf16[8,2048]{1,0:T(8,128)(2,1)S(1)}, bf16[8,2048]{1,0:T(8,128)(2,1)S(1)}, u32[]{:S(2)}, u32[]{:S(2)}) collective-permute-start(bf16[8,2048]{1,0:T(8,128)(2,1)S(1)} %get-tuple-element.24.refs_0_), channel_id=1, source_target_pairs={{0,16},{1,17},{2,18},{3,19},{4,20},{5,21},{6,22},{7,23},{8,24},{9,... | collective-permute-start | bytes 98312 | tf_op jit(solution)/shard_map/ppermute | solution.py:89
  74.5 4.7 %collective-permute-start.29 = (bf16[8,7552]{1,0:T(8,128)(2,1)S(1)}, bf16[8,7552]{1,0:T(8,128)(2,1)S(1)}, u32[]{:S(2)}, u32[]{:S(2)}) collective-permute-start(bf16[8,7552]{1,0:T(8,128)(2,1)S(1)} %get-tuple-element.30.refs_1_), channel_id=1, source_target_pairs={{0,4},{1,5},{2,6},{3,7},{4,0},{5,1},{6,2},{7,3},{8,12},{9,13},{10,... | collective-permute-start | bytes 362504 | tf_op jit(solution)/shard_map/ppermute | solution.py:76
  76.4 4.3 %collective-permute-start.28 = (bf16[8,7552]{1,0:T(8,128)(2,1)S(1)}, bf16[8,7552]{1,0:T(8,128)(2,1)S(1)}, u32[]{:S(2)}, u32[]{:S(2)}) collective-permute-start(bf16[8,7552]{1,0:T(8,128)(2,1)S(1)} %get-tuple-element.30.refs_1_), channel_id=1, source_target_pairs={{0,4},{1,5},{2,6},{3,7},{4,0},{5,1},{6,2},{7,3},{8,12},{9,13},{10,... | collective-permute-start | bytes 362504 | tf_op jit(solution)/shard_map/ppermute | solution.py:76
  76.6 4.3 %collective-permute-start.27 = (bf16[8,7552]{1,0:T(8,128)(2,1)S(1)}, bf16[8,7552]{1,0:T(8,128)(2,1)S(1)}, u32[]{:S(2)}, u32[]{:S(2)}) collective-permute-start(bf16[8,7552]{1,0:T(8,128)(2,1)S(1)} %get-tuple-element.30.refs_1_), channel_id=1, source_target_pairs={{0,4},{1,5},{2,6},{3,7},{4,0},{5,1},{6,2},{7,3},{8,12},{9,13},{10,... | collective-permute-start | bytes 362504 | tf_op jit(solution)/shard_map/ppermute | solution.py:76
  83.1 3.7 %collective-permute-start.32 = (bf16[8,2048]{1,0:T(8,128)(2,1)S(1)}, bf16[8,2048]{1,0:T(8,128)(2,1)S(1)}, u32[]{:S(2)}, u32[]{:S(2)}) collective-permute-start(bf16[8,2048]{1,0:T(8,128)(2,1)S(1)} %down_1.1.refs_2_), channel_id=1, source_target_pairs={{0,1},{1,0},{2,3},{3,2},{4,5},{5,4},{6,7},{7,6},{8,9},{9,8},{10,11... | collective-permute-start | bytes 98312 | tf_op jit(solution)/shard_map/ppermute | solution.py:76
  83.3 4.7 %collective-permute-start.31 = (bf16[8,2048]{1,0:T(8,128)(2,1)S(1)}, bf16[8,2048]{1,0:T(8,128)(2,1)S(1)}, u32[]{:S(2)}, u32[]{:S(2)}) collective-permute-start(bf16[8,2048]{1,0:T(8,128)(2,1)S(1)} %down_1.1.refs_2_), channel_id=1, source_target_pairs={{0,1},{1,0},{2,3},{3,2},{4,5},{5,4},{6,7},{7,6},{8,9},{9,8},{10,11... | collective-permute-start | bytes 98312 | tf_op jit(solution)/shard_map/ppermute | solution.py:76
  85.0 3.1 %collective-permute-start.30 = (bf16[8,2048]{1,0:T(8,128)(2,1)S(1)}, bf16[8,2048]{1,0:T(8,128)(2,1)S(1)}, u32[]{:S(2)}, u32[]{:S(2)}) collective-permute-start(bf16[8,2048]{1,0:T(8,128)(2,1)S(1)} %down_1.1.refs_2_), channel_id=1, source_target_pairs={{0,1},{1,0},{2,3},{3,2},{4,5},{5,4},{6,7},{7,6},{8,9},{9,8},{10,11... | collective-permute-start | bytes 98312 | tf_op jit(solution)/shard_map/ppermute | solution.py:76
  (16 other events, 89.9 us)
